TPU v7x, 32 devices: a whole 2x2x4 slice. The times are simulated.
32 devices in a mesh: dp: 16 (over z, y, core), mp: 2 (over x).
Axes of the slice: x: 2, y: 2, z: 4, core: 2. Of those that a mesh axis runs over, the one named last changes fastest.
Arguments:
- inputs: float32 [32, 1024, 1536], P('dp', 'mp'), may hold values from -6 to 6
- text_states: float32 [32, 64, 1536], P('dp', 'mp'), may hold values from -6 to 6
- cotangent: float32 [32, 1024, 1536], P('dp', 'mp'), may hold values from -6 to 6
- norm_params: float32 [1536, 6], P('dp'), as said below
- self_query_key: float32 [1536, 2, 1536], P('dp', None, 'mp')
- self_value: float32 [1536, 1536], P('dp', 'mp'), may hold values from -0.15625 to 0.15625
- self_output: float32 [1536, 1536], P('dp', 'mp'), may hold values from -1.25 to 1.25
- cross_query: float32 [1536, 1536], P('dp', 'mp')
- cross_key_value: float32 [1536, 2, 1536], P('dp', None, 'mp')
- cross_output: float32 [1536, 1536], P('dp', 'mp'), may hold values from -0.625 to 0.625
- hidden_in: float32 [1536, 6144], P('dp', 'mp'), may hold values from -0.15625 to 0.15625
- hidden_out: float32 [1536, 6144], P('dp', 'mp'), may hold values from -0.078125 to 0.078125
Outputs:
- output: float32 [32, 1024, 1536], P('dp', 'mp')
- grad_inputs: float32 [32, 1024, 1536], P('dp', 'mp')
- grad_text: float32 [32, 64, 1536], P('dp', 'mp')
- grad_norm_params: float32 [1536, 6], P('dp')
- grad_self_query_key: float32 [1536, 2, 1536], P('dp', None, 'mp')
- grad_self_value: float32 [1536, 1536], P('dp', 'mp')
- grad_self_output: float32 [1536, 1536], P('dp', 'mp')
- grad_cross_query: float32 [1536, 1536], P('dp', 'mp')
- grad_cross_key_value: float32 [1536, 2, 1536], P('dp', None, 'mp')
- grad_cross_output: float32 [1536, 1536], P('dp', 'mp')
- grad_hidden_in: float32 [1536, 6144], P('dp', 'mp')
- grad_hidden_out: float32 [1536, 6144], P('dp', 'mp')
- factors: float32 [2, 24], P(None, 'mp')
- clipped_self_query_key: float32 [1536, 2, 1536], P('dp', None, 'mp')
- clipped_cross_query: float32 [1536, 1536], P('dp', 'mp')
- clipped_cross_key: float32 [1536, 1536], P('dp', 'mp')
Inputs may be any that keep to these rules, and one draw needn't show every extreme that they name: `norm_params`: columns hold gain, bias, gain, bias, gain, bias of the three norms.
All inputs are finite; a program needn't handle non-finite values.
Results may differ from a plain program's by a relative error of at most 0.029.
Values may be sent and summed in bfloat16 or wider, within the bound.
A program may use at most 384 MiB of HBM per device.

v0:
```python
import jax
import jax.numpy as jnp
from jax import lax
from jax.sharding import PartitionSpec as P

D = 1536
HEADS = 24


EPSILON = 1e-05
CLIP_LIMIT = 7.0
MASKED = -1e30


def layer_norm(stream_rows, gain_row, bias_row):
    center = stream_rows - jnp.mean(stream_rows, axis=-1, keepdims=True)
    spread = jnp.mean(center * center, axis=-1, keepdims=True)
    return center * lax.rsqrt(spread + EPSILON) * gain_row + bias_row


def gelu_exact(values):
    return 0.5 * values * (1.0 + lax.erf(values * 2.0 ** (-0.5)))


def rounded(values):
    return values.astype(jnp.bfloat16)


def project(array, matrix):
    return jnp.einsum("cld,de->cle", array, matrix, preferred_element_type=jnp.float32)


def unproject(array, matrix):
    return jnp.einsum("cle,de->cld", array, matrix, preferred_element_type=jnp.float32)


def outer_sum(left, right):
    return jnp.einsum("cld,cle->de", left, right, preferred_element_type=jnp.float32)


def widen(values):
    return lax.all_gather(values, "mp", axis=1, tiled=True)


def settle(partial_sum):
    return lax.psum_scatter(
        partial_sum.astype(jnp.bfloat16), "mp", scatter_dimension=1, tiled=True
    ).astype(jnp.float32)


def widen_grad(values):
    return lax.all_gather(values, "mp", axis=1, tiled=True)


def settle_grad(partial_sum):
    return lax.psum_scatter(
        partial_sum.astype(jnp.bfloat16), "mp", scatter_dimension=1, tiled=True
    ).astype(jnp.float32)


def self_forward(queries, keys_all, values_all):
    frame_count, head_count, head_width = (queries.shape[1], queries.shape[2], queries.shape[3])
    block_rows = min(512, frame_count)
    block_count = frame_count // block_rows
    scaling = head_width ** (-0.5)
    row_ids = jnp.arange(block_rows)
    col_ids = jnp.arange(frame_count)

    def per_clip(triple):
        clip_queries, clip_keys, clip_values = triple

        def per_block(block_index):
            offset = block_index * block_rows
            block_queries = lax.dynamic_slice_in_dim(clip_queries, offset, block_rows, 0)
            scores = (
                jnp.einsum(
                    "qhe,khe->hqk", block_queries, clip_keys, preferred_element_type=jnp.float32
                )
                * scaling
            )
            allowed = col_ids[None, :] <= (offset + row_ids)[:, None]
            scores = jnp.where(allowed[None], scores, MASKED)
            highest = jnp.max(scores, axis=2, keepdims=True)
            exponents = jnp.exp(scores - highest)
            row_sums = jnp.sum(exponents, axis=2, keepdims=True)
            mixed = jnp.einsum(
                "hqk,khe->qhe",
                rounded(exponents / row_sums),
                clip_values,
                preferred_element_type=jnp.float32,
            )
            return (
                mixed,
                (highest + jnp.log(row_sums))[:, :, 0],
                jnp.max(highest[:, :, 0], axis=1),
            )

        mixed, log_sums, block_peaks = lax.map(per_block, jnp.arange(block_count))
        return (
            mixed.reshape(frame_count, head_count, head_width),
            log_sums,
            jnp.max(block_peaks, axis=0),
        )

    mixed, log_sums, clip_peaks = lax.map(per_clip, (queries, keys_all, values_all))
    return (mixed, log_sums, jnp.max(clip_peaks, axis=0))


def self_backward(queries, keys_all, values_all, log_sums, grad_mixed):
    frame_count, head_count, head_width = (queries.shape[1], queries.shape[2], queries.shape[3])
    block_rows = min(512, frame_count)
    block_count = frame_count // block_rows
    scaling = head_width ** (-0.5)
    row_ids = jnp.arange(block_rows)
    col_ids = jnp.arange(frame_count)

    def per_clip(bundle):
        clip_queries, clip_keys, clip_values, clip_logs, clip_grads = bundle

        def per_block(carried, block_index):
            grad_keys, grad_values = carried
            offset = block_index * block_rows
            block_queries = lax.dynamic_slice_in_dim(clip_queries, offset, block_rows, 0)
            block_grads = lax.dynamic_slice_in_dim(clip_grads, offset, block_rows, 0)
            scores = (
                jnp.einsum(
                    "qhe,khe->hqk", block_queries, clip_keys, preferred_element_type=jnp.float32
                )
                * scaling
            )
            allowed = col_ids[None, :] <= (offset + row_ids)[:, None]
            scores = jnp.where(allowed[None], scores, MASKED)
            weights = jnp.exp(scores - clip_logs[block_index][:, :, None])
            grad_values = grad_values + jnp.einsum(
                "hqk,qhe->khe", rounded(weights), block_grads, preferred_element_type=jnp.float32
            )
            grad_weights = jnp.einsum(
                "qhe,khe->hqk", block_grads, clip_values, preferred_element_type=jnp.float32
            )
            centered = grad_weights - jnp.sum(weights * grad_weights, axis=2, keepdims=True)
            grad_scores = rounded(weights * centered)
            grad_queries = (
                jnp.einsum(
                    "hqk,khe->qhe", grad_scores, clip_keys, preferred_element_type=jnp.float32
                )
                * scaling
            )
            grad_keys = (
                grad_keys
                + jnp.einsum(
                    "hqk,qhe->khe", grad_scores, block_queries, preferred_element_type=jnp.float32
                )
                * scaling
            )
            return ((grad_keys, grad_values), grad_queries)

        zero_keys = jnp.zeros(clip_keys.shape, jnp.float32)
        (grad_keys, grad_values), grad_queries = lax.scan(
            per_block, (zero_keys, zero_keys), jnp.arange(block_count)
        )
        return (grad_queries.reshape(frame_count, head_count, head_width), grad_keys, grad_values)

    return lax.map(per_clip, (queries, keys_all, values_all, log_sums, grad_mixed))


def cross_forward(queries, keys_all, values_all):
    scaling = queries.shape[3] ** (-0.5)
    scores = (
        jnp.einsum("clhe,cshe->chls", queries, keys_all, preferred_element_type=jnp.float32)
        * scaling
    )
    highest = jnp.max(scores, axis=3, keepdims=True)
    exponents = jnp.exp(scores - highest)
    weights = exponents / jnp.sum(exponents, axis=3, keepdims=True)
    mixed = jnp.einsum(
        "chls,cshe->clhe", rounded(weights), values_all, preferred_element_type=jnp.float32
    )
    return (mixed, weights, jnp.max(highest, axis=(0, 2, 3)))


def cross_backward(queries, keys_all, values_all, weights, grad_mixed):
    scaling = queries.shape[3] ** (-0.5)
    grad_values = jnp.einsum(
        "chls,clhe->cshe", rounded(weights), grad_mixed, preferred_element_type=jnp.float32
    )
    grad_weights = jnp.einsum(
        "clhe,cshe->chls", grad_mixed, values_all, preferred_element_type=jnp.float32
    )
    centered = grad_weights - jnp.sum(weights * grad_weights, axis=3, keepdims=True)
    grad_scores = rounded(weights * centered)
    grad_queries = (
        jnp.einsum("chls,cshe->clhe", grad_scores, keys_all, preferred_element_type=jnp.float32)
        * scaling
    )
    grad_keys = (
        jnp.einsum("chls,clhe->cshe", grad_scores, queries, preferred_element_type=jnp.float32)
        * scaling
    )
    return (grad_queries, grad_keys, grad_values)


def per_device(
    inputs,
    text_states,
    cotangent,
    norm_params,
    self_query_key,
    self_value,
    self_output,
    cross_query,
    cross_key_value,
    cross_output,
    hidden_in,
    hidden_out,
):
    (
        full_norms,
        full_query_key,
        full_value,
        full_output,
        full_cross_query,
        full_cross_pair,
        full_cross_output,
        full_hidden_in,
        full_hidden_out,
    ) = (
        lax.all_gather(rounded(norm_params), "dp", axis=0, tiled=True),
        lax.all_gather(rounded(self_query_key), "dp", axis=0, tiled=True),
        lax.all_gather(rounded(self_value), "dp", axis=0, tiled=True),
        lax.all_gather(rounded(self_output), "dp", axis=0, tiled=True),
        lax.all_gather(rounded(cross_query), "dp", axis=0, tiled=True),
        lax.all_gather(rounded(cross_key_value), "dp", axis=0, tiled=True),
        lax.all_gather(rounded(cross_output), "dp", axis=0, tiled=True),
        lax.all_gather(rounded(hidden_in), "dp", axis=0, tiled=True),
        lax.all_gather(rounded(hidden_out), "dp", axis=0, tiled=True),
    )
    norm_rows = full_norms.astype(jnp.float32)
    head_width = D // HEADS
    head_count = full_value.shape[1] // head_width

    def split_heads(array):
        return array.reshape(array.shape[0], array.shape[1], head_count, head_width)

    def merge_heads(array):
        return array.reshape(array.shape[0], array.shape[1], head_count * head_width)

    normed, pull_self = jax.vjp(layer_norm, inputs, norm_rows[:, 0], norm_rows[:, 1])
    normed_self = widen(rounded(normed))
    query_key_rows = jnp.einsum(
        "cld,dte->clte", normed_self, full_query_key, preferred_element_type=jnp.float32
    )
    queries = rounded(query_key_rows[:, :, 0])
    self_keys = rounded(query_key_rows[:, :, 1])
    values = rounded(project(normed_self, full_value))
    mixed, log_sums, self_peaks = self_forward(
        split_heads(queries), split_heads(self_keys), split_heads(values)
    )
    mixed_self = rounded(merge_heads(mixed))
    after_self = inputs + settle(unproject(mixed_self, full_output))
    normed, pull_cross = jax.vjp(layer_norm, after_self, norm_rows[:, 2], norm_rows[:, 3])
    normed_cross = widen(rounded(normed))
    cross_queries = rounded(project(normed_cross, full_cross_query))
    states = lax.all_gather(rounded(text_states), "mp", axis=1, tiled=True)
    key_value_rows = jnp.einsum(
        "csd,dte->cste", states, full_cross_pair, preferred_element_type=jnp.float32
    )
    cross_keys = rounded(key_value_rows[:, :, 0])
    cross_values = rounded(key_value_rows[:, :, 1])
    attended, cross_weights, cross_peaks = cross_forward(
        split_heads(cross_queries), split_heads(cross_keys), split_heads(cross_values)
    )
    mixed_cross = rounded(merge_heads(attended))
    after_cross = after_self + settle(unproject(mixed_cross, full_cross_output))
    normed, pull_hidden = jax.vjp(layer_norm, after_cross, norm_rows[:, 4], norm_rows[:, 5])
    normed_hidden = widen(rounded(normed))
    upward = project(normed_hidden, full_hidden_in)
    activated, pull_gelu = jax.vjp(gelu_exact, upward)
    activated = rounded(activated)
    output = after_cross + settle(unproject(activated, full_hidden_out))
    self_top, cross_top = lax.pmax((self_peaks, cross_peaks), "dp")
    grad_branch = widen_grad(rounded(cotangent))
    grad_hidden_out = outer_sum(grad_branch, activated)
    grad_upward = rounded(pull_gelu(project(grad_branch, full_hidden_out))[0])
    grad_hidden_in = outer_sum(normed_hidden, grad_upward)
    grad_normed = settle_grad(unproject(grad_upward, full_hidden_in))
    back_stream, grad_gain_three, grad_bias_three = pull_hidden(grad_normed)
    grad_stream = cotangent + back_stream
    grad_branch = widen_grad(rounded(grad_stream))
    grad_cross_output = outer_sum(grad_branch, mixed_cross)
    grad_attended = rounded(project(grad_branch, full_cross_output))
    grad_queries, grad_keys, grad_values = cross_backward(
        split_heads(cross_queries),
        split_heads(cross_keys),
        split_heads(cross_values),
        cross_weights,
        split_heads(grad_attended),
    )
    grad_queries = rounded(merge_heads(grad_queries))
    grad_pair = rounded(jnp.stack([merge_heads(grad_keys), merge_heads(grad_values)], axis=2))
    grad_cross_query = outer_sum(normed_cross, grad_queries)
    grad_cross_pair = jnp.einsum(
        "csd,cste->dte", states, grad_pair, preferred_element_type=jnp.float32
    )
    grad_text = lax.psum_scatter(
        jnp.einsum(
            "cste,dte->csd", grad_pair, full_cross_pair, preferred_element_type=jnp.float32
        ).astype(jnp.bfloat16),
        "mp",
        scatter_dimension=1,
        tiled=True,
    ).astype(jnp.float32)
    grad_normed = settle_grad(unproject(grad_queries, full_cross_query))
    back_stream, grad_gain_two, grad_bias_two = pull_cross(grad_normed)
    grad_stream = grad_stream + back_stream
    grad_branch = widen_grad(rounded(grad_stream))
    grad_self_output = outer_sum(grad_branch, mixed_self)
    grad_mixed = rounded(project(grad_branch, full_output))
    grad_queries, grad_keys, grad_values = self_backward(
        split_heads(queries),
        split_heads(self_keys),
        split_heads(values),
        log_sums,
        split_heads(grad_mixed),
    )
    grad_pair = rounded(jnp.stack([merge_heads(grad_queries), merge_heads(grad_keys)], axis=2))
    grad_values = rounded(merge_heads(grad_values))
    grad_self_pair = jnp.einsum(
        "cld,clte->dte", normed_self, grad_pair, preferred_element_type=jnp.float32
    )
    grad_self_value = outer_sum(normed_self, grad_values)
    grad_normed = settle_grad(
        jnp.einsum("clte,dte->cld", grad_pair, full_query_key, preferred_element_type=jnp.float32)
        + unproject(grad_values, full_value)
    )
    back_stream, grad_gain_one, grad_bias_one = pull_self(grad_normed)
    grad_inputs = grad_stream + back_stream
    grad_norm_rows = lax.psum(
        jnp.stack(
            [
                grad_gain_one,
                grad_bias_one,
                grad_gain_two,
                grad_bias_two,
                grad_gain_three,
                grad_bias_three,
            ],
            axis=1,
        ).astype(jnp.bfloat16),
        "mp",
    )
    (
        shard_norms,
        shard_self_pair,
        shard_self_value,
        shard_self_output,
        shard_cross_query,
        shard_cross_pair,
        shard_cross_output,
        shard_hidden_in,
        shard_hidden_out,
    ) = (
        lax.psum_scatter(grad_norm_rows, "dp", scatter_dimension=0, tiled=True).astype(jnp.float32),
        lax.psum_scatter(
            grad_self_pair.astype(jnp.bfloat16), "dp", scatter_dimension=0, tiled=True
        ).astype(jnp.float32),
        lax.psum_scatter(
            grad_self_value.astype(jnp.bfloat16), "dp", scatter_dimension=0, tiled=True
        ).astype(jnp.float32),
        lax.psum_scatter(
            grad_self_output.astype(jnp.bfloat16), "dp", scatter_dimension=0, tiled=True
        ).astype(jnp.float32),
        lax.psum_scatter(
            grad_cross_query.astype(jnp.bfloat16), "dp", scatter_dimension=0, tiled=True
        ).astype(jnp.float32),
        lax.psum_scatter(
            grad_cross_pair.astype(jnp.bfloat16), "dp", scatter_dimension=0, tiled=True
        ).astype(jnp.float32),
        lax.psum_scatter(
            grad_cross_output.astype(jnp.bfloat16), "dp", scatter_dimension=0, tiled=True
        ).astype(jnp.float32),
        lax.psum_scatter(
            grad_hidden_in.astype(jnp.bfloat16), "dp", scatter_dimension=0, tiled=True
        ).astype(jnp.float32),
        lax.psum_scatter(
            grad_hidden_out.astype(jnp.bfloat16), "dp", scatter_dimension=0, tiled=True
        ).astype(jnp.float32),
    )
    factors = CLIP_LIMIT / jnp.maximum(jnp.stack([self_top, cross_top]), CLIP_LIMIT)
    root_scales = jnp.repeat(jnp.sqrt(factors), head_width, axis=1)
    clipped_self = self_query_key * root_scales[0][None, None, :]
    clipped_query = cross_query * root_scales[1][None, :]
    clipped_key = cross_key_value[:, 0] * root_scales[1][None, :]
    return (
        output,
        grad_inputs,
        grad_text,
        shard_norms,
        shard_self_pair,
        shard_self_value,
        shard_self_output,
        shard_cross_query,
        shard_cross_pair,
        shard_cross_output,
        shard_hidden_in,
        shard_hidden_out,
        factors,
        clipped_self,
        clipped_query,
        clipped_key,
    )


def solution(mesh):
    in_specs = (
        P("dp", "mp", None),
        P("dp", "mp", None),
        P("dp", "mp", None),
        P("dp", None),
        P("dp", None, "mp"),
        P("dp", "mp"),
        P("dp", "mp"),
        P("dp", "mp"),
        P("dp", None, "mp"),
        P("dp", "mp"),
        P("dp", "mp"),
        P("dp", "mp"),
    )
    out_specs = (
        P("dp", "mp", None),
        P("dp", "mp", None),
        P("dp", "mp", None),
        P("dp", None),
        P("dp", None, "mp"),
        P("dp", "mp"),
        P("dp", "mp"),
        P("dp", "mp"),
        P("dp", None, "mp"),
        P("dp", "mp"),
        P("dp", "mp"),
        P("dp", "mp"),
        P(None, "mp"),
        P("dp", None, "mp"),
        P("dp", "mp"),
        P("dp", "mp"),
    )
    return jax.shard_map(
        per_device, mesh=mesh, in_specs=in_specs, out_specs=out_specs, check_vma=False
    )
```

profile of v0, /device:TPU:0, one launch (start us, length us, event | category | flops | bytes accessed | tf_op | source)
XLA Modules:
  0.0 2503.9 jit_solution(7192400032739193023)
XLA Ops:
  9.6 23.1 all-gather
  55.9 81.3 %all-gather.16.cloned.1.call-done = bf16[2,1024,1536]{2,1,0:T(8,128)(2,1)} async-done(((bf16[2,512,1536]{2,1,0:T(8,128)(2,1)}), bf16[2,1024,1536]{2,1,0:T(8,128)(2,1)}) %all-gather.16.cloned.1.call-update) | async-done | bytes 6291472 | tf_op jit(solution)/shard_map/all_gather | solution.py:42
  146.4 47.2 %all-gather.18.cloned.1.call-done = bf16[1536,2,768]{2,0,1:T(8,128)(2,1)} async-done(((bf16[96,2,768]{2,0,1:T(8,128)(2,1)}), bf16[1536,2,768]{2,0,1:T(8,128)(2,1)}) %all-gather.18.cloned.1.call-update) | async-done | bytes 4718608 | tf_op jit(solution)/shard_map/all_gather | solution.py:228
  193.5 13.5 fusion.79
  212.5 181.2 %while.62 = (s32[]{:T(128)}, bf16[2,1024,12,64]{1,3,2,0:T(8,128)(2,1)}, f32[2,2,12,512]{3,2,1,0:T(8,128)}, f32[2,12]{1,0:T(2,128)}, bf16[2,1024,12,64]{1,3,2,0:T...) while((s32[]{:T(128)}, ...), condition=%wide.region_9.10_spmd.clone, body=%wide.region_2.9_spmd.clone.sunk | while | flops 1692920320 | bytes 209282752 | solution.py:105
  217.8 73.0 %while.65 = (s32[]{:T(128)}, bf16[2,512,12,64]{1,3,2,0:T(8,128)(2,1)}, f32[2,12,512]{2,1,0:T(8,128)S(1)}, f32[2,12]{1,0:T(2,128)S(1)}, s32[1024]{0:T(1024)S(1)},...) while((s32[]{:T(128)}, ...), condition=%wide.region_7.7_spmd, body=%wide.region_3.6_spmd.sunk | while | flops 1692920320 | bytes 190286224 | solution.py:98
  219.4 10.8 fusion.224
  230.3 13.2 fusion.225
  256.1 10.7 fusion.224
  266.8 13.1 fusion.225
  308.4 72.6 %while.65 = (s32[]{:T(128)}, bf16[2,512,12,64]{1,3,2,0:T(8,128)(2,1)}, f32[2,12,512]{2,1,0:T(8,128)S(1)}, f32[2,12]{1,0:T(2,128)S(1)}, s32[1024]{0:T(1024)S(1)},...) while((s32[]{:T(128)}, ...), condition=%wide.region_7.7_spmd, body=%wide.region_3.6_spmd.sunk | while | flops 1692920320 | bytes 190286224 | solution.py:98
  310.1 10.7 fusion.224
  320.8 13.1 fusion.225
  346.4 10.7 fusion.224
  357.1 13.1 fusion.225
  405.8 72.8 %reduce-scatter.20.cloned.1.call-done = bf16[2,512,1536]{2,1,0:T(8,128)(2,1)} async-done(((bf16[2,1024,1536]{2,1,0:T(8,128)(2,1)}), bf16[2,512,1536]{2,1,0:T(8,128)(2,1)}) %reduce-scatter.20.cloned.1.call-update) | async-done | bytes 3145744 | tf_op jit(solution)/shard_map/reduce_scatter | solution.py:46
  496.2 38.8 %all-gather.24.cloned.1.call-done = bf16[1536,2,768]{2,0,1:T(8,128)(2,1)} async-done(((bf16[96,2,768]{2,0,1:T(8,128)(2,1)}), bf16[1536,2,768]{2,0,1:T(8,128)(2,1)}) %all-gather.24.cloned.1.call-update) | async-done | bytes 4718608 | tf_op jit(solution)/shard_map/all_gather | solution.py:232
  539.5 39.4 %all-gather.28.cloned.1.call-done = bf16[1536,768]{1,0:T(8,128)(2,1)} async-done(((bf16[96,768]{1,0:T(8,128)(2,1)}), bf16[1536,768]{1,0:T(8,128)(2,1)}) %all-gather.28.cloned.1.call-update) | async-done | bytes 2359312 | tf_op jit(solution)/shard_map/all_gather | solution.py:231
  578.9 81.4 %all-gather.26.cloned.1.call-done = bf16[2,1024,1536]{2,1,0:T(8,128)(2,1)} async-done(((bf16[2,512,1536]{2,1,0:T(8,128)(2,1)}), bf16[2,1024,1536]{2,1,0:T(8,128)(2,1)}) %all-gather.26.cloned.1.call-update) | async-done | bytes 6291472 | tf_op jit(solution)/shard_map/all_gather | solution.py:42
  679.5 26.1 %all-gather.30.cloned.1.call-done = bf16[1536,768]{1,0:T(8,128)(2,1)} async-done(((bf16[96,768]{1,0:T(8,128)(2,1)}), bf16[1536,768]{1,0:T(8,128)(2,1)}) %all-gather.30.cloned.1.call-update) | async-done | bytes 2359312 | tf_op jit(solution)/shard_map/all_gather | solution.py:233
  717.0 73.8 %reduce-scatter.22.cloned.1.call-done = bf16[2,512,1536]{2,1,0:T(8,128)(2,1)} async-done(((bf16[2,1024,1536]{2,1,0:T(8,128)(2,1)}), bf16[2,512,1536]{2,1,0:T(8,128)(2,1)}) %reduce-scatter.22.cloned.1.call-update) | async-done | bytes 3145744 | tf_op jit(solution)/shard_map/reduce_scatter | solution.py:46
  806.7 68.4 %all-gather.34.cloned.1.call-done = bf16[1536,3072]{1,0:T(8,128)(2,1)} async-done(((bf16[96,3072]{1,0:T(8,128)(2,1)}), bf16[1536,3072]{1,0:T(8,128)(2,1)}) %all-gather.34.cloned.1.call-update) | async-done | bytes 9437200 | tf_op jit(solution)/shard_map/all_gather | solution.py:234
  875.1 79.9 %all-gather.32.cloned.1.call-done = bf16[2,1024,1536]{2,1,0:T(8,128)(2,1)} async-done(((bf16[2,512,1536]{2,1,0:T(8,128)(2,1)}), bf16[2,1024,1536]{2,1,0:T(8,128)(2,1)}) %all-gather.32.cloned.1.call-update) | async-done | bytes 6291472 | tf_op jit(solution)/shard_map/all_gather | solution.py:42
  955.1 29.1 %multiply_convert_fusion.1 = (bf16[2,1024,3072]{2,1,0:T(8,128)(2,1)}, f32[2,1024,3072]{2,1,0:T(8,128)}) fusion(bf16[2,1024,1536]{2,1,0:T(8,128)(2,1)} %all-gather.32.cloned.1.call-done, bf16[1536,3072]{1,0:T(8,128)(2,1)} %all-gather.34.cloned.1.call-done), kind=kOutput, calls=%fused_computation.59 | convolution fusion | flops 19358810112 | bytes 53477376 | tf_op jit(solution)/shard_map/cld,de->cle/dot_general | solution.py:30
  984.2 52.9 %all-gather.38.cloned.1.call-done = bf16[2,1024,1536]{2,1,0:T(8,128)(2,1)} async-done(((bf16[2,512,1536]{2,1,0:T(8,128)(2,1)}), bf16[2,1024,1536]{2,1,0:T(8,128)(2,1)}) %all-gather.38.cloned.1.call-update) | async-done | bytes 6291472 | tf_op jit(solution)/shard_map/all_gather | solution.py:52
  1037.0 84.2 %all-gather.36.cloned.1.call-done = bf16[1536,3072]{1,0:T(8,128)(2,1)} async-done(((bf16[96,3072]{1,0:T(8,128)(2,1)}), bf16[1536,3072]{1,0:T(8,128)(2,1)}) %all-gather.36.cloned.1.call-update) | async-done | bytes 9437200 | tf_op jit(solution)/shard_map/all_gather | solution.py:235
  1121.2 36.3 %add_convert_fusion = bf16[2,1024,3072]{2,1,0:T(8,128)(2,1)} fusion(f32[2,1024,3072]{2,1,0:T(8,128)} %get-tuple-element.565, bf16[2,1024,1536]{2,1,0:T(8,128)(2,1)} %all-gather.38.cloned.1.call-done, bf16[1536,3072]{1,0:T(8,128)(2,1)} %all-gather.36.cloned.1.call-done), kind=kOutput, calls=%fused_computation.58 | convolution fusion | flops 19409141760 | bytes 53477376 | tf_op jit(solution)/shard_map/cld,de->cle/dot_general | solution.py:30
  1157.6 23.3 fusion.61
  1181.4 74.9 %reduce-scatter.26.cloned.1.call-done = bf16[2,512,1536]{2,1,0:T(8,128)(2,1)} async-done(((bf16[2,1024,1536]{2,1,0:T(8,128)(2,1)}), bf16[2,512,1536]{2,1,0:T(8,128)(2,1)}) %reduce-scatter.26.cloned.1.call-update) | async-done | bytes 3145744 | tf_op jit(solution)/shard_map/reduce_scatter | solution.py:56
  1271.5 80.5 %all-gather.40.cloned.1.call-done = bf16[2,1024,1536]{2,1,0:T(8,128)(2,1)} async-done(((bf16[2,512,1536]{2,1,0:T(8,128)(2,1)}), bf16[2,1024,1536]{2,1,0:T(8,128)(2,1)}) %all-gather.40.cloned.1.call-update) | async-done | bytes 6291472 | tf_op jit(solution)/shard_map/all_gather | solution.py:52
  1382.0 26.1 %fusion.64 = bf16[2,1024,1536]{2,1,0:T(8,128)(2,1)} fusion(bf16[2,1024,3072]{2,1,0:T(8,128)(2,1)} %get-tuple-element.564, bf16[1536,3072]{1,0:T(8,128)(2,1)} %all-gather.36.cloned.1.call-done), kind=kOutput, calls=%fused_computation.121 | convolution fusion | flops 19330498560 | bytes 28311552 | tf_op jit(solution)/shard_map/cle,de->cld/dot_general | solution.py:34
  1408.2 50.8 %reduce-scatter.28.cloned.1.call-done = bf16[2,512,1536]{2,1,0:T(8,128)(2,1)} async-done(((bf16[2,1024,1536]{2,1,0:T(8,128)(2,1)}), bf16[2,512,1536]{2,1,0:T(8,128)(2,1)}) %reduce-scatter.28.cloned.1.call-update) | async-done | bytes 3145744 | tf_op jit(solution)/shard_map/reduce_scatter | solution.py:56
  1470.0 68.3 %reduce-scatter.24.cloned.1.call-done = bf16[2,512,1536]{2,1,0:T(8,128)(2,1)} async-done(((bf16[2,1024,1536]{2,1,0:T(8,128)(2,1)}), bf16[2,512,1536]{2,1,0:T(8,128)(2,1)}) %reduce-scatter.24.cloned.1.call-update) | async-done | bytes 3145744 | tf_op jit(solution)/shard_map/reduce_scatter | solution.py:46
  1538.3 14.7 fusion.149
  1553.2 25.6 %fusion.37 = bf16[1536,3072]{0,1:T(8,128)(2,1)} fusion(bf16[2,1024,3072]{2,1,0:T(8,128)(2,1)} %get-tuple-element.564, bf16[2,1024,1536]{2,1,0:T(8,128)(2,1)} %all-gather.38.cloned.1.call-done), kind=kOutput, calls=%fused_computation.65 | convolution fusion | flops 19332071424 | bytes 28311552 | tf_op jit(solution)/shard_map/cld,cle->de/dot_general | solution.py:38
  1578.8 12.6 copy.193
  1591.5 25.9 %bitcast_convert_fusion.1 = bf16[1536,3072]{1,0:T(8,128)(2,1)} fusion(bf16[2,1024,1536]{2,1,0:T(8,128)(2,1)} %all-gather.32.cloned.1.call-done, bf16[2,1024,3072]{2,1,0:T(8,128)(2,1)} %add_convert_fusion), kind=kOutput, calls=%fused_computation.62 | convolution fusion | flops 19332071424 | bytes 28311552 | tf_op jit(solution)/shard_map/cld,cle->de/dot_general | solution.py:38
  1638.9 12.8 copy.164
  1696.3 425.1 %while.64 = (s32[]{:T(128)}, bf16[2,1024,12,64]{1,3,2,0:T(8,128)(2,1)}, bf16[2,1024,12,64]{1,3,2,0:T(8,128)(2,1)}, bf16[2,1024,12,64]{1,3,2,0:T(8,128)(2,1)}, bf...) while((s32[]{:T(128)}, ...), condition=%wide.region_30.31_spmd.clone, body=%wide.region_26.30_spmd.clone.sunk | while | flops 4125747712 | bytes 256148128 | solution.py:163
  1708.3 184.3 %while.66 = (s32[]{:T(128)}, f32[1024,12,64]{0,2,1:T(8,128)S(1)}, f32[1024,12,64]{0,2,1:T(8,128)}, bf16[2,512,12,64]{1,3,2,0:T(8,128)(2,1)}, s32[2]{0:T(128)S(1)...) while((s32[]{:T(128)}, f32[1024,12,64]{0,2,1:T(8,128)S(1)}, ...), condition=%wide.region_29.29_spmd.clone, body=%wide.region_27.28_spmd.clone.sunk | while | flops 4125747712 | bytes 221440336 | solution.py:158
  1711.9 13.9 fusion.221
  1725.8 13.9 bitcast_add_fusion.6
  1739.7 18.4 multiply_reduce_fusion.8
  1758.0 25.8 %multiply_convert_fusion.5 = bf16[12,512,1024]{2,1,0:T(8,128)(2,1)} fusion(f32[12,512,1024]{2,1,0:T(8,128)} %get-tuple-element.860, f32[12,512,1024]{2,1,0:T(8,128)} %fusion.221, f32[12,512]{1,0:T(8,128)S(1)} %get-tuple-element.861, f32[12,512]{1,0:T(8,128)S(1)} %dynamic-slice_bitcast_fusion.24, pred[512,1024]{1,0:T(8,128)(4,1)} %copy-done.1), kind=kLoop, calls=%fused_computation.25.clone.1 | loop fusion | flops 37748736 | bytes 63488000 | tf_op jit(solution)/shard_map/while/body/eval_jaxpr/while/body/eval_jaxpr/convert_element_type | solution.py:26
  1805.6 14.0 fusion.221
  1819.6 14.7 bitcast_add_fusion.6
  1834.3 18.4 multiply_reduce_fusion.8
  1852.7 22.4 multiply_convert_fusion.5
  1922.5 180.4 %while.66 = (s32[]{:T(128)}, f32[1024,12,64]{0,2,1:T(8,128)S(1)}, f32[1024,12,64]{0,2,1:T(8,128)}, bf16[2,512,12,64]{1,3,2,0:T(8,128)(2,1)}, s32[2]{0:T(128)S(1)...) while((s32[]{:T(128)}, f32[1024,12,64]{0,2,1:T(8,128)S(1)}, ...), condition=%wide.region_29.29_spmd.clone, body=%wide.region_27.28_spmd.clone.sunk | while | flops 4125747712 | bytes 221440336 | solution.py:158
  1926.1 13.9 fusion.221
  1940.1 13.5 bitcast_add_fusion.6
  1953.6 18.3 multiply_reduce_fusion.8
  1971.9 22.7 multiply_convert_fusion.5
  2015.6 13.9 fusion.221
  2029.5 14.6 bitcast_add_fusion.6
  2044.1 18.3 multiply_reduce_fusion.8
  2062.4 22.5 multiply_convert_fusion.5
  2138.5 14.5 bitcast_convert_fusion.2
  2163.5 15.7 fusion.36
  2185.7 32.8 %all-reduce.1 = (f32[1,12]{1,0:T(1,128)S(1)}, f32[1,12]{1,0:T(1,128)S(1)}) all-reduce(f32[1,12]{1,0:T(1,128)S(1)} %bitcast.330, f32[1,12]{1,0:T(1,128)S(1)} %bitcast.329), channel_id=1, replica_groups=mesh['dp'=16,'mp'=2] {'dp'}, use_global_device_ids=true, to_apply=%region_54.55 | all-reduce | flops 24 | bytes 192 | tf_op jit(solution)/shard_map/pmax | solution.py:280
  2240.2 25.2 %reduce-scatter.36.cloned.1.call-done = bf16[96,768]{1,0:T(8,128)(2,1)} async-done(((bf16[1536,768]{1,0:T(8,128)(2,1)}), bf16[96,768]{1,0:T(8,128)(2,1)}) %reduce-scatter.36.cloned.1.call-update) | async-done | bytes 147472 | tf_op jit(solution)/shard_map/reduce_scatter | solution.py:366
  2267.0 76.8 %reduce-scatter.34.cloned.1.call-done = bf16[96,2,768]{2,0,1:T(8,128)(2,1)} async-done(((bf16[1536,2,768]{2,0,1:T(8,128)(2,1)}), bf16[96,2,768]{2,0,1:T(8,128)(2,1)}) %reduce-scatter.34.cloned.1.call-update) | async-done | bytes 294928 | tf_op jit(solution)/shard_map/reduce_scatter | solution.py:363
  2345.9 77.0 %reduce-scatter.30.cloned.1.call-done = bf16[2,512,1536]{2,1,0:T(8,128)(2,1)} async-done(((bf16[2,1024,1536]{2,1,0:T(8,128)(2,1)}), bf16[2,512,1536]{2,1,0:T(8,128)(2,1)}) %reduce-scatter.30.cloned.1.call-update) | async-done | bytes 3145744 | tf_op jit(solution)/shard_map/reduce_scatter | solution.py:56
  2442.3 48.2 %reduce-scatter.48.cloned.1.call-done = bf16[96,6]{1,0:T(8,128)(2,1)} async-done(((bf16[1536,6]{1,0:T(8,128)(2,1)}), bf16[96,6]{1,0:T(8,128)(2,1)}) %reduce-scatter.48.cloned.1.call-update) | async-done | bytes 1168
  (463 shorter events, 544.9 us)
Async XLA Ops:
  7.2 48.7 %all-gather.20.cloned.1.call-start = ((), (), s32[]{:S(2)}) async-start(), calls=%async_computation.17 | async-start | bytes 2506752 | tf_op jit(solution)/shard_map/all_gather | solution.py:229
  8.9 128.3 %all-gather.16.cloned.1.call-start = ((), (), s32[]{:S(2)}) async-start(), calls=%async_computation.15 | async-start | bytes 9437184 | tf_op jit(solution)/shard_map/all_gather | solution.py:42
  45.9 147.7 %all-gather.18.cloned.1.call-start = ((), (), s32[]{:S(2)}) async-start(), calls=%async_computation.16 | async-start | bytes 5013504 | tf_op jit(solution)/shard_map/all_gather | solution.py:228
  46.7 346.9 %all-gather.22.cloned.1.call-start = ((), (), s32[]{:S(2)}) async-start(), calls=%async_computation.18 | async-start | bytes 2506752 | tf_op jit(solution)/shard_map/all_gather | solution.py:230
  47.5 431.1 %reduce-scatter.20.cloned.1.call-start = ((), (), s32[]{:S(2)}) async-start(), calls=%async_computation.19 | async-start | bytes 9437184 | tf_op jit(solution)/shard_map/reduce_scatter | solution.py:46
  217.8 73.0 %copy-start.61 = (f32[2,12]{1,0:T(2,128)S(1)}, f32[2,12]{1,0:T(2,128)}, u32[]{:S(2)}) copy-start(f32[2,12]{1,0:T(2,128)} %get-tuple-element.986) | copy-start | bytes 292 | tf_op jit(solution)/shard_map/while
  219.4 24.0 copy-start.11
  230.2 15.6 copy-start
  256.1 23.8 copy-start.11
  266.8 15.5 copy-start
  308.4 72.7 %copy-start.61 = (f32[2,12]{1,0:T(2,128)S(1)}, f32[2,12]{1,0:T(2,128)}, u32[]{:S(2)}) copy-start(f32[2,12]{1,0:T(2,128)} %get-tuple-element.986) | copy-start | bytes 292 | tf_op jit(solution)/shard_map/while
  310.1 23.8 copy-start.11
  320.8 15.5 copy-start
  346.4 23.8 copy-start.11
  357.1 15.5 copy-start
  402.8 132.2 %all-gather.24.cloned.1.call-start = ((), (), s32[]{:S(2)}) async-start(), calls=%async_computation.20 | async-start | bytes 5013504 | tf_op jit(solution)/shard_map/all_gather | solution.py:232
  404.6 174.3 %all-gather.28.cloned.1.call-start = ((), (), s32[]{:S(2)}) async-start(), calls=%async_computation.22 | async-start | bytes 2506752 | tf_op jit(solution)/shard_map/all_gather | solution.py:231
  405.4 254.9 %all-gather.26.cloned.1.call-start = ((), (), s32[]{:S(2)}) async-start(), calls=%async_computation.21 | async-start | bytes 9437184 | tf_op jit(solution)/shard_map/all_gather | solution.py:42
  488.1 217.6 %all-gather.30.cloned.1.call-start = ((), (), s32[]{:S(2)}) async-start(), calls=%async_computation.23 | async-start | bytes 2506752 | tf_op jit(solution)/shard_map/all_gather | solution.py:233
  488.8 301.9 %reduce-scatter.22.cloned.1.call-start = ((), (), s32[]{:S(2)}) async-start(), calls=%async_computation.24 | async-start | bytes 9437184 | tf_op jit(solution)/shard_map/reduce_scatter | solution.py:46
  496.2 82.7 %copy-start.19 = (bf16[2,64,1536]{2,1,0:T(8,128)(2,1)}, bf16[2,64,1536]{2,1,0:T(8,128)(2,1)S(1)}, u32[]{:S(2)}) copy-start(bf16[2,64,1536]{2,1,0:T(8,128)(2,1)S(1)} %all_gather.53) | copy-start | bytes 1179652
  538.4 129.9 %copy-start.16 = (bf16[2,64,1,768]{1,3,0,2:T(8,128)(2,1)}, bf16[2,64,1,768]{1,3,0,2:T(8,128)(2,1)S(1)}, u32[]{:S(2)}) copy-start(bf16[2,64,1,768]{1,3,0,2:T(8,128)(2,1)S(1)} %copy.218) | copy-start | bytes 589828
  714.8 160.3 %all-gather.34.cloned.1.call-start = ((), (), s32[]{:S(2)}) async-start(), calls=%async_computation.26 | async-start | bytes 10027008 | tf_op jit(solution)/shard_map/all_gather | solution.py:234
  716.9 238.1 %all-gather.32.cloned.1.call-start = ((), (), s32[]{:S(2)}) async-start(), calls=%async_computation.25 | async-start | bytes 9437184 | tf_op jit(solution)/shard_map/all_gather | solution.py:42
  800.3 236.7 %all-gather.38.cloned.1.call-start = ((), (), s32[]{:S(2)}) async-start(), calls=%async_computation.29 | async-start | bytes 9437184 | tf_op jit(solution)/shard_map/all_gather | solution.py:52
  805.7 315.5 %all-gather.36.cloned.1.call-start = ((), (), s32[]{:S(2)}) async-start(), calls=%async_computation.27 | async-start | bytes 10027008 | tf_op jit(solution)/shard_map/all_gather | solution.py:235
  806.7 449.6 %reduce-scatter.26.cloned.1.call-start = ((), (), s32[]{:S(2)}) async-start(), calls=%async_computation.30 | async-start | bytes 9437184 | tf_op jit(solution)/shard_map/reduce_scatter | solution.py:56
  1121.2 36.3 %copy-start.64 = (bf16[1536,3072]{1,0:T(8,128)(2,1)S(1)}, bf16[1536,3072]{1,0:T(8,128)(2,1)}, u32[]{:S(2)}) copy-start(bf16[1536,3072]{1,0:T(8,128)(2,1)} %all-gather.34.cloned.1.call-done) | copy-start | bytes 28311556
  1180.9 80.4 %copy-start.56 = (f32[2,512]{1,0:T(2,128)S(1)}, f32[2,512]{1,0:T(2,128)}, u32[]{:S(2)}) copy-start(f32[2,512]{1,0:T(2,128)} %copy-done.55) | copy-start | bytes 12292
  1180.9 80.4 %copy-start.46 = (f32[2,512]{1,0:T(2,128)S(1)}, f32[2,512]{1,0:T(2,128)}, u32[]{:S(2)}) copy-start(f32[2,512]{1,0:T(2,128)} %copy-done.45) | copy-start | bytes 12292
  1180.9 171.0 %all-gather.40.cloned.1.call-start = ((), (), s32[]{:S(2)}) async-start(), calls=%async_computation.31 | async-start | bytes 9437184 | tf_op jit(solution)/shard_map/all_gather | solution.py:52
  1271.5 88.6 %copy-start.31 = (f32[2,12,1024]{2,1,0:T(8,128)S(1)}, f32[2,12,1024]{2,1,0:T(8,128)}, u32[]{:S(2)}) copy-start(f32[2,12,1024]{2,1,0:T(8,128)} %get-tuple-element.560) | copy-start | bytes 294916
  1271.5 187.6 %reduce-scatter.28.cloned.1.call-start = ((), (), s32[]{:S(2)}) async-start(), calls=%async_computation.32 | async-start | bytes 9437184 | tf_op jit(solution)/shard_map/reduce_scatter | solution.py:56
  1381.8 156.4 %reduce-scatter.24.cloned.1.call-start = ((), (), s32[]{:S(2)}) async-start(), calls=%async_computation.28 | async-start | bytes 9437184 | tf_op jit(solution)/shard_map/reduce_scatter | solution.py:46
  1408.1 50.9 %copy-start.40 = (f32[1536]{0:T(1024)S(1)}, f32[1536]{0:T(1024)}, u32[]{:S(2)}) copy-start(f32[1536]{0:T(1024)} %get-tuple-element.454) | copy-start | bytes 18436
  1408.2 50.9 %copy-start.44 = (f32[2,512]{1,0:T(2,128)S(1)}, f32[2,512]{1,0:T(2,128)}, u32[]{:S(2)}) copy-start(f32[2,512]{1,0:T(2,128)} %copy-done.43) | copy-start | bytes 12292
  1408.2 55.9 %copy-start.54 = (f32[2,512]{1,0:T(2,128)S(1)}, f32[2,512]{1,0:T(2,128)}, u32[]{:S(2)}) copy-start(f32[2,512]{1,0:T(2,128)} %copy-done.53) | copy-start | bytes 12292
  1408.2 55.9 %copy-start.50 = (f32[2,512]{1,0:T(2,128)S(1)}, f32[2,512]{1,0:T(2,128)}, u32[]{:S(2)}) copy-start(f32[2,512]{1,0:T(2,128)} %copy-done.49) | copy-start | bytes 12292
  1408.2 263.1 %all-gather.42.cloned.1.call-start = ((), (), s32[]{:S(2)}) async-start(), calls=%async_computation.33 | async-start | bytes 9437184 | tf_op jit(solution)/shard_map/all_gather | solution.py:52
  1553.0 671.1 %reduce-scatter.46.cloned.1.call-start = ((), (), s32[]{:S(2)}) async-start(), calls=%async_computation.42 | async-start | bytes 10027008
  1591.5 637.3 %reduce-scatter.44.cloned.1.call-start = ((), (), s32[]{:S(2)}) async-start(), calls=%async_computation.41 | async-start | bytes 10027008 | tf_op jit(solution)/shard_map/reduce_scatter | solution.py:381
  1617.5 613.6 %reduce-scatter.32.cloned.1.call-start = ((), (), s32[]{:S(2)}) async-start(), calls=%async_computation.35 | async-start | bytes 589824 | tf_op jit(solution)/shard_map/reduce_scatter | solution.py:304
  1635.2 597.5 %all-reduce.4.cloned.1.call-start = ((), (), s32[]{:S(2)}) async-start(), calls=%async_computation.44 | async-start | bytes 9437184
  1651.7 583.0 %reduce-scatter.42.cloned.1.call-start = ((), (), s32[]{:S(2)}) async-start(), calls=%async_computation.40 | async-start | bytes 2506752 | tf_op jit(solution)/shard_map/reduce_scatter | solution.py:378
  1661.8 574.6 %reduce-scatter.40.cloned.1.call-start = ((), (), s32[]{:S(2)}) async-start(), calls=%async_computation.39 | async-start | bytes 2506752 | tf_op jit(solution)/shard_map/reduce_scatter | solution.py:372
  1671.2 567.3 %reduce-scatter.38.cloned.1.call-start = ((), (), s32[]{:S(2)}) async-start(), calls=%async_computation.38 | async-start | bytes 2506752 | tf_op jit(solution)/shard_map/reduce_scatter | solution.py:369
  1680.7 584.7 %reduce-scatter.36.cloned.1.call-start = ((), (), s32[]{:S(2)}) async-start(), calls=%async_computation.37 | async-start | bytes 2506752 | tf_op jit(solution)/shard_map/reduce_scatter | solution.py:366
  1711.8 14.0 copy-start.1
  1711.8 14.0 copy-start.2
  1805.6 14.0 copy-start.1
  1805.6 14.0 copy-start.2
  1926.1 14.0 copy-start.1
  1926.1 14.0 copy-start.2
  2138.4 205.4 %reduce-scatter.34.cloned.1.call-start = ((), (), s32[]{:S(2)}) async-start(), calls=%async_computation.36 | async-start | bytes 5013504 | tf_op jit(solution)/shard_map/reduce_scatter | solution.py:363
  2153.0 269.9 %reduce-scatter.30.cloned.1.call-start = ((), (), s32[]{:S(2)}) async-start(), calls=%async_computation.34 | async-start | bytes 9437184 | tf_op jit(solution)/shard_map/reduce_scatter | solution.py:56
  2179.2 44.2 %copy-start.6 = (bf16[2,512,1536]{2,1,0:T(8,128)(2,1)S(1)}, bf16[2,512,1536]{2,1,0:T(8,128)(2,1)}, u32[]{:S(2)}) copy-start(bf16[2,512,1536]{2,1,0:T(8,128)(2,1)} %reduce-scatter.26.cloned.1.call-done) | copy-start | bytes 9437188
  2179.3 44.7 %copy-start.59 = (bf16[1536]{0:T(1024)(128)(2,1)S(1)}, bf16[1536]{0:T(1024)(128)(2,1)}, u32[]{:S(2)}) copy-start(bf16[1536]{0:T(1024)(128)(2,1)} %get-tuple-element.445) | copy-start | bytes 9220
  2179.3 311.2 %reduce-scatter.48.cloned.1.call-start = ((), (), s32[]{:S(2)}) async-start(), calls=%async_computation.43 | async-start | bytes 417792
  2223.5 15.1 copy-start.60
  2224.0 14.0 copy-start.9
  2224.0 199.0 %copy-start.38 = (f32[1536]{0:T(1024)S(1)}, f32[1536]{0:T(1024)}, u32[]{:S(2)}) copy-start(f32[1536]{0:T(1024)} %copy-done.37) | copy-start | bytes 18436
  2224.0 199.0 %copy-start.42 = (f32[2,512]{1,0:T(2,128)S(1)}, f32[2,512]{1,0:T(2,128)}, u32[]{:S(2)}) copy-start(f32[2,512]{1,0:T(2,128)} %copy-done.41) | copy-start | bytes 12292
  2238.5 189.5 %copy-start.52 = (f32[2,512]{1,0:T(2,128)S(1)}, f32[2,512]{1,0:T(2,128)}, u32[]{:S(2)}) copy-start(f32[2,512]{1,0:T(2,128)} %copy-done.51) | copy-start | bytes 12292
  2345.9 82.6 %copy-start.48 = (f32[2,512]{1,0:T(2,128)S(1)}, f32[2,512]{1,0:T(2,128)}, u32[]{:S(2)}) copy-start(f32[2,512]{1,0:T(2,128)} %copy-done.47) | copy-start | bytes 12292
  (51 other events, 278.0 us)
Sparse Core Ops, SparseCore 0:
  10.9 44.9 all-gather.19
  58.0 79.1 all-gather.15
  140.1 53.4 all-gather.17
  196.2 40.7 all-gather.21
  402.9 75.6 reduce-scatter.19
  481.6 53.4 all-gather.23
  538.1 40.7 all-gather.27
  581.1 79.1 all-gather.25
  663.4 42.2 all-gather.29
  714.9 75.8 reduce-scatter.21
  793.7 81.4 all-gather.33
  876.5 78.4 all-gather.31
  956.6 80.3 all-gather.37
  1039.7 81.4 all-gather.35
  1181.0 75.1 reduce-scatter.25
  1271.6 80.3 all-gather.39
  1381.9 77.0 reduce-scatter.27
  1461.2 77.0 reduce-scatter.23
  1553.1 80.3 all-gather.41
  1638.0 111.3 reduce-scatter.45
  1753.5 111.0 reduce-scatter.43
  1867.5 12.8 reduce-scatter.31
  1884.1 117.0 all-reduce.3
  2004.8 62.5 reduce-scatter.41
  2071.6 62.0 reduce-scatter.39
  2137.3 62.0 reduce-scatter.37
  2203.4 61.8 reduce-scatter.35
  2269.2 74.5 reduce-scatter.33
  2346.8 76.0 reduce-scatter.29
  2434.9 55.5 reduce-scatter.47
where the time goes:
time: 2520 us; the launch traced here: 2500 us
  waiting for transfers between devices  1260 us (50%)
  matrix products  694 us (28%)
  other arithmetic  269 us (11%)
  local copies, waits for them, and re-layouts  182 us (7%)
  blocking collectives  68.2 us (3%)
    all_gather x3, waiting for transfers between devices, widen(): return lax.all_gather(values, 'mp', axis=1, tiled=True)  243 us
    reduce_scatter x3, waiting for transfers between devices, settle(): lax.psum_scatter(partial_sum.astype(jnp.bfloat16), 'mp', scatter_dimensio...  215 us
    reduce_scatter x3, waiting for transfers between devices, settle_grad(): lax.psum_scatter(partial_sum.astype(jnp.bfloat16), 'mp', scatter_dimensio...  203 us
    convert_element_type x18, other arithmetic, rounded(): return values.astype(jnp.bfloat16)  136 us
    all_gather x3, waiting for transfers between devices, widen_grad(): return lax.all_gather(values, 'mp', axis=1, tiled=True)  133 us
    dot_general x6, matrix products, project(): jnp.einsum('cld,de->cle', array, matrix, preferred_element_type=jnp.float32)  100 us
    dot_general x8, matrix products, per_block(): jnp.einsum('qhe,khe->hqk', block_queries, clip_keys, preferred_element_ty...  98.7 us
    dot_general x6, matrix products, outer_sum(): jnp.einsum('cld,cle->de', left, right, preferred_element_type=jnp.float32)  89.5 us
  transfers between devices with their start and end apart: 30, of which 21 were waited for; matrix products, arithmetic and copies ran while one was open for 39% of the time, Pallas kernels for 0%

commit v1 on v0

--- a/solution.py
+++ b/solution.py
@@ -1,6 +1,10 @@
+import functools
+
 import jax
 import jax.numpy as jnp
 from jax import lax
+from jax.experimental import pallas as pl
+from jax.experimental.pallas import tpu as pltpu
 from jax.sharding import PartitionSpec as P
 
 D = 1536
@@ -410,6 +414,968 @@
     )
 
 
+NT = (((1,), (1,)), ((), ()))
+TN = (((0,), (0,)), ((), ()))
+NN = (((1,), (0,)), ((), ()))
+f32 = jnp.float32
+bf16 = jnp.bfloat16
+LANES = 128
+MESH = pl.DeviceIdType.MESH
+Z, Y, CORES = 4, 2, 2
+
+
+def dotf(a, b, dims):
+    return lax.dot_general(a, b, dims, preferred_element_type=f32)
+
+
+def head_masks():
+    lane = lax.broadcasted_iota(jnp.int32, (1, LANES), 1)
+    return [lane < 64, lane >= 64]
+
+
+def self_forward_kernel(rows_at_once, q_ref, k_ref, v_ref, o_ref, lse_ref, peak_ref):
+    frames, size = q_ref.shape[0], rows_at_once
+    masks = head_masks()
+    key_row = lax.broadcasted_iota(jnp.int32, (size, size), 0)
+    query_col = lax.broadcasted_iota(jnp.int32, (size, size), 1)
+    allowed = key_row <= query_col
+    zero = jnp.zeros((), bf16)
+    peaks = [None, None]
+    values = [jnp.where(mask, v_ref[...], zero) for mask in masks]
+    for block in range(frames // size):
+        first = block * size
+        rows = slice(first, first + size)
+        q = q_ref[rows, :] * jnp.asarray(0.125, bf16)
+        mixed = None
+        for h in range(2):
+            qh = jnp.where(masks[h], q, zero)
+            diagonal = jnp.where(allowed, dotf(k_ref[rows, :], qh, NT), MASKED)
+            top = jnp.max(diagonal, axis=0, keepdims=True)
+            if first:
+                full = dotf(k_ref[0:first, :], qh, NT)
+                top = jnp.maximum(top, jnp.max(full, axis=0, keepdims=True))
+            diagonal = jnp.exp(diagonal - top)
+            total = jnp.sum(diagonal, axis=0, keepdims=True)
+            part = dotf(diagonal.astype(bf16), values[h][rows, :], TN)
+            if first:
+                full = jnp.exp(full - top)
+                total = total + jnp.sum(full, axis=0, keepdims=True)
+                part = part + dotf(full.astype(bf16), values[h][0:first, :], TN)
+            lse_ref[h : h + 1, rows] = top + jnp.log(total)
+            part = part * (1.0 / total).reshape(size, 1)
+            mixed = part if mixed is None else mixed + part
+            peaks[h] = top if peaks[h] is None else jnp.maximum(peaks[h], top)
+        o_ref[rows, :] = mixed.astype(bf16)
+    for h in range(2):
+        peak_ref[h : h + 1, :] = jnp.broadcast_to(
+            jnp.max(peaks[h], axis=1, keepdims=True), (1, LANES)
+        )
+
+
+def self_attend(qkv, width):
+    frames, pairs = qkv.shape[1], width // LANES
+    at = lambda offset: pl.BlockSpec((None, frames, LANES), lambda m, i: (m, 0, offset + i))
+    stat = lambda n: pl.BlockSpec((None, None, 8, n), lambda m, i: (m, i, 0, 0))
+    return pl.pallas_call(
+        functools.partial(self_forward_kernel, 512),
+        grid=(2, pairs),
+        out_shape=(
+            jax.ShapeDtypeStruct((2, frames, width), bf16),
+            jax.ShapeDtypeStruct((2, pairs, 8, frames), f32),
+            jax.ShapeDtypeStruct((2, pairs, 8, LANES), f32),
+        ),
+        in_specs=[at(0), at(pairs), at(2 * pairs)],
+        out_specs=(at(0), stat(frames), stat(LANES)),
+        compiler_params=pltpu.CompilerParams(vmem_limit_bytes=40 << 20),
+        cost_estimate=pl.CostEstimate(
+            flops=16 * frames * frames * width,
+            bytes_accessed=16 * frames * width,
+            transcendentals=0,
+        ),
+    )(qkv, qkv, qkv)
+
+
+def self_backward_kernel(
+    rows_at_once, q_ref, k_ref, v_ref, g_ref, lse_ref, dq_ref, dk_ref, dv_ref, dk_sum, dv_sum
+):
+    frames, size = q_ref.shape[0], rows_at_once
+    masks = head_masks()
+    key_row = lax.broadcasted_iota(jnp.int32, (size, size), 0)
+    query_col = lax.broadcasted_iota(jnp.int32, (size, size), 1)
+    allowed = key_row <= query_col
+    zero = jnp.zeros((), bf16)
+    keys = [jnp.where(mask, k_ref[...], zero) for mask in masks]
+    blocks = frames // size
+    for block in reversed(range(blocks)):
+        first = block * size
+        spans = [(slice(first, first + size), True)]
+        if first:
+            spans.append((slice(0, first), False))
+        rows = spans[0][0]
+        q = q_ref[rows, :] * jnp.asarray(0.125, bf16)
+        g = g_ref[rows, :]
+        dq = None
+        dk, dv = [None] * len(spans), [None] * len(spans)
+        for h in range(2):
+            qh, gh = jnp.where(masks[h], q, zero), jnp.where(masks[h], g, zero)
+            lse = lse_ref[h : h + 1, rows]
+            weights, grads, center = [], [], None
+            for span, masked in spans:
+                scores = dotf(k_ref[span, :], qh, NT)
+                if masked:
+                    scores = jnp.where(allowed, scores, MASKED)
+                weights.append(jnp.exp(scores - lse))
+                grads.append(dotf(v_ref[span, :], gh, NT))
+                part = jnp.sum(weights[-1] * grads[-1], axis=0, keepdims=True)
+                center = part if center is None else center + part
+            for i, (span, _) in enumerate(spans):
+                ds = (weights[i] * (grads[i] - center)).astype(bf16)
+                a = dotf(weights[i].astype(bf16), gh, NN)
+                b = dotf(ds, qh, NN)
+                c = dotf(ds, keys[h][span, :], TN)
+                dv[i] = a if dv[i] is None else dv[i] + a
+                dk[i] = b if dk[i] is None else dk[i] + b
+                dq = c if dq is None else dq + c
+        dq_ref[rows, :] = (dq * 0.125).astype(bf16)
+        for i, (span, _) in enumerate(spans):
+            if block == blocks - 1:
+                dk_sum[span, :] = dk[i]
+                dv_sum[span, :] = dv[i]
+            else:
+                dk_sum[span, :] += dk[i]
+                dv_sum[span, :] += dv[i]
+    dk_ref[...] = dk_sum[...].astype(bf16)
+    dv_ref[...] = dv_sum[...].astype(bf16)
+
+
+class Hop:
+    def __init__(self, kind, group):
+        self.kind, self.group = kind, group
+        rows, width = group.rows // 2, group.width
+        self.chunk = (rows, width)
+        self.count = {"x1": 8, "y1": 8, "y2": 4, "x2": 4, "za": 3, "zb": 3}[kind]
+        self.lead = {"x1": (Z, Y), "y1": (2, Z), "y2": (Z,), "x2": (Z,), "za": (3,), "zb": (3,)}[kind]
+        self.names = {
+            "x1": ["own", "there"],
+            "y1": ["own", "there"],
+            "y2": ["own", "there", "x1"],
+            "x2": ["own", "there", "y1"],
+            "za": ["own", "there", "x1", "y2"],
+            "zb": ["own", "there", "y1", "x2"],
+        }[kind]
+
+    def shape(self):
+        return jax.ShapeDtypeStruct(self.lead + self.chunk, bf16)
+
+    def scratch(self):
+        return [
+            pltpu.VMEM((self.count, len(self.names)) + self.chunk, bf16),
+            pltpu.VMEM((self.count,) + self.chunk, bf16),
+            pltpu.SemaphoreType.DMA((self.count, len(self.names))),
+            pltpu.SemaphoreType.DMA((self.count,)),
+            pltpu.SemaphoreType.DMA((self.count,)),
+        ]
+
+    def bind(self, sources, target, scratch):
+        self.sources, self.target = sources, target
+        self.loads, self.sent, self.load_sem, self.send_sem, self.recv_sem = scratch
+
+    def index(self, t):
+        half = self.chunk[0]
+        low, high = pl.ds(0, half), pl.ds(half, half)
+        if self.kind == "x1":
+            at = (1, t // 2, t % 2, low)
+            return [at, at], (t // 2, t % 2)
+        if self.kind == "y1":
+            at = (t // 4, t % 4, 1, high)
+            return [at, at], (t // 4, t % 4)
+        if self.kind == "y2":
+            at = (0, t, 1, low)
+            return [at, at, (t, 1)], (t,)
+        if self.kind == "x2":
+            at = (1, t, 0, high)
+            return [at, at, (1, t)], (t,)
+        z = (lax.axis_index("dp") // (Y * CORES) + t + 1) % Z
+        if self.kind == "za":
+            at = (0, z, 0, low)
+            return [at, at, (z, 0), (z,)], (t,)
+        at = (0, z, 0, high)
+        return [at, at, (0, z), (z,)], (t,)
+
+    def partner(self, t):
+        dp, mp = lax.axis_index("dp"), lax.axis_index("mp")
+        if self.kind in ("x1", "x2"):
+            return (dp, 1 - mp)
+        if self.kind in ("y1", "y2"):
+            return (dp + CORES - 2 * CORES * ((dp // CORES) % Y), mp)
+        group = Y * CORES
+        return (((dp // group + t + 1) % Z) * group + dp % group, mp)
+
+    def partners(self):
+        return [self.partner(t) for t in range(3 if self.kind in ("za", "zb") else 1)]
+
+    def load(self, t):
+        return [
+            pltpu.make_async_copy(source.at[at], self.loads.at[t, i], self.load_sem.at[t, i])
+            for i, (source, at) in enumerate(zip(self.sources, self.index(t)[0]))
+        ]
+
+    def send(self, t):
+        return pltpu.make_async_remote_copy(
+            src_ref=self.sent.at[t],
+            dst_ref=self.target.at[self.index(t)[1]],
+            send_sem=self.send_sem.at[t],
+            recv_sem=self.recv_sem.at[t],
+            device_id=self.partner(t),
+            device_id_type=MESH,
+        )
+
+    def begin(self):
+        for t in range(self.count):
+            for copy in self.load(t):
+                copy.start()
+
+    def each(self, steps):
+        return self.count if steps < 3 else -(-self.count // 2)
+
+    def work(self, step, steps, j):
+        t = step * self.each(steps) + j
+
+        @pl.when(t < self.count)
+        def _():
+            for copy in self.load(t):
+                copy.wait()
+            total = self.loads[t, 0].astype(f32)
+            for i in range(1, len(self.names)):
+                total = total + self.loads[t, i].astype(f32)
+            self.sent[t] = total.astype(bf16)
+            self.send(t).start()
+
+    def finish(self):
+        for t in range(self.count):
+            self.send(t).wait()
+
+
+class Group:
+    def __init__(self, own, there):
+        self.arrays = {"own": own, "there": there}
+        self.rows, self.width = own.shape[3], own.shape[4]
+
+    def result(self, z):
+        a = self.arrays
+        half = self.rows // 2
+        take = lambda array, at=0: lax.dynamic_index_in_dim(array, z, at, keepdims=False)
+        total = take(a["own"][0, :, 0]).astype(f32) + take(a["there"][0, :, 0]).astype(f32)
+        low = take(a["x1"][:, 0]).astype(f32) + take(a["y2"]).astype(f32)
+        high = take(a["y1"][0]).astype(f32) + take(a["x2"]).astype(f32)
+        for k in range(3):
+            low = low + a["za"][k].astype(f32)
+            high = high + a["zb"][k].astype(f32)
+        return total + jnp.concatenate([low, high], axis=0)
+
+
+def meet(partners):
+    barrier = pltpu.get_barrier_semaphore()
+    for partner in partners:
+        pl.semaphore_signal(barrier, inc=1, device_id=partner, device_id_type=MESH)
+    pl.semaphore_wait(barrier, len(partners))
+
+
+def core_partner():
+    dp = lax.axis_index("dp")
+    return (dp + 1 - 2 * (dp % CORES), lax.axis_index("mp"))
+
+
+def hosted(body, number, grid, args, in_specs, out_shape, out_specs, scratch, plan, flops, core=False):
+    hops = [Hop(kind, group) for kind, group in plan]
+    arrays, places = [], {}
+    for hop in hops:
+        for name in hop.names:
+            key = (id(hop.group), name)
+            if key not in places:
+                places[key] = len(arrays)
+                arrays.append(hop.group.arrays[name])
+    steps = 1
+    for n in grid:
+        steps *= n
+    kinds = set(hop.kind[0] for hop in hops)
+
+    def kernel(*refs):
+        counts = [len(args), len(arrays), len(out_shape), len(hops), len(scratch)]
+        parts, at = [], 0
+        for n in counts:
+            parts.append(refs[at : at + n])
+            at += n
+        for k, hop in enumerate(hops):
+            sources = [parts[1][places[(id(hop.group), name)]] for name in hop.names]
+            hop.bind(sources, parts[3][k], refs[at : at + 5])
+            at += 5
+        step = 0
+        for axis, n in enumerate(grid):
+            step = step * n + pl.program_id(axis)
+
+        @pl.when(step == 0)
+        def _():
+            partners = [core_partner()] if core else []
+            for kind in sorted(kinds):
+                partners += [hop for hop in hops if hop.kind[0] == kind][0].partners()
+            if partners:
+                meet(partners)
+            for hop in hops:
+                hop.begin()
+
+        for j in range(max([hop.each(steps) for hop in hops], default=0)):
+            for hop in hops:
+                if j < hop.each(steps):
+                    hop.work(step, steps, j)
+        body(*parts[0], *parts[2], *parts[4])
+
+        @pl.when(step == steps - 1)
+        def _():
+            for hop in hops:
+                hop.finish()
+
+    hbm = pl.BlockSpec(memory_space=pl.ANY)
+    extra = [s for hop in hops for s in hop.scratch()]
+    outs = pl.pallas_call(
+        kernel,
+        grid=grid,
+        in_specs=list(in_specs) + [hbm] * len(arrays),
+        out_specs=tuple(out_specs) + (hbm,) * len(hops),
+        out_shape=tuple(out_shape) + tuple(hop.shape() for hop in hops),
+        scratch_shapes=list(scratch) + extra,
+        compiler_params=pltpu.CompilerParams(
+            vmem_limit_bytes=56 << 20,
+            **(dict(collective_id=number, has_side_effects=True) if hops or core else {}),
+        ),
+        cost_estimate=pl.CostEstimate(flops=flops, bytes_accessed=flops // 500, transcendentals=0),
+    )(*args, *arrays)
+    for hop, array in zip(hops, outs[len(out_shape) :]):
+        hop.group.arrays[hop.kind] = array
+    return outs[: len(out_shape)]
+
+
+def self_attend_back(number, plan, qkv, grad, lse, width, begin, end):
+    frames, pairs = qkv.shape[1], width // LANES
+    at = lambda offset: pl.BlockSpec((None, frames, LANES), lambda m, i: (m, 0, offset + i))
+    out = jax.ShapeDtypeStruct((2, frames, (end - begin) * LANES), bf16)
+    return hosted(
+        functools.partial(self_backward_kernel, 256),
+        number,
+        (2, end - begin),
+        [qkv, qkv, qkv, grad, lse],
+        [
+            at(begin),
+            at(pairs + begin),
+            at(2 * pairs + begin),
+            at(begin),
+            pl.BlockSpec((None, None, 8, frames), lambda m, i: (m, begin + i, 0, 0)),
+        ],
+        [out] * 3,
+        [at(0)] * 3,
+        [pltpu.VMEM((frames, LANES), f32)] * 2,
+        plan,
+        16 * frames * frames * LANES * (end - begin),
+    )
+
+
+def half_spec(array, half):
+    if array.ndim == 2:
+        return pl.BlockSpec(array.shape, lambda *grid: (0, 0), pipeline_mode=pl.Buffered(1))
+    return pl.BlockSpec(
+        (None,) + array.shape[1:], lambda *grid: (half, 0, 0), pipeline_mode=pl.Buffered(1)
+    )
+
+
+def exchanged_grad(number, plan, xs, tiles, rows):
+    depth = xs[0].shape[1]
+    specs = [pl.BlockSpec(x.shape, lambda j, m: (0, 0), pipeline_mode=pl.Buffered(1)) for x in xs]
+    args, halves = list(xs), []
+    for _, arrays in tiles:
+        halves.append([])
+        for half in range(2):
+            halves[-1].append(range(len(args), len(args) + len(arrays)))
+            args += arrays
+            specs += [half_spec(array, half) for array in arrays]
+    tile = sum(array.shape[2] for array in tiles[0][1])
+    count = len(tiles)
+    steps = 2 * count
+    longest = max(x.shape[0] for x in xs)
+    shape = jax.ShapeDtypeStruct((2, Z, Y, rows, count * tile), bf16)
+    hbm = pl.BlockSpec(memory_space=pl.ANY)
+
+    def body(*refs):
+        own_ref, there_ref = refs[len(args) : len(args) + 2]
+        turned, own, other, own_sem, send_sem, recv_sem = refs[len(args) + 2 :]
+        dp, mp = lax.axis_index("dp"), lax.axis_index("mp")
+        core, across = dp % CORES, (dp // CORES) % Y
+        j, m = pl.program_id(0), pl.program_id(1)
+        step = 2 * j + m
+
+        def place(step):
+            column = (step // 2) * tile
+            column = column if isinstance(column, int) else pl.multiple_of(column, LANES)
+            every = slice(None)
+            return ((step + mp) % 2, every, every, every, pl.ds(column, tile))
+
+        def kept(step):
+            slot = step % 2
+            return pltpu.make_async_copy(own.at[slot], own_ref.at[place(step)], own_sem.at[slot])
+
+        def sent(step):
+            return pltpu.make_async_remote_copy(
+                src_ref=other.at[step % 2],
+                dst_ref=there_ref.at[place(step)],
+                send_sem=send_sem.at[step],
+                recv_sem=recv_sem.at[step],
+                device_id=core_partner(),
+                device_id_type=MESH,
+            )
+
+        @pl.when(step >= 2)
+        def _():
+            kept(step - 2).wait()
+            sent(step - 2).wait_send()
+
+        for k, (source, _) in enumerate(tiles):
+            frames = xs[source].shape[0]
+
+            if k == 0 or tiles[k - 1][0] != source:
+
+                @pl.when((j == k) & (m == 0))
+                def _(source=source, frames=frames):
+                    turned[:, 0:frames] = refs[source][...].T
+
+            for half in range(2):
+
+                @pl.when((j == k) & (m == half))
+                def _(k=k, half=half, frames=frames):
+                    pieces = [refs[i][...] for i in halves[k][half]]
+                    y = pieces[0] if len(pieces) == 1 else jnp.concatenate(pieces, axis=1)
+                    for z in range(Z):
+                        span = slice(z * Y * CORES * rows, (z + 1) * Y * CORES * rows)
+                        part = dotf(turned[span, 0:frames], y, NN).astype(bf16)
+                        for i in range(Y):
+                            first = part[2 * i * rows : (2 * i + 1) * rows]
+                            second = part[(2 * i + 1) * rows : (2 * i + 2) * rows]
+                            own[m, z, (i + across) % 2] = jnp.where(core == 0, first, second)
+                            other[m, z, (i + across) % 2] = jnp.where(core == 0, second, first)
+
+        kept(step).start()
+        sent(step).start()
+
+        @pl.when(step == steps - 1)
+        def _():
+            for t in (steps - 2, steps - 1):
+                kept(t).wait()
+                sent(t).wait_send()
+            for t in range(steps):
+                sent(t).wait_recv()
+
+    outs = hosted(
+        body,
+        number,
+        (count, 2),
+        args,
+        specs,
+        [shape, shape],
+        [hbm, hbm],
+        [
+            pltpu.VMEM((depth, longest), bf16),
+            pltpu.VMEM((2, Z, Y, rows, tile), bf16),
+            pltpu.VMEM((2, Z, Y, rows, tile), bf16),
+            pltpu.SemaphoreType.DMA((2,)),
+            pltpu.SemaphoreType.DMA((steps,)),
+            pltpu.SemaphoreType.DMA((steps,)),
+        ],
+        plan,
+        4 * longest * depth * count * tile,
+        core=True,
+    )
+    return Group(*outs)
+
+
+def project_kernel(x_ref, w_ref, o_ref):
+    step = x_ref.shape[0] // 4
+    for i in range(4):
+        rows = slice(i * step, (i + 1) * step)
+        o_ref[rows, :] = dotf(x_ref[rows, :], w_ref[...], NN).astype(o_ref.dtype)
+
+
+def project_both(x, whole, begin, width, tile=768):
+    (frames, depth), first = x.shape, begin // tile
+    return pl.pallas_call(
+        project_kernel,
+        grid=(2, width // tile),
+        in_specs=[
+            pl.BlockSpec((frames, depth), lambda m, j: (0, 0)),
+            pl.BlockSpec((None, depth, tile), lambda m, j: (m, 0, first + j)),
+        ],
+        out_specs=pl.BlockSpec((None, frames, tile), lambda m, j: (m, 0, j)),
+        out_shape=jax.ShapeDtypeStruct((2, frames, width), bf16),
+        compiler_params=pltpu.CompilerParams(vmem_limit_bytes=40 << 20),
+        cost_estimate=pl.CostEstimate(
+            flops=4 * frames * depth * width,
+            bytes_accessed=4 * (frames + depth) * width,
+            transcendentals=0,
+        ),
+    )(x, whole)
+
+
+def unproject_both(number, plan, pieces, whole, begin, width, base=None):
+    frames, depth, tile = pieces[0][0].shape[-2], whole.shape[1], 256
+    first, direct = begin // width, len(pieces) == 2
+    bases = [] if base is None else [base]
+
+    def body(*refs):
+        n = len(pieces)
+        w_refs, refs_left = refs[n : n + 2], refs[n + 2 :]
+        o_ref = refs_left[len(bases)]
+
+        if not direct:
+            joint = refs_left[-1]
+
+            @pl.when(pl.program_id(0) == 0)
+            def _():
+                for ref, (_, half, column) in zip(refs, pieces):
+                    joint[half, :, column : column + ref.shape[1]] = ref[...]
+
+        for i in range(4):
+            rows = slice(i * frames // 4, (i + 1) * frames // 4)
+            ys = [refs[m][rows, :] if direct else joint[m, rows, :] for m in range(2)]
+            total = dotf(ys[0], w_refs[0][...], NT) + dotf(ys[1], w_refs[1][...], NT)
+            o_ref[rows, :] = refs_left[0][rows, :] + total if bases else total
+
+    weights = lambda m: pl.BlockSpec((None, tile, width), lambda j: (m, j, first))
+    across = pl.BlockSpec((frames, tile), lambda j: (0, j))
+    return hosted(
+        body,
+        number,
+        (depth // tile,),
+        [p[0] for p in pieces] + [whole, whole] + bases,
+        [half_spec(array, half) for array, half, _ in pieces] + [weights(0), weights(1)] + [across] * len(bases),
+        [jax.ShapeDtypeStruct((frames, depth), f32)],
+        [across],
+        [] if direct else [pltpu.VMEM((2, frames, width), bf16)],
+        plan,
+        4 * frames * depth * width,
+    )[0]
+
+
+def halves_of(array):
+    return [(array, 0, 0), (array, 1, 0)]
+
+
+def relay(number, plan, value):
+    def body(value_ref, total_ref, sums, got, send_sem, recv_sem):
+        dp, mp = lax.axis_index("dp"), lax.axis_index("mp")
+        group = Y * CORES
+        z, rest = dp // group, dp % group
+        partners = [core_partner(), (dp, 1 - mp), (dp + CORES - 2 * CORES * ((dp // CORES) % Y), mp)]
+        partners.append(((z + 1 - 2 * (z % 2)) * group + rest, mp))
+        partners.append((((z + 2) % Z) * group + rest, mp))
+        sums[0] = value_ref[...]
+        for i, partner in enumerate(partners):
+            copy = pltpu.make_async_remote_copy(
+                src_ref=sums.at[i],
+                dst_ref=got.at[i],
+                send_sem=send_sem.at[i],
+                recv_sem=recv_sem.at[i],
+                device_id=partner,
+                device_id_type=MESH,
+            )
+            copy.start()
+            copy.wait()
+            sums[i + 1] = sums[i] + got[i]
+        total_ref[...] = sums[5]
+
+    whole = pl.BlockSpec(value.shape, lambda i: (0, 0))
+    return hosted(
+        body,
+        number,
+        (1,),
+        [value],
+        [whole],
+        [jax.ShapeDtypeStruct(value.shape, f32)],
+        [whole],
+        [
+            pltpu.VMEM((6,) + value.shape, f32),
+            pltpu.VMEM((5,) + value.shape, f32),
+            pltpu.SemaphoreType.DMA((5,)),
+            pltpu.SemaphoreType.DMA((5,)),
+        ],
+        plan,
+        10**9,
+        core=True,
+    )[0]
+
+
+def last_hop(number, plan):
+    hosted(lambda: None, number, (1,), [], [], [], [], [], plan, 10**9)
+
+
+def pair_rows(array, masks):
+    zero = jnp.zeros((), bf16)
+    return jnp.concatenate([jnp.where(mask, array, zero) for mask in masks], axis=0)
+
+
+def cross_weights_of(q, keys, masks):
+    scores = dotf(q * jnp.asarray(0.125, bf16), keys, NT)
+    tops = [jnp.max(jnp.where(mask, scores, MASKED), axis=1, keepdims=True) for mask in masks]
+    exponents = jnp.exp(scores - jnp.where(masks[0], tops[0], tops[1]))
+    sums = [jnp.sum(jnp.where(mask, exponents, 0.0), axis=1, keepdims=True) for mask in masks]
+    return exponents * jnp.where(masks[0], 1.0 / sums[0], 1.0 / sums[1]), tops
+
+
+def cross_forward_kernel(q_ref, k_ref, v_ref, o_ref, peak_ref):
+    masks = head_masks()
+    weights, tops = cross_weights_of(q_ref[...], pair_rows(k_ref[...], masks), masks)
+    o_ref[...] = dotf(weights.astype(bf16), pair_rows(v_ref[...], masks), NN).astype(bf16)
+    for h in range(2):
+        peak_ref[h : h + 1, :] = jnp.broadcast_to(
+            jnp.max(tops[h], axis=0, keepdims=True), (1, LANES)
+        )
+
+
+def cross_specs(frames, text, pairs):
+    at = lambda n, offset: pl.BlockSpec((None, n, LANES), lambda m, i: (m, 0, offset + i))
+    return at(frames, 0), at(text, 0), at(text, pairs)
+
+
+def cross_attend(q, kv, width):
+    frames, text, pairs = q.shape[1], kv.shape[1], width // LANES
+    long, keys, values = cross_specs(frames, text, pairs)
+    return pl.pallas_call(
+        cross_forward_kernel,
+        grid=(2, pairs),
+        out_shape=(
+            jax.ShapeDtypeStruct((2, frames, width), bf16),
+            jax.ShapeDtypeStruct((2, pairs, 8, LANES), f32),
+        ),
+        in_specs=[long, keys, values],
+        out_specs=(long, pl.BlockSpec((None, None, 8, LANES), lambda m, i: (m, i, 0, 0))),
+        compiler_params=pltpu.CompilerParams(vmem_limit_bytes=32 << 20),
+        cost_estimate=pl.CostEstimate(
+            flops=32 * frames * LANES * width, bytes_accessed=8 * frames * width, transcendentals=0
+        ),
+    )(q, kv, kv)
+
+
+def cross_backward_kernel(q_ref, k_ref, v_ref, g_ref, dq_ref, dk_ref, dv_ref):
+    masks = head_masks()
+    text = k_ref.shape[0]
+    keys, values = pair_rows(k_ref[...], masks), pair_rows(v_ref[...], masks)
+    q, g = q_ref[...], g_ref[...]
+    weights, _ = cross_weights_of(q, keys, masks)
+    grads = dotf(g, values, NT)
+    products = weights * grads
+    centers = [jnp.sum(jnp.where(mask, products, 0.0), axis=1, keepdims=True) for mask in masks]
+    ds = (weights * (grads - jnp.where(masks[0], centers[0], centers[1]))).astype(bf16)
+    dq_ref[...] = (dotf(ds, keys, NN) * 0.125).astype(bf16)
+    dk = dotf(ds, q, TN) * 0.125
+    dv = dotf(weights.astype(bf16), g, TN)
+    dk_ref[...] = jnp.where(masks[0], dk[:text], dk[text:]).astype(bf16)
+    dv_ref[...] = jnp.where(masks[0], dv[:text], dv[text:]).astype(bf16)
+
+
+def cross_attend_back(q, kv, grad, width):
+    frames, text, pairs = q.shape[1], kv.shape[1], width // LANES
+    long, keys, values = cross_specs(frames, text, pairs)
+    return pl.pallas_call(
+        cross_backward_kernel,
+        grid=(2, pairs),
+        out_shape=(
+            jax.ShapeDtypeStruct((2, frames, width), bf16),
+            jax.ShapeDtypeStruct((2, text, width), bf16),
+            jax.ShapeDtypeStruct((2, text, width), bf16),
+        ),
+        in_specs=[long, keys, values, long],
+        out_specs=(long, keys, keys),
+        compiler_params=pltpu.CompilerParams(vmem_limit_bytes=32 << 20),
+        cost_estimate=pl.CostEstimate(
+            flops=64 * frames * LANES * width, bytes_accessed=12 * frames * width, transcendentals=0
+        ),
+    )(q, kv, kv, grad)
+
+
+def weight_grad_whole_kernel(x_ref, y0_ref, y1_ref, *refs):
+    half, tile = pl.program_id(0), pl.program_id(1)
+    o_ref, turned = refs[-2:]
+
+    @pl.when((half == 0) & (tile == 0))
+    def _():
+        turned[...] = x_ref[...].T
+
+    for m, y_ref in enumerate((y0_ref, y1_ref)):
+
+        @pl.when(half == m)
+        def _(y_ref=y_ref):
+            step = o_ref.shape[0] // 4
+            for i in range(4):
+                rows = slice(i * step, (i + 1) * step)
+                o_ref[rows, :] = dotf(turned[rows, :], y_ref[...], NN).astype(bf16)
+
+
+def weight_grad_whole(x, ys, tile, columns, begin, into=None):
+    frames, depth = x.shape
+    width = ys[0].shape[1]
+    tiles, first = width // tile, begin // tile
+    given = [] if into is None else [into]
+    return pl.pallas_call(
+        weight_grad_whole_kernel,
+        grid=(2, tiles),
+        in_specs=[
+            pl.BlockSpec((frames, depth), lambda m, j: (0, 0)),
+            pl.BlockSpec((frames, tile), lambda m, j: (0, jnp.where(m == 0, j, tiles - 1))),
+            pl.BlockSpec((frames, tile), lambda m, j: (0, jnp.where(m == 0, 0, j))),
+        ]
+        + [pl.BlockSpec(memory_space=pl.ANY)] * len(given),
+        out_specs=pl.BlockSpec((None, depth, tile), lambda m, j: (m, 0, first + j)),
+        scratch_shapes=[pltpu.VMEM((depth, frames), bf16)],
+        out_shape=jax.ShapeDtypeStruct((2, depth, columns), bf16),
+        input_output_aliases={3: 0} if given else {},
+        compiler_params=pltpu.CompilerParams(vmem_limit_bytes=40 << 20),
+        cost_estimate=pl.CostEstimate(
+            flops=4 * frames * depth * width,
+            bytes_accessed=4 * (depth + frames) * width + 2 * frames * depth,
+            transcendentals=0,
+        ),
+    )(x, *ys, *given)
+
+
+def swap(values, axis_name, pairs):
+    return lax.ppermute(values, axis_name, pairs)
+
+
+MP_PAIRS = [(0, 1), (1, 0)]
+CORE_PAIRS = [(i, i ^ 1) for i in range(Z * Y * CORES)]
+
+
+def over_all(value, join):
+    value = join(value, swap(value, "dp", CORE_PAIRS))
+    value = join(value, swap(value, "mp", MP_PAIRS))
+    for bit in (2, 4, 8):
+        pairs = [(i, i ^ bit) for i in range(Z * Y * CORES)]
+        value = join(value, swap(value, "dp", pairs))
+    return value
+
+
+def joined(arrays):
+    return jnp.concatenate(arrays, axis=1)
+
+
+def norm_rows_of(stream):
+    center = stream - jnp.mean(stream, axis=-1, keepdims=True)
+    inverse = lax.rsqrt(jnp.mean(center * center, axis=-1, keepdims=True) + EPSILON)
+    return center * inverse, inverse
+
+
+def norm_back(stream, gain, grad):
+    rows, inverse = norm_rows_of(stream)
+    scaled = grad * gain
+    back = inverse * (
+        scaled
+        - jnp.mean(scaled, axis=-1, keepdims=True)
+        - rows * jnp.mean(scaled * rows, axis=-1, keepdims=True)
+    )
+    return back, jnp.sum(grad * rows, axis=0), jnp.sum(grad, axis=0)
+
+
+def clip_per_device(
+    inputs,
+    text_states,
+    cotangent,
+    norm_params,
+    self_query_key,
+    self_value,
+    self_output,
+    cross_query,
+    cross_key_value,
+    cross_output,
+    hidden_in,
+    hidden_out,
+):
+    dp, mp = lax.axis_index("dp"), lax.axis_index("mp")
+    z = dp // (Y * CORES)
+    rows, width = self_value.shape
+    both = range(2)
+
+    def gathered(pieces):
+        shard = jnp.concatenate([rounded(p).reshape(rows, -1) for p in pieces], axis=1)
+        whole = lax.all_gather(shard, ("mp", "dp"), axis=0, tiled=True)
+        return whole.reshape(2, D, shard.shape[1])
+
+    def to_clip(array, kind):
+        own = lax.dynamic_index_in_dim(array, mp, 0, keepdims=False)
+        sent = rounded(lax.dynamic_index_in_dim(array, 1 - mp, 0, keepdims=False))
+        own, got = own.astype(kind), swap(sent, "mp", MP_PAIRS).astype(kind)
+        return jnp.where(
+            mp == 0, jnp.concatenate([own, got], axis=0), jnp.concatenate([got, own], axis=0)
+        )
+
+    def to_frames(array):
+        count = array.shape[0] // 2
+        own = lax.dynamic_slice_in_dim(array, mp * count, count, 0)
+        sent = rounded(lax.dynamic_slice_in_dim(array, (1 - mp) * count, count, 0))
+        got = swap(sent, "mp", MP_PAIRS).astype(f32)
+        return jnp.where(mp == 0, jnp.stack([own, got]), jnp.stack([got, own]))
+
+    norms_padded = jnp.pad(norm_params, ((0, 0), (0, LANES - norm_params.shape[1])))
+    hidden = hidden_in.shape[1]
+    self_all = gathered([self_query_key, self_value, self_output, norms_padded])
+    cross_all = gathered([cross_query, cross_key_value, cross_output, hidden_in])
+    out_all = gathered([hidden_out])
+    norms = self_all[0, :, 4 * width : 4 * width + norm_params.shape[1]].astype(f32).T
+    self_o = [self_all[m, :, 3 * width : 4 * width] for m in both]
+    cross_q = [cross_all[m, :, :width] for m in both]
+    cross_kv = [cross_all[m, :, width : 3 * width] for m in both]
+    cross_o = [cross_all[m, :, 3 * width : 4 * width] for m in both]
+    in_w = [cross_all[m, :, 4 * width :] for m in both]
+
+    def times(array, matrix):
+        return dotf(array, matrix, NN)
+
+    def times_turned(arrays, matrices):
+        return dotf(arrays[0], matrices[0], NT) + dotf(arrays[1], matrices[1], NT)
+
+    stream = to_clip(inputs, f32)
+    states = to_clip(text_states, bf16)
+    normed_self = rounded(norm_rows_of(stream)[0] * norms[0] + norms[1])
+    qkv = project_both(normed_self, self_all, 0, 3 * width)
+    qkv, cotangent = lax.optimization_barrier((qkv, cotangent))
+    upstream = to_clip(cotangent, f32)
+    mixed_self, lse, self_peaks = self_attend(qkv, width)
+    after_self = unproject_both(0, [], halves_of(mixed_self), self_all, 3 * width, width, stream)
+    normed_cross = rounded(norm_rows_of(after_self)[0] * norms[2] + norms[3])
+    queries = project_both(normed_cross, cross_all, 0, width)
+    text_kv = jnp.stack([rounded(times(states, cross_kv[m])) for m in both])
+    mixed_cross, cross_peaks = cross_attend(queries, text_kv, width)
+    after_cross = unproject_both(0, [], halves_of(mixed_cross), cross_all, 3 * width, width, after_self)
+    normed_hidden = rounded(norm_rows_of(after_cross)[0] * norms[4] + norms[5])
+    upward = [times(normed_hidden, in_w[m]) for m in both]
+    activated, pulls = zip(*[jax.vjp(gelu_exact, up) for up in upward])
+    activated = [rounded(a) for a in activated]
+
+    branch = rounded(upstream)
+    hidden_grad = weight_grad_whole(branch, activated, 512, 2 * hidden, hidden)
+    def peaks_of(peaks):
+        return peaks[:, :, :2, 0].reshape(2, -1)
+
+    tops = over_all(jnp.stack([peaks_of(self_peaks), peaks_of(cross_peaks)]), jnp.maximum)
+    tops = lax.dynamic_index_in_dim(tops, mp, 1, keepdims=False)
+    factors = CLIP_LIMIT / jnp.maximum(tops, CLIP_LIMIT)
+    root_scales = jnp.repeat(jnp.sqrt(factors), D // HEADS, axis=1)
+    clipped = (
+        self_query_key * root_scales[0][None, None, :],
+        cross_query * root_scales[1][None, :],
+        cross_key_value[:, 0] * root_scales[1][None, :],
+    )
+    out_all, hidden_grad, clipped = lax.optimization_barrier((out_all, hidden_grad, clipped))
+    grad_up = [rounded(pulls[m](times(branch, out_all[m]))[0]) for m in both]
+    hidden_grad = weight_grad_whole(normed_hidden, grad_up, 512, 2 * hidden, 0, hidden_grad)
+    grad_up, hidden_grad = lax.optimization_barrier((grad_up, hidden_grad))
+    shard_hidden = lax.psum_scatter(
+        hidden_grad.reshape(2 * D, 2 * hidden), ("mp", "dp"), scatter_dimension=0, tiled=True
+    ).astype(f32)
+    back, gain_three, bias_three = norm_back(
+        after_cross, norms[4], times_turned(grad_up, in_w)
+    )
+    grad_stream = upstream + back
+
+    branch_cross = rounded(grad_stream)
+    grad_mixed = project_both(branch_cross, cross_all, 3 * width, width)
+    dq, dk, dv = cross_attend_back(queries, text_kv, grad_mixed, width)
+    grad_normed = unproject_both(0, [], halves_of(dq), cross_all, 0, width)
+    back, gain_two, bias_two = norm_back(after_self, norms[2], grad_normed)
+    dkv = [joined([dk[m], dv[m]]) for m in both]
+    grad_text = to_frames(times_turned(dkv, cross_kv))
+    grad_stream = grad_stream + back
+    branch_self = rounded(grad_stream)
+    group_pair = exchanged_grad(1, [], [normed_cross, states], [(0, [dq]), (1, [dk]), (1, [dv])], rows)
+    group_out = exchanged_grad(
+        2, [], [branch_cross, branch_self], [(0, [mixed_cross]), (1, [mixed_self])], rows
+    )
+    grad_mixed = project_both(branch_self, self_all, 3 * width, width)
+    cut = width // 2 // LANES
+    early = self_attend_back(
+        3, [("x1", group_pair), ("y1", group_pair)], qkv, grad_mixed, lse, width, 0, cut
+    )
+    activated, early = lax.optimization_barrier((activated, early))
+    output = unproject_both(
+        4, [("x1", group_out), ("y1", group_out)], [(a, m, 0) for m, a in enumerate(activated)], out_all, 0, hidden, after_cross
+    )
+    output = to_frames(output)
+    group_early = exchanged_grad(
+        5, [("x2", group_pair), ("y2", group_pair)], [normed_self], [(0, list(early))], rows
+    )
+    late = self_attend_back(
+        6,
+        [("x2", group_out), ("y2", group_out), ("za", group_pair), ("zb", group_pair)],
+        qkv,
+        grad_mixed,
+        lse,
+        width,
+        cut,
+        2 * cut,
+    )
+    late, output, grad_text = lax.optimization_barrier((late, output, grad_text))
+    group_late = exchanged_grad(
+        7, [("x1", group_early), ("y1", group_early)], [normed_self], [(0, list(late))], rows
+    )
+    pieces = []
+    for half in both:
+        for part, arrays in enumerate((early, late)):
+            pieces += [(a, half, i * width + part * cut * LANES) for i, a in enumerate(arrays)]
+    grad_normed = unproject_both(
+        8,
+        [
+            ("x1", group_late),
+            ("y1", group_late),
+            ("x2", group_early),
+            ("y2", group_early),
+            ("za", group_out),
+            ("zb", group_out),
+        ],
+        pieces,
+        self_all,
+        0,
+        3 * width,
+    )
+    back, gain_one, bias_one = norm_back(stream, norms[0], grad_normed)
+    norm_grads = jnp.stack([gain_one, bias_one, gain_two, bias_two, gain_three, bias_three])
+    grad_inputs, norm_grads = lax.optimization_barrier((grad_stream + back, norm_grads))
+    grad_inputs = to_frames(grad_inputs)
+    norm_grads = relay(
+        9,
+        [("x2", group_late), ("y2", group_late), ("za", group_early), ("zb", group_early)],
+        jnp.pad(norm_grads, ((0, 2), (0, 0))),
+    )[:6]
+    last_hop(10, [("za", group_late), ("zb", group_late)])
+    shard_pair, shard_outs = group_pair.result(z), group_out.result(z)
+    halves = [group_early.result(z), group_late.result(z)]
+    half = width // 2
+    shard_self = [joined([h[:, i * half : (i + 1) * half] for h in halves]) for i in range(3)]
+
+    shard_norms = lax.dynamic_slice_in_dim(norm_grads, dp * rows, rows, 1).T
+
+    return (
+        output,
+        grad_inputs,
+        grad_text,
+        shard_norms,
+        jnp.stack(shard_self[:2], axis=1),
+        shard_self[2],
+        shard_outs[:, width:],
+        shard_pair[:, :width],
+        shard_pair[:, width:].reshape(rows, 2, width),
+        shard_outs[:, :width],
+        shard_hidden[:, :hidden],
+        shard_hidden[:, hidden:],
+        factors,
+        *clipped,
+    )
+
+
 def solution(mesh):
     in_specs = (
         P("dp", "mp", None),
@@ -443,6 +1409,7 @@
         P("dp", "mp"),
         P("dp", "mp"),
     )
+    by_clip = mesh.shape["mp"] == 2 and mesh.shape["dp"] == 16
     return jax.shard_map(
-        per_device, mesh=mesh, in_specs=in_specs, out_specs=out_specs, check_vma=False
-    )
+        clip_per_device if by_clip else per_device, mesh=mesh, in_specs=in_specs, out_specs=out_specs, check_vma=False
+    )

time: 2520 us -> 1230 us (0.49)
  waiting for transfers between devices: 1260 us -> 260 us
  Pallas kernels: 0 us -> 615 us
  matrix products: 694 us -> 126 us
  other arithmetic: 269 us -> 105 us
  local copies, waits for them, and re-layouts: 182 us -> 78.4 us
  blocking collectives: 68.2 us -> 0 us
    pallas_call x0 -> x22, Pallas kernels: none -> 615 us  [the longest x13 449 us: hosted(): pl.pallas_call(kernel, grid=grid, in_specs=list(in_specs) + [hbm] * len(a...]
    dot_general x58 -> x10, matrix products: 688 us -> 126 us  [dotf(): return lax.dot_general(a, b, dims, preferred_element_type=f32)]
    reduce_scatter x13 -> x1, waiting for transfers between devices: 519 us -> 0.01 us  [clip_per_device(): lax.psum_scatter(hidden_grad.reshape(2 * D, 2 * hidden), ('mp', 'dp'), sc...]
    all_gather x14 -> x3, waiting for transfers between devices: 688 us -> 187 us  [gathered(): whole = lax.all_gather(shard, ('mp', 'dp'), axis=0, tiled=True)]
    convert_element_type x18 -> x14, other arithmetic: 136 us -> 33.4 us  [rounded(): return values.astype(jnp.bfloat16)]
    ppermute x0 -> x11, waiting for transfers between devices: none -> 72.4 us  [swap(): return lax.ppermute(values, axis_name, pairs)]
    reduce_max x7 -> x0, other arithmetic: 52.5 us -> none  [the longest x4 52.4 us: per_block(): jnp.max(highest[:, :, 0], axis=1)]
    unnamed x33 -> x4, waiting for transfers between devices: 48.7 us -> 0.07 us
  transfers between devices with their start and end apart: 30 -> 15, of which waited for: 21 -> 6; matrix products, arithmetic and copies ran while one was open for 39% -> 20% of each run, Pallas kernels for 0% -> 49%
where the time goes in v1:
time: 1230 us; the launch traced here: 1210 us
  Pallas kernels  615 us (50%)
  waiting for transfers between devices  260 us (21%)
  matrix products  126 us (10%)
  other arithmetic  105 us (9%)
  local copies, waits for them, and re-layouts  78.4 us (6%)
  between operations  15.7 us (1%)
    pallas_call x13, Pallas kernels, hosted(): pl.pallas_call(kernel, grid=grid, in_specs=list(in_specs) + [hbm] * len(a...  449 us
    all_gather x3, waiting for transfers between devices, gathered(): whole = lax.all_gather(shard, ('mp', 'dp'), axis=0, tiled=True)  187 us
    dot_general x10, matrix products, dotf(): return lax.dot_general(a, b, dims, preferred_element_type=f32)  126 us
    ppermute x11, waiting for transfers between devices, swap(): return lax.ppermute(values, axis_name, pairs)  72.4 us
    pallas_call x2, Pallas kernels, weight_grad_whole(): pl.pallas_call(weight_grad_whole_kernel, grid=(2, tiles), in_specs=[pl.Bl...  53.3 us
    pallas_call x4, Pallas kernels, project_both(): pl.pallas_call(project_kernel, grid=(2, width // tile), in_specs=[pl.Bloc...  41.5 us
    pallas_call x1, Pallas kernels, self_attend(): pl.pallas_call(functools.partial(self_forward_kernel, 512), grid=(2, pair...  39.9 us
    convert_element_type x14, other arithmetic, rounded(): return values.astype(jnp.bfloat16)  33.4 us
  transfers between devices with their start and end apart: 15, of which 6 were waited for; matrix products, arithmetic and copies ran while one was open for 20% of the time, Pallas kernels for 49%

profile of v1, /device:TPU:0, one launch (start us, length us, event | category | flops | bytes accessed | tf_op | source)
XLA Modules:
  0.0 1212.5 jit_solution(15498367940856902045)
XLA Ops:
  17.4 3.2 fusion.25
  20.6 2.9 collective-permute-start
  23.7 2.4 dynamic-slice_bitcast_fusion.3
  26.1 52.7 %collective-permute-done.2 = bf16[32,1536]{1,0:T(8,128)(2,1)S(1)} collective-permute-done((bf16[32,1536]{1,0:T(8,128)(2,1)S(1)}, bf16[32,1536]{1,0:T(8,128)(2,1)S(1)}, u32[]{:S(2)}, u32[]{:S(2)}) %collective-permute-start.2) | collective-permute-done | bytes 98336 | tf_op jit(solution)/shard_map/ppermute | solution.py:1147
  81.7 2.7 copy-done.22
  85.2 76.5 %all-gather.4.cloned.1.call-done = bf16[3072,3200]{1,0:T(8,128)(2,1)} async-done(((bf16[96,3200]{1,0:T(8,128)(2,1)}), bf16[3072,3200]{1,0:T(8,128)(2,1)}) %all-gather.4.cloned.1.call-update) | async-done | bytes 19660816 | tf_op jit(solution)/shard_map/all_gather | solution.py:1205
  162.7 2.3 slice_reduce_fusion.1
  165.1 3.5 add_convert_fusion.4.x_ref.refs_0_
  168.6 17.9 %shard_map.243.q_ref.k_ref.v_ref.refs_0_.refs_1_.refs_2_ = bf16[2,1024,2304]{2,1,0:T(8,128)(2,1)S(1)} custom-call(bf16[1024,1536]{1,0:T(8,128)(2,1)S(1)} %add_convert_fusion.4.x_ref.refs_0_, bf16[2,1536,3200]{2,1,0:T(8,128)(2,1)} %bitcast.265), custom_call_target="tpu_custom_call" | custom-call | flops 14495514624 | bytes 23592960 | tf_op jit(solution)/shard_map/pallas_call | solution.py:907
  188.2 39.9 %shard_map.244 = (bf16[2,1024,768]{2,1,0:T(8,128)(2,1)S(1)}, f32[2,6,8,1024]{3,2,1,0:T(8,128)S(1)}, f32[2,6,8,128]{3,2,1,0:T(8,128)S(1)}) custom-call(bf16[2,1024,2304]{2,1,0:T(8,128)(2,1)S(1)} %shard_map.243.q_ref.k_ref.v_ref.refs_0_.refs_1_.refs_2_, bf16[2,1024,2304]{2,1,0:T(8,128)(2,1)S(1)} %shard_map.243.q_ref.k_ref.v_ref.refs_0_.refs_1_.refs_2_, ...), custom_call_target="tpu_custom_call" | custom-call | flops 12884901888 | bytes 12582912 | tf_op jit(solution)/shard_map/pallas_call | solution.py:479
  230.7 3.2 fusion.26
  235.3 11.8 shard_map.245.refs_4_
  247.1 3.1 reduce_sum.161
  250.3 3.7 multiply_reduce_fusion.7
  257.8 18.7 %collective-permute-done.1 = bf16[512,1536]{1,0:T(8,128)(2,1)} collective-permute-done((bf16[512,1536]{1,0:T(8,128)(2,1)}, bf16[512,1536]{1,0:T(8,128)(2,1)}, u32[]{:S(2)}, u32[]{:S(2)}) %collective-permute-start.1) | collective-permute-done | bytes 1572896 | tf_op jit(solution)/shard_map/ppermute | solution.py:1147
  276.5 2.3 convert_element_type.396
  280.4 2.3 fusion.19.x_ref
  282.7 102.7 %all-gather.6.cloned.1.call-done = bf16[3072,6144]{1,0:T(8,128)(2,1)} async-done(((bf16[96,6144]{1,0:T(8,128)(2,1)}), bf16[3072,6144]{1,0:T(8,128)(2,1)}) %all-gather.6.cloned.1.call-update) | async-done | bytes 37748752 | tf_op jit(solution)/shard_map/all_gather | solution.py:1205
  385.4 3.3 fusion.23
  388.7 3.3 fusion.24
  392.0 7.1 shard_map.246.q_ref
  399.1 11.7 shard_map.247
  412.9 12.3 %shard_map.248.refs_4_ = f32[1024,1536]{1,0:T(8,128)} custom-call(bf16[2,1024,768]{2,1,0:T(8,128)(2,1)} %copy-done.3, bf16[2,1024,768]{2,1,0:T(8,128)(2,1)} %copy-done.3, bf16[2,1536,6144]{2,1,0:T(8,128)(2,1)} %bitcast.253, bf16[2,1536,6144]{2,1,0:T(8,128)(2,1)} %bitcast.254, f32[1024,1536]{1,0:T(8,128)} %shard_map.245.refs_4_), custom_call_target="tpu_custom_call" | custom-call | flops 4831838208 | bytes 9663676 | tf_op jit(solution)/shard_map/pallas_call | solution.py:740
  425.2 3.2 reduce_sum.163
  428.4 3.7 multiply_reduce_fusion.6
  437.3 16.1 %multiply_convert_fusion = (bf16[1024,3072]{1,0:T(8,128)(2,1)}, f32[1024,3072]{1,0:T(8,128)}) fusion(bf16[1024,1536]{1,0:T(8,128)(2,1)S(1)} %add_convert_fusion.2.x_ref, bf16[2,1536,6144]{2,1,0:T(8,128)(2,1)} %bitcast.255), kind=kOutput, calls=%fused_computation.2 | convolution fusion | flops 9679405056 | bytes 31457280 | tf_op jit(solution)/shard_map/dot_general | solution.py:428
  453.5 17.1 %multiply_convert_fusion.1 = (bf16[1024,3072]{1,0:T(8,128)(2,1)S(1)}, f32[1024,3072]{1,0:T(8,128)}) fusion(bf16[1024,1536]{1,0:T(8,128)(2,1)S(1)} %add_convert_fusion.2.x_ref, bf16[2,1536,6144]{2,1,0:T(8,128)(2,1)} %bitcast.256), kind=kOutput, calls=%fused_computation.4 | convolution fusion | flops 9679405056 | bytes 31457280 | tf_op jit(solution)/shard_map/dot_general | solution.py:428
  472.1 26.6 %shard_map.249.refs_0_ = bf16[2,1536,6144]{2,1,0:T(8,128)(2,1)} custom-call(bf16[1024,1536]{1,0:T(8,128)(2,1)S(1)} %copy-done.10, bf16[1024,3072]{1,0:T(8,128)(2,1)S(1)} %get-tuple-element.108.y0_ref.refs_0_, bf16[1024,3072]{1,0:T(8,128)(2,1)} %get-tuple-element.109.y1_ref.refs_1_), custom_call_target="tpu_custom_call" | custom-call | flops 19327352832 | bytes 34603008 | tf_op jit(solution)/shard_map/pallas_call | solution.py:1124
  503.5 8.3 all-gather.8.cloned.1.call-done
  511.8 21.7 %add_convert_fusion.y1_ref = bf16[1024,3072]{1,0:T(8,128)(2,1)} fusion(f32[1024,3072]{1,0:T(8,128)} %get-tuple-element.237, bf16[1024,1536]{1,0:T(8,128)(2,1)} %fusion.19.x_ref, bf16[2,1536,3072]{2,1,0:T(8,128)(2,1)} %bitcast.285), kind=kOutput, calls=%fused_computation | convolution fusion | flops 9704570880 | bytes 31457280 | tf_op jit(solution)/shard_map/dot_general | solution.py:428
  533.5 16.4 %add_convert_fusion.1.y0_ref = bf16[1024,3072]{1,0:T(8,128)(2,1)S(1)} fusion(f32[1024,3072]{1,0:T(8,128)} %get-tuple-element.235, bf16[1024,1536]{1,0:T(8,128)(2,1)S(1)} %copy-done.11, bf16[2,1536,3072]{2,1,0:T(8,128)(2,1)} %bitcast.286), kind=kOutput, calls=%fused_computation.1 | convolution fusion | flops 9704570880 | bytes 31457280 | tf_op jit(solution)/shard_map/dot_general | solution.py:428
  549.9 26.7 %shard_map.250 = bf16[2,1536,6144]{2,1,0:T(8,128)(2,1)} custom-call(bf16[1024,1536]{1,0:T(8,128)(2,1)S(1)} %add_convert_fusion.2.x_ref, bf16[1024,3072]{1,0:T(8,128)(2,1)S(1)} %add_convert_fusion.1.y0_ref, bf16[1024,3072]{1,0:T(8,128)(2,1)} %add_convert_fusion.y1_ref, bf16[2,1536,6144]{2,1,0:T(8,128)(2,1)} %shard_map.249.refs_0_), custom_call_target="tpu_custom_call", output_to_operand_aliasing={{}: (3, {})} | custom-call | flops 19327352832 | bytes 34603008 | tf_op jit(solution)/shard_map/pallas_call | solution.py:1124
  576.7 15.5 %fusion.6 = f32[1024,1536]{1,0:T(8,128)} fusion(bf16[1024,3072]{1,0:T(8,128)(2,1)} %copy-done.9, bf16[2,1536,6144]{2,1,0:T(8,128)(2,1)} %bitcast.257), kind=kOutput, calls=%fused_computation.14 | convolution fusion | flops 9663676416 | bytes 22020096 | tf_op jit(solution)/shard_map/dot_general | solution.py:428
  592.2 24.8 %multiply_reduce_fusion = (f32[1536]{0:T(1024)}, f32[1024]{0:T(1024)S(1)}, f32[1024]{0:T(1024)S(1)}, f32[1536]{0:T(1024)}, f32[1024,1536]{1,0:T(8,128)}) fusion(f32[1024,1536]{1,0:T(8,128)} %shard_map.248.refs_4_, f32[1024]{0:T(1024)S(1)} %copy-done.58, f32[1024]{0:T(1024)S(1)} %copy-done.56, f32[1536]{0:T(1024)S(1)} %copy-done.50, ...), kind=kOutput, calls=%fused_computation.22 | convolution fusion | flops 9679398912 | bytes 34637824 | tf_op jit(solution)/shard_map/dot_general | solution.py:428
  617.0 13.4 %fusion.45 = (bf16[1024,1536]{1,0:T(8,128)(2,1)S(1)}, f32[1024,1536]{1,0:T(8,128)}) fusion(f32[1024]{0:T(1024)S(1)} %get-tuple-element.239, f32[1024,1536]{1,0:T(8,128)} %shard_map.248.refs_4_, f32[1024]{0:T(1024)S(1)} %copy-done.56, f32[1024]{0:T(1024)S(1)} %get-tuple-element.240, f32[1024,1536]{1,0:T(8,128)} %get-tuple-element.238, ...), kind=kLoop, calls=%fused_computation.172 | loop fusion | flops 18874368 | bytes 28334080 | tf_op jit(solution)/shard_map/convert_element_type | solution.py:30
  630.4 8.4 shard_map.251.g_ref
  638.9 20.1 %shard_map.252 = (bf16[2,1024,768]{2,1,0:T(8,128)(2,1)S(1)}, bf16[2,64,768]{2,1,0:T(8,128)(2,1)S(1)}, bf16[2,64,768]{2,1,0:T(8,128)(2,1)S(1)}) custom-call(bf16[2,1024,768]{2,1,0:T(8,128)(2,1)S(1)} %copy-done.13, bf16[2,64,1536]{2,1,0:T(8,128)(2,1)S(1)} %copy-done.16, bf16[2,64,1536]{2,1,0:T(8,128)(2,1)S(1)} %copy-done.16, ...), custom_call_target="tpu_custom_call" | custom-call | flops 6442450944 | bytes 9437184 | tf_op jit(solution)/shard_map/pallas_call | solution.py:1084
  662.0 18.9 %shard_map.256 = (bf16[2,4,2,96,2304]{4,3,2,1,0:T(8,128)(2,1)}, bf16[2,4,2,96,2304]{4,3,2,1,0:T(8,128)(2,1)}) custom-call(bf16[1024,1536]{1,0:T(8,128)(2,1)} %copy-done.7, bf16[64,1536]{1,0:T(8,128)(2,1)} %copy-done.39, bf16[2,1024,768]{2,1,0:T(8,128)(2,1)} %copy-done.4, bf16[2,1024,768]{2,1,0:T(8,128)(2,1)} %copy-done.4, bf16[2,64,768]{2,1,0:T(8,128)(2,1)} %copy-done.19, ...), custom_call_target="tpu_custom_call" | custom-call | flops 14495514624 | bytes 28991028 | tf_op jit(solution)/shard_map/pallas_call | solution.py:740
  680.9 3.0 slice.299
  683.9 2.9 slice.300
  686.8 10.5 shard_map.253
  697.4 5.5 multiply_reduce_fusion.1
  702.9 5.7 fusion.44
  708.6 8.1 shard_map.254.refs_3_
  718.4 65.0 %shard_map.257 = (bf16[2,1024,384]{2,1,0:T(8,128)(2,1)}, bf16[2,1024,384]{2,1,0:T(8,128)(2,1)}, bf16[2,1024,384]{2,1,0:T(8,128)(2,1)}, bf16[4,2,48,2304]{3,2,1,0:T(8,128)(2,1)}, bf16[2,4,48,2304]{3,2,1,0:T(8,128)(2,1)}) custom-call(bf16[2,1024,2304]{2,1,0:T(8,128)(2,1)} %copy-done, bf16[2,1024,2304]{2,1,0:T(8,128)(2,1)} %copy-done, ...), custom_call_target="tpu_custom_call" | custom-call | flops 6442450944 | bytes 12884901 | tf_op jit(solution)/shard_map/pallas_call | solution.py:740
  785.9 4.0 fusion.15
  789.9 4.1 fusion.20
  796.3 18.9 %shard_map.255 = (bf16[2,4,2,96,1536]{4,3,2,1,0:T(8,128)(2,1)}, bf16[2,4,2,96,1536]{4,3,2,1,0:T(8,128)(2,1)}) custom-call(bf16[1024,1536]{1,0:T(8,128)(2,1)} %copy-done.8, bf16[1024,1536]{1,0:T(8,128)(2,1)} %copy-done.5, bf16[2,1024,768]{2,1,0:T(8,128)(2,1)} %copy-done.3, bf16[2,1024,768]{2,1,0:T(8,128)(2,1)} %copy-done.3, bf16[2,1024,768]{2,1,0:T(8,128)(2,1)} %copy-done.2, ...), custom_call_target="tpu_custom_call" | custom-call | flops 9663676416 | bytes 19327352 | tf_op jit(solution)/shard_map/pallas_call | solution.py:740
  815.2 51.0 %shard_map.258 = (f32[1024,1536]{1,0:T(8,128)}, bf16[4,2,48,1536]{3,2,1,0:T(8,128)(2,1)}, bf16[2,4,48,1536]{3,2,1,0:T(8,128)(2,1)}) custom-call(bf16[1024,3072]{1,0:T(8,128)(2,1)} %copy-done.21, bf16[1024,3072]{1,0:T(8,128)(2,1)} %get-tuple-element.109.y1_ref.refs_1_, bf16[2,1536,3072]{2,1,0:T(8,128)(2,1)} %bitcast.287, bf16[2,1536,3072]{2,1,0:T(8,128)(2,1)} %bitcast.288, ...), custom_call_target="tpu_custom_call" | custom-call | flops 19327352832 | bytes 38654704 | tf_op jit(solution)/shard_map/pallas_call | solution.py:740
  866.2 3.3 dynamic-slice_convert_fusion.1
  869.4 53.7 %shard_map.259 = (bf16[2,4,2,96,1152]{4,3,2,1,0:T(8,128)(2,1)}, bf16[2,4,2,96,1152]{4,3,2,1,0:T(8,128)(2,1)}, bf16[4,48,2304]{2,1,0:T(8,128)(2,1)}, bf16[4,48,2304]{2,1,0:T(8,128)(2,1)}) custom-call(bf16[1024,1536]{1,0:T(8,128)(2,1)} %copy-done.6, bf16[2,1024,384]{2,1,0:T(8,128)(2,1)} %get-tuple-element.113.refs_1_.refs_4_.refs_0_.refs_6_, ...), custom_call_target="tpu_custom_call" | custom-call | flops 7247757312 | bytes 14495514 | tf_op jit(solution)/shard_map/pallas_call | solution.py:740
  923.1 57.8 %shard_map.260 = (bf16[2,1024,384]{2,1,0:T(8,128)(2,1)}, bf16[2,1024,384]{2,1,0:T(8,128)(2,1)}, bf16[2,1024,384]{2,1,0:T(8,128)(2,1)}, bf16[4,48,1536]{2,1,0:T(8...) custom-call(bf16[2,1024,2304]{2,1,0:T(8,128)(2,1)} %copy-done, ...), custom_call_target="tpu_custom_call" | custom-call | flops 6442450944 | bytes 12884901 | tf_op jit(solution)/shard_map/pallas_call | solution.py:740
  990.7 2.4 slice.288
  993.1 2.4 slice.289
  995.4 2.3 reshape.262
  1007.3 3.0 maximum_select_fusion.2
  1010.3 26.5 %shard_map.261 = (bf16[2,4,2,96,1152]{4,3,2,1,0:T(8,128)(2,1)}, bf16[2,4,2,96,1152]{4,3,2,1,0:T(8,128)(2,1)}, bf16[4,2,48,1152]{3,2,1,0:T(8,128)(2,1)}, bf16[2,4,48,1152]{3,2,1,0:T(8,128)(2,1)}) custom-call(bf16[1024,1536]{1,0:T(8,128)(2,1)} %copy-done.6, bf16[2,1024,384]{2,1,0:T(8,128)(2,1)} %get-tuple-element.124.refs_1_.refs_4_.refs_3_.refs_9_, ...), custom_call_target="tpu_custom_call" | custom-call | flops 7247757312 | bytes 14495514 | tf_op jit(solution)/shard_map/pallas_call | solution.py:740
  1044.9 49.8 %shard_map.262 = (f32[1024,1536]{1,0:T(8,128)}, bf16[4,2,48,1152]{3,2,1,0:T(8,128)(2,1)}, bf16[2,4,48,1152]{3,2,1,0:T(8,128)(2,1)}, bf16[4,48,1152]{2,1,0:T(8,12...) custom-call(bf16[2,1024,384]{2,1,0:T(8,128)(2,1)} %get-tuple-element.113.refs_1_.r, ...), custom_call_target="tpu_custom_call" | custom-call | flops 14495514624 | bytes 28991028 | tf_op jit(solution)/shard_map/pallas_call | solution.py:740
  1094.8 5.0 multiply_reduce_fusion.2
  1100.0 7.6 multiply_add_fusion
  1110.4 56.4 %shard_map.263 = (f32[8,1536]{1,0:T(8,128)}, bf16[4,48,1152]{2,1,0:T(8,128)(2,1)}, bf16[4,48,1152]{2,1,0:T(8,128)(2,1)}, bf16[3,48,1152]{2,1,0:T(8,128)(2,1)}, bf16[3,48,1152]{2,1,0:T(8,128)(2,1)}) custom-call(f32[8,1536]{1,0:T(8,128)} %pad.10.refs_0_, bf16[2,4,2,96,1152]{4,3,2,1,0:T(8,128)(2,1)} %get-tuple-element.129.refs_14_.refs_1_.refs_0_, ...), custom_call_target="tpu_custom_call" | custom-call | flops 1000000000 | bytes 2000000 | tf_op jit(solution)/shard_map/pallas_call | solution.py:740
  1166.8 16.1 %shard_map.264 = (bf16[3,48,1152]{2,1,0:T(8,128)(2,1)}, bf16[3,48,1152]{2,1,0:T(8,128)(2,1)}) custom-call(bf16[2,4,2,96,1152]{4,3,2,1,0:T(8,128)(2,1)} %get-tuple-element.129.refs_14_.refs_1_.refs_0_, bf16[2,4,2,96,1152]{4,3,2,1,0:T(8,128)(2,1)} %get-tuple-element.130.refs_15_.refs_2_.refs_1_, bf16[4,2,48,1152]{3,2,1,0:T(8,128)(2,1)} %get-tuple-element.140.refs_4_.refs_2_, ...), custom_call_target="tpu_custom_call" | custom-call | flops 1000000000 | bytes 2000000 | tf_op jit(solution)/shard_map/pallas_call | solution.py:740
  1199.6 3.0 maximum_select_fusion.3
  1202.6 2.9 fusion.47
  (276 shorter events, 95.8 us)
Async XLA Ops:
  7.2 7.9 copy-start.32
  7.2 8.0 copy-start.34
  7.2 8.0 copy-start.38
  7.2 9.2 copy-start.33
  7.2 154.4 %all-gather.4.cloned.1.call-start = ((), (), s32[]{:S(2)}) async-start(), calls=%async_computation.1 | async-start | bytes 20275200 | tf_op jit(solution)/shard_map/all_gather | solution.py:1205
  13.7 371.7 %all-gather.6.cloned.1.call-start = ((), (), s32[]{:S(2)}) async-start(), calls=%async_computation.2 | async-start | bytes 38928384 | tf_op jit(solution)/shard_map/all_gather | solution.py:1205
  15.1 8.5 copy-start.48
  16.4 495.4 %all-gather.8.cloned.1.call-start = ((), (), s32[]{:S(2)}) async-start(), calls=%async_computation.3 | async-start | bytes 19464192 | tf_op jit(solution)/shard_map/all_gather | solution.py:1205
  17.4 1185.2 %reduce-scatter.2.cloned.1.call-start = ((), (), s32[]{:S(2)}) async-start(), calls=%async_computation.4 | async-start | bytes 38928384 | tf_op jit(solution)/shard_map/reduce_scatter | solution.py:1277
  20.6 58.2 %collective-permute-start = (bf16[512,1536]{1,0:T(8,128)(2,1)}, bf16[512,1536]{1,0:T(8,128)(2,1)}, u32[]{:S(2)}, u32[]{:S(2)}) collective-permute-start(bf16[512,1536]{1,0:T(8,128)(2,1)} %fusion.25), channel_id=1, source_target_pairs={{0,1},{1,0},{2,3},{3,2},{4,5},{5,4},{6,7},{7,6},{8,9},{9,8},{10,11... | collective-permute-start | bytes 4718600 | tf_op jit(solution)/shard_map/ppermute | solution.py:1147
  23.6 55.2 %collective-permute-start.2 = (bf16[32,1536]{1,0:T(8,128)(2,1)S(1)}, bf16[32,1536]{1,0:T(8,128)(2,1)S(1)}, u32[]{:S(2)}, u32[]{:S(2)}) collective-permute-start(bf16[32,1536]{1,0:T(8,128)(2,1)S(1)} %get-tuple-element.225), channel_id=1, source_target_pairs={{0,1},{1,0},{2,3},{3,2},{4,5},{5,4},{6,7},{7,6},{8,9},{9,8},{10,11... | collective-permute-start | bytes 294920 | tf_op jit(solution)/shard_map/ppermute | solution.py:1147
  78.8 309.9 %copy-start.39 = (bf16[64,1536]{1,0:T(8,128)(2,1)}, bf16[64,1536]{1,0:T(8,128)(2,1)S(1)}, u32[]{:S(2)}) copy-start(bf16[64,1536]{1,0:T(8,128)(2,1)S(1)} %maximum_select_fusion.5.refs_1_) | copy-start | bytes 589828
  81.7 86.8 %copy-start.44 = (f32[1024]{0:T(1024)}, f32[1024]{0:T(1024)S(1)}, u32[]{:S(2)}) copy-start(f32[1024]{0:T(1024)S(1)} %broadcast_multiply_fusion.10) | copy-start | bytes 12292
  85.2 83.4 %copy-start.51 = (f32[1024]{0:T(1024)}, f32[1024]{0:T(1024)S(1)}, u32[]{:S(2)}) copy-start(f32[1024]{0:T(1024)S(1)} %add_rsqrt_fusion.2) | copy-start | bytes 12292
  165.0 91.1 %copy-start.42 = (f32[1536]{0:T(1024)}, f32[1536]{0:T(1024)S(1)}, u32[]{:S(2)}) copy-start(f32[1536]{0:T(1024)S(1)} %get-tuple-element.205) | copy-start | bytes 18436
  165.1 268.5 %copy-start.49 = (f32[1536]{0:T(1024)}, f32[1536]{0:T(1024)S(1)}, u32[]{:S(2)}) copy-start(f32[1536]{0:T(1024)S(1)} %get-tuple-element.202) | copy-start | bytes 18436
  188.2 39.9 %copy-start = (bf16[2,1024,2304]{2,1,0:T(8,128)(2,1)}, bf16[2,1024,2304]{2,1,0:T(8,128)(2,1)S(1)}, u32[]{:S(2)}) copy-start(bf16[2,1024,2304]{2,1,0:T(8,128)(2,1)S(1)} %shard_map.243.q_ref.k_ref.v_ref.refs_0_.refs_1_.refs_2_) | copy-start | bytes 28311556
  233.9 42.5 %collective-permute-start.1 = (bf16[512,1536]{1,0:T(8,128)(2,1)}, bf16[512,1536]{1,0:T(8,128)(2,1)}, u32[]{:S(2)}, u32[]{:S(2)}) collective-permute-start(bf16[512,1536]{1,0:T(8,128)(2,1)} %fusion.26), channel_id=1, source_target_pairs={{0,1},{1,0},{2,3},{3,2},{4,5},{5,4},{6,7},{7,6},{8,9},{9,8},{10,11... | collective-permute-start | bytes 4718600 | tf_op jit(solution)/shard_map/ppermute | solution.py:1147
  256.1 22.6 %copy-start.25 = (f32[512,1536]{1,0:T(8,128)}, f32[512,1536]{1,0:T(8,128)S(1)}, u32[]{:S(2)}) copy-start(f32[512,1536]{1,0:T(8,128)S(1)} %dynamic-slice_bitcast_fusion.2) | copy-start | bytes 9437188
  257.8 134.2 %copy-start.7 = (bf16[1024,1536]{1,0:T(8,128)(2,1)}, bf16[1024,1536]{1,0:T(8,128)(2,1)S(1)}, u32[]{:S(2)}) copy-start(bf16[1024,1536]{1,0:T(8,128)(2,1)S(1)} %add_convert_fusion.3.x_ref.refs_0_) | copy-start | bytes 9437188
  392.0 7.1 copy-start.15
  399.1 11.7 copy-start.12
  412.6 19.5 %collective-permute-start.3 = (f32[2,2,12]{2,1,0:T(2,128)S(1)}, f32[2,2,12]{2,1,0:T(2,128)S(1)}, u32[]{:S(2)}, u32[]{:S(2)}) collective-permute-start(f32[2,2,12]{2,1,0:T(2,128)S(1)} %constant_dynamic-update-slice_fusion), channel_id=1, source_target_pairs={{0,2},{2,0},{4,6},{6,4},{8,10},{10,8},{12,14},{14,12},{16,18},{18,... | collective-permute-start | bytes 584 | tf_op jit(solution)/shard_map/ppermute | solution.py:1147
  428.4 6.4 copy-start.55
  432.2 21.2 %copy-start.57 = (f32[1024]{0:T(1024)}, f32[1024]{0:T(1024)S(1)}, u32[]{:S(2)}) copy-start(f32[1024]{0:T(1024)S(1)} %add_rsqrt_fusion) | copy-start | bytes 12292
  432.2 3.7 collective-permute-start.4
  435.9 17.5 %collective-permute-start.5 = (f32[2,2,12]{2,1,0:T(2,128)S(1)}, f32[2,2,12]{2,1,0:T(2,128)S(1)}, u32[]{:S(2)}, u32[]{:S(2)}) collective-permute-start(f32[2,2,12]{2,1,0:T(2,128)S(1)} %max.20), channel_id=1, source_target_pairs={{0,4},{2,6},{4,0},{6,2},{8,12},{10,14},{12,8},{14,10},{16,20},{18,... | collective-permute-start | bytes 584 | tf_op jit(solution)/shard_map/ppermute | solution.py:1147
  453.4 18.7 %copy-start.10 = (bf16[1024,1536]{1,0:T(8,128)(2,1)S(1)}, bf16[1024,1536]{1,0:T(8,128)(2,1)}, u32[]{:S(2)}) copy-start(bf16[1024,1536]{1,0:T(8,128)(2,1)} %fusion.19.x_ref) | copy-start | bytes 9437188
  453.4 17.2 %collective-permute-start.6 = (f32[2,2,12]{2,1,0:T(2,128)S(1)}, f32[2,2,12]{2,1,0:T(2,128)S(1)}, u32[]{:S(2)}, u32[]{:S(2)}) collective-permute-start(f32[2,2,12]{2,1,0:T(2,128)S(1)} %max.21), channel_id=1, source_target_pairs={{0,8},{2,10},{4,12},{6,14},{8,0},{10,2},{12,4},{14,6},{16,24},{18,... | collective-permute-start | bytes 584 | tf_op jit(solution)/shard_map/ppermute | solution.py:1147
  470.6 28.1 %copy-start.21 = (bf16[1024,3072]{1,0:T(8,128)(2,1)}, bf16[1024,3072]{1,0:T(8,128)(2,1)S(1)}, u32[]{:S(2)}) copy-start(bf16[1024,3072]{1,0:T(8,128)(2,1)S(1)} %get-tuple-element.108.y0_ref.refs_0_) | copy-start | bytes 18874372
  470.7 28.1 %collective-permute-start.7 = (f32[2,2,12]{2,1,0:T(2,128)S(1)}, f32[2,2,12]{2,1,0:T(2,128)S(1)}, u32[]{:S(2)}, u32[]{:S(2)}) collective-permute-start(f32[2,2,12]{2,1,0:T(2,128)S(1)} %max.22), channel_id=1, source_target_pairs={{0,16},{2,18},{4,20},{6,22},{8,24},{10,26},{12,28},{14,30},{16,0},... | collective-permute-start | bytes 584 | tf_op jit(solution)/shard_map/ppermute | solution.py:1147
  472.1 29.6 %slice-start.6 = ((f32[96,2,768]{2,1,0:T(2,128)}), f32[96,1,768]{2,1,0:T(1,128)S(1)}, s32[]{:S(2)}) async-start(f32[96,2,768]{2,1,0:T(2,128)} %param.20), calls=%async_computation.11 | async-start | bytes 589824 | tf_op jit(solution)/shard_map/slice | solution.py:1271
  511.8 21.7 %copy-start.11 = (bf16[1024,1536]{1,0:T(8,128)(2,1)S(1)}, bf16[1024,1536]{1,0:T(8,128)(2,1)}, u32[]{:S(2)}) copy-start(bf16[1024,1536]{1,0:T(8,128)(2,1)} %fusion.19.x_ref) | copy-start | bytes 9437188
  549.9 26.7 %copy-start.9 = (bf16[1024,3072]{1,0:T(8,128)(2,1)}, bf16[1024,3072]{1,0:T(8,128)(2,1)S(1)}, u32[]{:S(2)}) copy-start(bf16[1024,3072]{1,0:T(8,128)(2,1)S(1)} %add_convert_fusion.1.y0_ref) | copy-start | bytes 18874372
  576.6 15.6 %copy-start.50 = (f32[1536]{0:T(1024)S(1)}, f32[1536]{0:T(1024)}, u32[]{:S(2)}) copy-start(f32[1536]{0:T(1024)} %copy-done.49) | copy-start | bytes 18436
  576.7 15.6 %copy-start.56 = (f32[1024]{0:T(1024)S(1)}, f32[1024]{0:T(1024)}, u32[]{:S(2)}) copy-start(f32[1024]{0:T(1024)} %copy-done.55) | copy-start | bytes 12292
  576.7 15.5 %copy-start.58 = (f32[1024]{0:T(1024)S(1)}, f32[1024]{0:T(1024)}, u32[]{:S(2)}) copy-start(f32[1024]{0:T(1024)} %copy-done.57) | copy-start | bytes 12292
  592.2 24.8 %copy-start.26 = (f32[512,1536]{1,0:T(8,128)S(1)}, f32[512,1536]{1,0:T(8,128)}, u32[]{:S(2)}) copy-start(f32[512,1536]{1,0:T(8,128)} %copy-done.25) | copy-start | bytes 9437188
  630.4 8.4 copy-start.8
  630.4 8.5 copy-start.13
  630.4 8.5 copy-start.16
  680.9 16.4 %slice-start.2 = ((s8[6291456]{0:T(1024)(128)(4,1)}), s8[4194304]{0:T(1024)(128)(4,1)S(1)}, s32[]{:S(2)}) async-start(s8[6291456]{0:T(1024)(128)(4,1)} %bitcast.273), calls=%async_computation.7 | async-start | bytes 8388608
  686.8 10.5 slice-start.3
  686.8 10.5 copy-start.43
  686.8 10.5 copy-start.47
  686.8 10.5 copy-start.54
  708.6 8.1 copy-start.5
  718.4 67.5 %copy-start.20 = (bf16[2,64,768]{2,1,0:T(8,128)(2,1)S(1)}, bf16[2,64,768]{2,1,0:T(8,128)(2,1)}, u32[]{:S(2)}) copy-start(bf16[2,64,768]{2,1,0:T(8,128)(2,1)} %copy-done.19) | copy-start | bytes 589828
  718.4 67.5 %copy-start.18 = (bf16[2,64,768]{2,1,0:T(8,128)(2,1)S(1)}, bf16[2,64,768]{2,1,0:T(8,128)(2,1)}, u32[]{:S(2)}) copy-start(bf16[2,64,768]{2,1,0:T(8,128)(2,1)} %copy-done.17) | copy-start | bytes 589828
  794.1 210.6 %collective-permute-start.9 = (bf16[32,1536]{1,0:T(8,128)(2,1)S(1)}, bf16[32,1536]{1,0:T(8,128)(2,1)S(1)}, u32[]{:S(2)}, u32[]{:S(2)}) collective-permute-start(bf16[32,1536]{1,0:T(8,128)(2,1)S(1)} %dynamic-slice_convert_fusion.4), channel_id=1, source_target_pairs={{0,1},{1,0},{2,3},{3,2},{4,5},{5,4},{6,7},{7,6},{8,9},{9,8},{10,11... | collective-permute-start | bytes 294920 | tf_op jit(solution)/shard_map/ppermute | solution.py:1147
  869.4 136.0 %collective-permute-start.8 = (bf16[512,1536]{1,0:T(8,128)(2,1)}, bf16[512,1536]{1,0:T(8,128)(2,1)}, u32[]{:S(2)}, u32[]{:S(2)}) collective-permute-start(bf16[512,1536]{1,0:T(8,128)(2,1)} %dynamic-slice_convert_fusion.1), channel_id=1, source_target_pairs={{0,1},{1,0},{2,3},{3,2},{4,5},{5,4},{6,7},{7,6},{8,9},{9,8},{10,11... | collective-permute-start | bytes 4718600 | tf_op jit(solution)/shard_map/ppermute | solution.py:1147
  982.4 6.7 copy-start.28
  983.9 6.0 copy-start.29
  1036.8 57.9 %slice-start.4 = ((s8[6291456]{0:T(1024)(128)(4,1)}), s8[4194304]{0:T(1024)(128)(4,1)S(1)}, s32[]{:S(2)}) async-start(s8[6291456]{0:T(1024)(128)(4,1)} %bitcast.275), calls=%async_computation.9 | async-start | bytes 8388608
  1044.9 49.8 %slice-start.5 = ((s8[6291456]{0:T(1024)(128)(4,1)}), s8[2097152]{0:T(1024)(128)(4,1)S(1)}, s32[]{:S(2)}) async-start(s8[6291456]{0:T(1024)(128)(4,1)} %bitcast.275), calls=%async_computation.10 | async-start | bytes 4194304
  1044.9 49.9 %copy-start.41 = (f32[1536]{0:T(1024)S(1)}, f32[1536]{0:T(1024)}, u32[]{:S(2)}) copy-start(f32[1536]{0:T(1024)} %copy-done.40) | copy-start | bytes 18436
  1044.9 49.9 %copy-start.45 = (f32[1024]{0:T(1024)S(1)}, f32[1024]{0:T(1024)}, u32[]{:S(2)}) copy-start(f32[1024]{0:T(1024)} %copy-done.44) | copy-start | bytes 12292
  1044.9 49.9 %copy-start.52 = (f32[1024]{0:T(1024)S(1)}, f32[1024]{0:T(1024)}, u32[]{:S(2)}) copy-start(f32[1024]{0:T(1024)} %copy-done.51) | copy-start | bytes 12292
  1099.9 8.3 copy-start.30
  1100.0 9.1 copy-start.31
  1110.0 87.7 %collective-permute-start.10 = (bf16[512,1536]{1,0:T(8,128)(2,1)S(1)}, bf16[512,1536]{1,0:T(8,128)(2,1)}, u32[]{:S(2)}, u32[]{:S(2)}) collective-permute-start(bf16[512,1536]{1,0:T(8,128)(2,1)S(1)} %dynamic-slice_convert_fusion), channel_id=1, source_target_pairs={{0,1},{1,0},{2,3},{3,2},{4,5},{5,4},{6,7},{7,6},{8,9},{9,8},{10,11... | collective-permute-start | bytes 4718600 | tf_op jit(solution)/shard_map/ppermute | solution.py:1147
  1166.8 17.4 %copy-start.37 = (bf16[3,48,1152]{2,1,0:T(8,128)(2,1)S(1)}, bf16[3,48,1152]{2,1,0:T(8,128)(2,1)}, u32[]{:S(2)}) copy-start(bf16[3,48,1152]{2,1,0:T(8,128)(2,1)} %get-tuple-element.145) | copy-start | bytes 995332
  1182.9 7.1 copy-start.36
  1182.9 11.6 copy-start.35
  (20 other events, 61.0 us)
Sparse Core Ops, SparseCore 0:
  13.9 147.7 all-gather.3
  165.1 220.2 all-gather.5
  388.9 122.8 all-gather.7
  576.8 407.1 reduce-scatter.1

commit v2 on v1

--- a/solution.py
+++ b/solution.py
@@ -1,4 +1,5 @@
 import functools
+import math
 
 import jax
 import jax.numpy as jnp
@@ -656,6 +657,121 @@
             self.send(t).wait()
 
 
+class Swap:
+    kind, names = "x0", ["sent"]
+
+    def __init__(self, holder):
+        self.group = holder
+
+    def shape(self):
+        sent = self.group.arrays["sent"]
+        return jax.ShapeDtypeStruct(sent.shape, sent.dtype)
+
+    def scratch(self):
+        return [pltpu.SemaphoreType.DMA((1,)), pltpu.SemaphoreType.DMA((1,))]
+
+    def bind(self, sources, target, scratch):
+        self.source, self.target = sources[0], target
+        self.send_sem, self.recv_sem = scratch
+
+    def partners(self):
+        return [(lax.axis_index("dp"), 1 - lax.axis_index("mp"))]
+
+    def copy(self):
+        return pltpu.make_async_remote_copy(
+            src_ref=self.source,
+            dst_ref=self.target,
+            send_sem=self.send_sem.at[0],
+            recv_sem=self.recv_sem.at[0],
+            device_id=self.partners()[0],
+            device_id_type=MESH,
+        )
+
+    def each(self, steps):
+        return 1
+
+    def begin(self):
+        pass
+
+    def work(self, step, steps, j):
+        @pl.when(step == 0)
+        def _():
+            self.copy().start()
+
+    def finish(self):
+        self.copy().wait()
+
+
+class Total:
+    kind = "total"
+    names = ["own", "there", "x1", "y2", "y1", "x2", "za", "zb"]
+
+    def __init__(self, group):
+        self.group = group
+        low = group.rows // 2
+        self.low, self.high = pl.ds(0, low), pl.ds(low, group.rows - low)
+
+    def shape(self):
+        return jax.ShapeDtypeStruct((self.group.rows, self.group.width), f32)
+
+    def scratch(self):
+        half, width = self.group.rows // 2, self.group.width
+        return [
+            pltpu.VMEM((2, 7, half, width), bf16),
+            pltpu.VMEM((2 * half, width), f32),
+            pltpu.SemaphoreType.DMA((2, 7)),
+            pltpu.SemaphoreType.DMA(()),
+        ]
+
+    def bind(self, sources, target, scratch):
+        self.sources, self.target = dict(zip(self.names, sources)), target
+        self.terms, self.sum, self.load_sem, self.store_sem = scratch
+
+    def partners(self):
+        return []
+
+    def loads(self):
+        z = lax.axis_index("dp") // (Y * CORES)
+        a = self.sources
+        low = [a["own"].at[0, z, 0, self.low], a["there"].at[0, z, 0, self.low], a["x1"].at[z, 0]]
+        low += [a["y2"].at[z]] + [a["za"].at[k] for k in range(3)]
+        high = [a["own"].at[0, z, 0, self.high], a["there"].at[0, z, 0, self.high]]
+        high += [a["y1"].at[0, z], a["x2"].at[z]] + [a["zb"].at[k] for k in range(3)]
+        return [
+            pltpu.make_async_copy(source, self.terms.at[p, i], self.load_sem.at[p, i])
+            for p, part in enumerate((low, high))
+            for i, source in enumerate(part)
+        ]
+
+    def each(self, steps):
+        return 0
+
+    def begin(self):
+        for copy in self.loads():
+            copy.start()
+
+    def finish(self):
+        for copy in self.loads():
+            copy.wait()
+        half = self.group.rows // 2
+        for p in range(2):
+            total = self.terms[p, 0].astype(f32)
+            for i in range(1, 7):
+                total = total + self.terms[p, i].astype(f32)
+            self.sum[p * half : (p + 1) * half, :] = total
+        copy = pltpu.make_async_copy(self.sum, self.target, self.store_sem)
+        copy.start()
+        copy.wait()
+
+
+class Holder:
+    def __init__(self, sent):
+        self.arrays = {"sent": sent}
+
+    def got(self):
+        return self.arrays["x0"]
+
+
 class Group:
     def __init__(self, own, there):
         self.arrays = {"own": own, "there": there}
@@ -687,7 +803,8 @@
 
 
 def hosted(body, number, grid, args, in_specs, out_shape, out_specs, scratch, plan, flops, core=False):
-    hops = [Hop(kind, group) for kind, group in plan]
+    special = {"x0": Swap, "total": Total}
+    hops = [special[k](group) if k in special else Hop(k, group) for k, group in plan]
     arrays, places = [], {}
     for hop in hops:
         for name in hop.names:
@@ -698,7 +815,7 @@
     steps = 1
     for n in grid:
         steps *= n
-    kinds = set(hop.kind[0] for hop in hops)
+    kinds = set(hop.kind[0] for hop in hops if hop.kind != "total")
 
     def kernel(*refs):
         counts = [len(args), len(arrays), len(out_shape), len(hops), len(scratch)]
@@ -708,8 +825,9 @@
             at += n
         for k, hop in enumerate(hops):
             sources = [parts[1][places[(id(hop.group), name)]] for name in hop.names]
-            hop.bind(sources, parts[3][k], refs[at : at + 5])
-            at += 5
+            taken = len(hop.scratch())
+            hop.bind(sources, parts[3][k], refs[at : at + taken])
+            at += taken
         step = 0
         for axis, n in enumerate(grid):
             step = step * n + pl.program_id(axis)
@@ -732,7 +850,7 @@
 
         @pl.when(step == steps - 1)
         def _():
-            for hop in hops:
+            for hop in sorted(hops, key=lambda hop: hop.kind != "total"):
                 hop.finish()
 
     hbm = pl.BlockSpec(memory_space=pl.ANY)
@@ -893,6 +1011,140 @@
         core=True,
     )
     return Group(*outs)
+
+
+def gather_kernel(parts, swaps, *refs):
+    shard_ref, sent_refs = refs[0], refs[1 : 1 + swaps]
+    whole_ref, got_refs = refs[1 + swaps], refs[2 + swaps : 2 + 2 * swaps]
+    own_sem, swap_send, swap_recv, send_sem, recv_sem = refs[2 + 2 * swaps :]
+    dp, x = lax.axis_index("dp"), lax.axis_index("mp")
+    group = Y * CORES
+    z, rest = dp // group, dp % group
+    across = rest + CORES - 2 * CORES * (rest // CORES)
+    rows, columns = shard_ref.shape
+    x_peer, y_peer, core_peer = (dp, 1 - x), (z * group + across, x), core_partner()
+    z_peers = [(((z + k) % Z) * group + rest, x) for k in range(1, Z)]
+    cut = 5 * rows // 6
+    low, high, every = pl.ds(0, cut), pl.ds(cut, rows - cut), slice(None)
+    meet([x_peer, y_peer, core_peer] + z_peers)
+    started = []
+
+    def send(part, slot, source, at, peer):
+        copy = pltpu.make_async_remote_copy(
+            src_ref=source,
+            dst_ref=whole_ref.at[at],
+            send_sem=send_sem.at[part, slot],
+            recv_sem=recv_sem.at[part, slot],
+            device_id=peer,
+            device_id_type=MESH,
+        )
+        copy.start()
+        started.append(copy)
+        return copy
+
+    def pass_on(part, slot, at, peer):
+        return send(part, slot, whole_ref.at[at], at, peer)
+
+    def columns_of(part):
+        begin, end = parts[part]
+        return pl.ds(begin, end - begin)
+
+    swapped = []
+    for i in range(swaps):
+        copy = pltpu.make_async_remote_copy(
+            src_ref=sent_refs[i],
+            dst_ref=got_refs[i],
+            send_sem=swap_send.at[i],
+            recv_sem=swap_recv.at[i],
+            device_id=x_peer,
+            device_id_type=MESH,
+        )
+        copy.start()
+        swapped.append(copy)
+    own = pltpu.make_async_copy(shard_ref, whole_ref.at[x, z, rest], own_sem)
+    own.start()
+    along, over, turned, late = {}, {}, {}, []
+    for part in range(len(parts)):
+        cut = columns_of(part)
+        at = (x, z, rest, every, cut)
+        along[part] = [
+            send(part, k, shard_ref.at[every, cut], at, peer) for k, peer in enumerate(z_peers)
+        ]
+        late.append(send(part, 3, shard_ref.at[every, cut], at, core_peer))
+    own.wait()
+
+    def first(part):
+        cut = columns_of(part)
+        for copy in along[part]:
+            copy.wait_recv()
+        over[part] = [
+            pass_on(part, 4, (x, every, rest, low, cut), x_peer),
+            pass_on(part, 5, (x, every, rest, high, cut), y_peer),
+        ]
+        for k in range(1, Z):
+            late.append(pass_on(part, 5 + k, (x, (z + k) % Z, rest, every, cut), core_peer))
+
+    def second(part):
+        cut = columns_of(part)
+        for copy in over[part]:
+            copy.wait_recv()
+        turned[part] = [
+            pass_on(part, 9, (0, every, rest, low, cut), y_peer),
+            pass_on(part, 10, (x, every, rest, high, cut), x_peer),
+            pass_on(part, 11, (1, every, rest, low, cut), y_peer),
+            pass_on(part, 12, (x, every, across, high, cut), x_peer),
+        ]
+        late.append(pass_on(part, 13, (1 - x, every, rest, low, cut), core_peer))
+        late.append(pass_on(part, 14, (x, every, across, high, cut), core_peer))
+
+    def third(part):
+        cut = columns_of(part)
+        for copy in turned[part]:
+            copy.wait_recv()
+        late.append(pass_on(part, 15, (0, every, across, low, cut), core_peer))
+        late.append(pass_on(part, 16, (1, every, across, low, cut), core_peer))
+        late.append(pass_on(part, 17, (1 - x, every, rest, high, cut), core_peer))
+        late.append(pass_on(part, 18, (1 - x, every, across, high, cut), core_peer))
+
+    first(0)
+    for part in range(len(parts)):
+        second(part)
+        if part + 1 < len(parts):
+            first(part + 1)
+        if part:
+            third(part - 1)
+    third(len(parts) - 1)
+    for copy in late:
+        copy.wait_recv()
+    for copy in started:
+        copy.wait_send()
+    for copy in swapped:
+        copy.wait()
+
+
+def gather_now(number, shard, swaps):
+    rows, columns = shard.shape
+    tiles = columns // LANES
+    cuts = [0, tiles // 3 * LANES, 2 * tiles // 3 * LANES, columns]
+    parts = list(zip(cuts[:-1], cuts[1:]))
+    hbm = pl.BlockSpec(memory_space=pl.ANY)
+    outs = pl.pallas_call(
+        functools.partial(gather_kernel, parts, len(swaps)),
+        in_specs=[hbm] * (1 + len(swaps)),
+        out_specs=(hbm,) * (1 + len(swaps)),
+        out_shape=(jax.ShapeDtypeStruct((2, Z, Y * CORES, rows, columns), shard.dtype),)
+        + tuple(jax.ShapeDtypeStruct(a.shape, a.dtype) for a in swaps),
+        scratch_shapes=[
+            pltpu.SemaphoreType.DMA(()),
+            pltpu.SemaphoreType.DMA((len(swaps),)),
+            pltpu.SemaphoreType.DMA((len(swaps),)),
+            pltpu.SemaphoreType.DMA((len(parts), 19)),
+            pltpu.SemaphoreType.DMA((len(parts), 19)),
+        ],
+        compiler_params=pltpu.CompilerParams(collective_id=number, has_side_effects=True),
+        cost_estimate=pl.CostEstimate(flops=10**9, bytes_accessed=10**8, transcendentals=0),
+    )(shard, *swaps)
+    return outs[0], outs[1:]
 
 
 def project_kernel(x_ref, w_ref, o_ref):
@@ -1200,31 +1452,43 @@
     rows, width = self_value.shape
     both = range(2)
 
-    def gathered(pieces):
-        shard = jnp.concatenate([rounded(p).reshape(rows, -1) for p in pieces], axis=1)
+    def shard_of(pieces):
+        return jnp.concatenate([rounded(p).reshape(rows, -1) for p in pieces], axis=1)
+
+    def gathered(shard):
         whole = lax.all_gather(shard, ("mp", "dp"), axis=0, tiled=True)
         return whole.reshape(2, D, shard.shape[1])
 
-    def to_clip(array, kind):
-        own = lax.dynamic_index_in_dim(array, mp, 0, keepdims=False)
-        sent = rounded(lax.dynamic_index_in_dim(array, 1 - mp, 0, keepdims=False))
-        own, got = own.astype(kind), swap(sent, "mp", MP_PAIRS).astype(kind)
+    def other_half(array):
+        return rounded(lax.dynamic_index_in_dim(array, 1 - mp, 0, keepdims=False))
+
+    def whole_clip(array, got, kind):
+        own = lax.dynamic_index_in_dim(array, mp, 0, keepdims=False).astype(kind)
+        got = got.astype(kind)
         return jnp.where(
             mp == 0, jnp.concatenate([own, got], axis=0), jnp.concatenate([got, own], axis=0)
         )
 
-    def to_frames(array):
+    def other_frames(array):
+        count = array.shape[0] // 2
+        return rounded(lax.dynamic_slice_in_dim(array, (1 - mp) * count, count, 0))
+
+    def own_frames(array, got):
         count = array.shape[0] // 2
         own = lax.dynamic_slice_in_dim(array, mp * count, count, 0)
-        sent = rounded(lax.dynamic_slice_in_dim(array, (1 - mp) * count, count, 0))
-        got = swap(sent, "mp", MP_PAIRS).astype(f32)
+        got = got.astype(f32)
         return jnp.where(mp == 0, jnp.stack([own, got]), jnp.stack([got, own]))
 
     norms_padded = jnp.pad(norm_params, ((0, 0), (0, LANES - norm_params.shape[1])))
     hidden = hidden_in.shape[1]
-    self_all = gathered([self_query_key, self_value, self_output, norms_padded])
-    cross_all = gathered([cross_query, cross_key_value, cross_output, hidden_in])
-    out_all = gathered([hidden_out])
+    self_shard = shard_of([self_query_key, self_value, self_output, norms_padded])
+    cross_shard = shard_of([cross_query, cross_key_value, cross_output, hidden_in])
+    sent = (other_half(inputs), other_half(text_states))
+    self_shard, cross_shard, sent = lax.optimization_barrier((self_shard, cross_shard, sent))
+    cross_all = gathered(cross_shard)
+    self_all, (got_inputs, got_text) = gather_now(16, self_shard, sent)
+    self_all = self_all.reshape(2, D, self_shard.shape[1])
+    out_all = gathered(rounded(hidden_out))
     norms = self_all[0, :, 4 * width : 4 * width + norm_params.shape[1]].astype(f32).T
     self_o = [self_all[m, :, 3 * width : 4 * width] for m in both]
     cross_q = [cross_all[m, :, :width] for m in both]
@@ -1238,12 +1502,12 @@
     def times_turned(arrays, matrices):
         return dotf(arrays[0], matrices[0], NT) + dotf(arrays[1], matrices[1], NT)
 
-    stream = to_clip(inputs, f32)
-    states = to_clip(text_states, bf16)
+    stream = whole_clip(inputs, got_inputs, f32)
+    states = whole_clip(text_states, got_text, bf16)
     normed_self = rounded(norm_rows_of(stream)[0] * norms[0] + norms[1])
     qkv = project_both(normed_self, self_all, 0, 3 * width)
     qkv, cotangent = lax.optimization_barrier((qkv, cotangent))
-    upstream = to_clip(cotangent, f32)
+    upstream = whole_clip(cotangent, swap(other_half(cotangent), "mp", MP_PAIRS), f32)
     mixed_self, lse, self_peaks = self_attend(qkv, width)
     after_self = unproject_both(0, [], halves_of(mixed_self), self_all, 3 * width, width, stream)
     normed_cross = rounded(norm_rows_of(after_self)[0] * norms[2] + norms[3])
@@ -1277,9 +1541,10 @@
     shard_hidden = lax.psum_scatter(
         hidden_grad.reshape(2 * D, 2 * hidden), ("mp", "dp"), scatter_dimension=0, tiled=True
     ).astype(f32)
-    back, gain_three, bias_three = norm_back(
-        after_cross, norms[4], times_turned(grad_up, in_w)
-    )
+    grad_normed = unproject_both(
+        0, [], [(a, m, 0) for m, a in enumerate(grad_up)], cross_all, 4 * width, hidden
+    )
+    back, gain_three, bias_three = norm_back(after_cross, norms[4], grad_normed)
     grad_stream = upstream + back
 
     branch_cross = rounded(grad_stream)
@@ -1288,7 +1553,8 @@
     grad_normed = unproject_both(0, [], halves_of(dq), cross_all, 0, width)
     back, gain_two, bias_two = norm_back(after_self, norms[2], grad_normed)
     dkv = [joined([dk[m], dv[m]]) for m in both]
-    grad_text = to_frames(times_turned(dkv, cross_kv))
+    grad_text = times_turned(dkv, cross_kv)
+    swap_text = Holder(other_frames(grad_text))
     grad_stream = grad_stream + back
     branch_self = rounded(grad_stream)
     group_pair = exchanged_grad(1, [], [normed_cross, states], [(0, [dq]), (1, [dk]), (1, [dv])], rows)
@@ -1296,7 +1562,8 @@
         2, [], [branch_cross, branch_self], [(0, [mixed_cross]), (1, [mixed_self])], rows
     )
     grad_mixed = project_both(branch_self, self_all, 3 * width, width)
-    cut = width // 2 // LANES
+    pairs = width // LANES
+    cut = 2 * pairs // 3
     early = self_attend_back(
         3, [("x1", group_pair), ("y1", group_pair)], qkv, grad_mixed, lse, width, 0, cut
     )
@@ -1304,21 +1571,26 @@
     output = unproject_both(
         4, [("x1", group_out), ("y1", group_out)], [(a, m, 0) for m, a in enumerate(activated)], out_all, 0, hidden, after_cross
     )
-    output = to_frames(output)
+    swap_output = Holder(other_frames(output))
     group_early = exchanged_grad(
-        5, [("x2", group_pair), ("y2", group_pair)], [normed_self], [(0, list(early))], rows
+        5, [("x0", swap_text), ("x2", group_pair), ("y2", group_pair)], [normed_self], [(0, list(early))], rows
     )
     late = self_attend_back(
         6,
-        [("x2", group_out), ("y2", group_out), ("za", group_pair), ("zb", group_pair)],
+        [
+            ("x2", group_out),
+            ("y2", group_out),
+            ("za", group_pair),
+            ("zb", group_pair),
+            ("x0", swap_output),
+        ],
         qkv,
         grad_mixed,
         lse,
         width,
         cut,
-        2 * cut,
-    )
-    late, output, grad_text = lax.optimization_barrier((late, output, grad_text))
+        pairs,
+    )
     group_late = exchanged_grad(
         7, [("x1", group_early), ("y1", group_early)], [normed_self], [(0, list(late))], rows
     )
@@ -1343,18 +1615,32 @@
     )
     back, gain_one, bias_one = norm_back(stream, norms[0], grad_normed)
     norm_grads = jnp.stack([gain_one, bias_one, gain_two, bias_two, gain_three, bias_three])
-    grad_inputs, norm_grads = lax.optimization_barrier((grad_stream + back, norm_grads))
-    grad_inputs = to_frames(grad_inputs)
+    grad_inputs = grad_stream + back
+    sent = other_frames(grad_inputs)
+    swaps_inputs = [Holder(sent[: sent.shape[0] // 2]), Holder(sent[sent.shape[0] // 2 :])]
     norm_grads = relay(
         9,
-        [("x2", group_late), ("y2", group_late), ("za", group_early), ("zb", group_early)],
+        [
+            ("x2", group_late),
+            ("y2", group_late),
+            ("za", group_early),
+            ("zb", group_early),
+            ("x0", swaps_inputs[0]),
+            ("total", group_pair),
+            ("total", group_out),
+        ],
         jnp.pad(norm_grads, ((0, 2), (0, 0))),
     )[:6]
-    last_hop(10, [("za", group_late), ("zb", group_late)])
-    shard_pair, shard_outs = group_pair.result(z), group_out.result(z)
-    halves = [group_early.result(z), group_late.result(z)]
-    half = width // 2
-    shard_self = [joined([h[:, i * half : (i + 1) * half] for h in halves]) for i in range(3)]
+    last_hop(10, [("za", group_late), ("zb", group_late), ("x0", swaps_inputs[1]), ("total", group_early)])
+    grad_inputs = own_frames(grad_inputs, jnp.concatenate([h.got() for h in swaps_inputs]))
+    grad_text = own_frames(grad_text, swap_text.got())
+    output = own_frames(output, swap_output.got())
+    shard_pair, shard_outs = group_pair.arrays["total"], group_out.arrays["total"]
+    halves = [group_early.arrays["total"], group_late.result(z)]
+    sizes = [cut * LANES, width - cut * LANES]
+    shard_self = [
+        joined([h[:, i * n : (i + 1) * n] for h, n in zip(halves, sizes)]) for i in range(3)
+    ]
 
     shard_norms = lax.dynamic_slice_in_dim(norm_grads, dp * rows, rows, 1).T
 

time: 1230 us -> 1070 us (0.87); the launches traced: 1210 us -> 1070 us
  waiting for transfers between devices: 260 us -> 0.45 us
  Pallas kernels: 615 us -> 807 us
  matrix products: 126 us -> 81.6 us
  local copies, waits for them, and re-layouts: 78.4 us -> 58.3 us
    pallas_call x0 -> x1, Pallas kernels: none -> 201 us  [gather_now(): pl.pallas_call(functools.partial(gather_kernel, parts, len(swaps)), in_sp...]
    all_gather x3 -> x2, waiting for transfers between devices: 187 us -> 0.01 us  [gathered(): whole = lax.all_gather(shard, ('mp', 'dp'), axis=0, tiled=True)]
    ppermute x11 -> x6, waiting for transfers between devices: 72.4 us -> 0.4 us  [swap(): return lax.ppermute(values, axis_name, pairs)]
    dot_general x10 -> x8, matrix products: 126 us -> 81.6 us  [dotf(): return lax.dot_general(a, b, dims, preferred_element_type=f32)]
    pallas_call x13 -> x14, Pallas kernels: 449 us -> 437 us  [hosted(): pl.pallas_call(kernel, grid=grid, in_specs=list(in_specs) + [hbm] * len(a...]
  transfers between devices with their start and end apart: 15 -> 9, of which waited for: 6 -> 1; matrix products, arithmetic and copies ran while one was open for 20% -> 16% of each run, Pallas kernels for 49% -> 73%
where the time goes in v2:
time: 1070 us
  Pallas kernels  807 us (75%)
  other arithmetic  98.2 us (9%)
  matrix products  81.6 us (8%)
  local copies, waits for them, and re-layouts  58.3 us (5%)
  between operations  15.8 us (1%)
    pallas_call x14, Pallas kernels, hosted(): pl.pallas_call(kernel, grid=grid, in_specs=list(in_specs) + [hbm] * len(a...  437 us
    pallas_call x1, Pallas kernels, gather_now(): pl.pallas_call(functools.partial(gather_kernel, parts, len(swaps)), in_sp...  201 us
    dot_general x8, matrix products, dotf(): return lax.dot_general(a, b, dims, preferred_element_type=f32)  81.6 us
    pallas_call x2, Pallas kernels, weight_grad_whole(): pl.pallas_call(weight_grad_whole_kernel, grid=(2, tiles), in_specs=[pl.Bl...  54 us
    pallas_call x4, Pallas kernels, project_both(): pl.pallas_call(project_kernel, grid=(2, width // tile), in_specs=[pl.Bloc...  42.6 us
    pallas_call x1, Pallas kernels, self_attend(): pl.pallas_call(functools.partial(self_forward_kernel, 512), grid=(2, pair...  39.8 us
    convert_element_type x14, other arithmetic, rounded(): return values.astype(jnp.bfloat16)  34.3 us
  transfers between devices with their start and end apart: 9, of which 1 were waited for; matrix products, arithmetic and copies ran while one was open for 16% of the time, Pallas kernels for 73%

profile of v2, /device:TPU:0, one launch (start us, length us, event | category | flops | bytes accessed | tf_op | source)
XLA Modules:
  0.0 1067.2 jit_solution(17808377776323305548)
XLA Ops:
  15.5 3.2 fusion.22.refs_1_
  22.4 201.1 %shard_map.243 = (bf16[2,4,4,96,3200]{4,3,2,1,0:T(8,128)(2,1)}, bf16[512,1536]{1,0:T(8,128)(2,1)}, bf16[32,1536]{1,0:T(8,128)(2,1)}) custom-call(bf16[96,3200]{1,0:T(8,128)(2,1)} %fusion.25.refs_0_, bf16[512,1536]{1,0:T(8,128)(2,1)} %fusion.22.refs_1_, bf16[32,1536]{1,0:T(8,128)(2,1)} %get-tuple-element.96.refs_2_), custom_call_target="tpu_custom_call" | custom-call | flops 1000000000 | bytes 100000000 | tf_op jit(solution)/shard_map/pallas_call | solution.py:1131
  223.4 1.9 convert_element_type.202
  226.5 2.3 slice_reduce_fusion.1
  231.3 1.9 copy-done.23
  234.5 19.1 %shard_map.244.q_ref.k_ref.v_ref.refs_0_.refs_1_.refs_2_ = bf16[2,1024,2304]{2,1,0:T(8,128)(2,1)S(1)} custom-call(bf16[1024,1536]{1,0:T(8,128)(2,1)S(1)} %add_convert_fusion.4.x_ref.refs_0_, bf16[2,1536,3200]{2,1,0:T(8,128)(2,1)} %bitcast.160), custom_call_target="tpu_custom_call" | custom-call | flops 14495514624 | bytes 23592960 | tf_op jit(solution)/shard_map/pallas_call | solution.py:1159
  253.7 5.6 fusion.23
  259.3 39.8 %shard_map.245 = (bf16[2,1024,768]{2,1,0:T(8,128)(2,1)S(1)}, f32[2,6,8,1024]{3,2,1,0:T(8,128)S(1)}, f32[2,6,8,128]{3,2,1,0:T(8,128)S(1)}) custom-call(bf16[2,1024,2304]{2,1,0:T(8,128)(2,1)S(1)} %shard_map.244.q_ref.k_ref.v_ref.refs_0_.refs_1_.refs_2_, bf16[2,1024,2304]{2,1,0:T(8,128)(2,1)S(1)} %shard_map.244.q_ref.k_ref.v_ref.refs_0_.refs_1_.refs_2_, ...), custom_call_target="tpu_custom_call" | custom-call | flops 12884901888 | bytes 12582912 | tf_op jit(solution)/shard_map/pallas_call | solution.py:480
  301.7 11.8 %shard_map.246.refs_4_ = f32[1024,1536]{1,0:T(8,128)} custom-call(bf16[2,1024,768]{2,1,0:T(8,128)(2,1)} %copy-done.3, bf16[2,1024,768]{2,1,0:T(8,128)(2,1)} %copy-done.3, bf16[2,1536,3200]{2,1,0:T(8,128)(2,1)} %bitcast.161, bf16[2,1536,3200]{2,1,0:T(8,128)(2,1)} %bitcast.162, f32[1024,1536]{1,0:T(8,128)} %copy-done.23), custom_call_target="tpu_custom_call" | custom-call | flops 4831838208 | bytes 9663676 | tf_op jit(solution)/shard_map/pallas_call | solution.py:858
  313.5 3.2 reduce_sum.161
  316.7 4.1 multiply_reduce_fusion.7
  320.9 2.2 dynamic-slice_bitcast_fusion.2
  324.5 2.9 convert_element_type.215
  327.5 1.7 copy-done.27
  329.1 2.3 fusion.16.x_ref
  331.5 3.3 fusion.20
  334.7 3.3 fusion.21
  338.1 7.1 shard_map.247.q_ref
  345.2 11.7 %shard_map.248 = (bf16[2,1024,768]{2,1,0:T(8,128)(2,1)S(1)}, f32[2,6,8,128]{3,2,1,0:T(8,128)S(1)}) custom-call(bf16[2,1024,768]{2,1,0:T(8,128)(2,1)S(1)} %shard_map.247.q_ref, bf16[2,64,1536]{2,1,0:T(8,128)(2,1)S(1)} %pad_maximum_fusion.2.k_ref.v_ref, bf16[2,64,1536]{2,1,0:T(8,128)(2,1)S(1)} %pad_maximum_fusion.2.k_ref.v_ref), custom_call_target="tpu_custom_call" | custom-call | flops 3221225472 | bytes 6291456 | tf_op jit(solution)/shard_map/pallas_call | solution.py:1300
  359.7 11.8 %shard_map.249.refs_4_ = f32[1024,1536]{1,0:T(8,128)} custom-call(bf16[2,1024,768]{2,1,0:T(8,128)(2,1)} %copy-done.4, bf16[2,1024,768]{2,1,0:T(8,128)(2,1)} %copy-done.4, bf16[2,1536,6144]{2,1,0:T(8,128)(2,1)} %bitcast.148, bf16[2,1536,6144]{2,1,0:T(8,128)(2,1)} %bitcast.149, f32[1024,1536]{1,0:T(8,128)} %shard_map.246.refs_4_), custom_call_target="tpu_custom_call" | custom-call | flops 4831838208 | bytes 9663676 | tf_op jit(solution)/shard_map/pallas_call | solution.py:858
  371.6 3.1 reduce_sum.163
  374.7 5.5 multiply_reduce_fusion.6
  380.3 1.9 collective-permute-start.2
  384.0 2.5 collective-permute-start.3
  386.5 16.0 %multiply_convert_fusion = (bf16[1024,3072]{1,0:T(8,128)(2,1)}, f32[1024,3072]{1,0:T(8,128)}) fusion(bf16[1024,1536]{1,0:T(8,128)(2,1)S(1)} %add_convert_fusion.2.x_ref, bf16[2,1536,6144]{2,1,0:T(8,128)(2,1)} %bitcast.150), kind=kOutput, calls=%fused_computation.2 | convolution fusion | flops 9679405056 | bytes 31457280 | tf_op jit(solution)/shard_map/dot_general | solution.py:429
  403.2 15.1 %multiply_convert_fusion.1 = (bf16[1024,3072]{1,0:T(8,128)(2,1)S(1)}, f32[1024,3072]{1,0:T(8,128)}) fusion(bf16[1024,1536]{1,0:T(8,128)(2,1)S(1)} %add_convert_fusion.2.x_ref, bf16[2,1536,6144]{2,1,0:T(8,128)(2,1)} %bitcast.151), kind=kOutput, calls=%fused_computation.4 | convolution fusion | flops 9679405056 | bytes 31457280 | tf_op jit(solution)/shard_map/dot_general | solution.py:429
  418.3 27.0 %shard_map.250.refs_0_ = bf16[2,1536,6144]{2,1,0:T(8,128)(2,1)} custom-call(bf16[1024,1536]{1,0:T(8,128)(2,1)S(1)} %copy-done.10, bf16[1024,3072]{1,0:T(8,128)(2,1)S(1)} %get-tuple-element.120.y0_ref.refs_0_, bf16[1024,3072]{1,0:T(8,128)(2,1)} %get-tuple-element.121.y1_ref.refs_1_), custom_call_target="tpu_custom_call" | custom-call | flops 19327352832 | bytes 34603008 | tf_op jit(solution)/shard_map/pallas_call | solution.py:1376
  446.2 2.1 broadcast_multiply_fusion
  448.3 1.8 fusion.26
  450.1 19.7 %add_convert_fusion.y1_ref.refs_1_ = bf16[1024,3072]{1,0:T(8,128)(2,1)} fusion(f32[1024,3072]{1,0:T(8,128)} %get-tuple-element.269, bf16[1024,1536]{1,0:T(8,128)(2,1)} %fusion.16.x_ref, bf16[2,1536,3072]{2,1,0:T(8,128)(2,1)} %bitcast.186), kind=kOutput, calls=%fused_computation | convolution fusion | flops 9704570880 | bytes 31457280 | tf_op jit(solution)/shard_map/dot_general | solution.py:429
  469.8 16.2 %add_convert_fusion.1.y0_ref.refs_0_ = bf16[1024,3072]{1,0:T(8,128)(2,1)S(1)} fusion(f32[1024,3072]{1,0:T(8,128)} %get-tuple-element.267, bf16[1024,1536]{1,0:T(8,128)(2,1)S(1)} %copy-done.11, bf16[2,1536,3072]{2,1,0:T(8,128)(2,1)} %bitcast.187), kind=kOutput, calls=%fused_computation.1 | convolution fusion | flops 9704570880 | bytes 31457280 | tf_op jit(solution)/shard_map/dot_general | solution.py:429
  486.0 27.1 %shard_map.251 = bf16[2,1536,6144]{2,1,0:T(8,128)(2,1)} custom-call(bf16[1024,1536]{1,0:T(8,128)(2,1)S(1)} %add_convert_fusion.2.x_ref, bf16[1024,3072]{1,0:T(8,128)(2,1)S(1)} %add_convert_fusion.1.y0_ref.refs_0_, bf16[1024,3072]{1,0:T(8,128)(2,1)} %add_convert_fusion.y1_ref.refs_1_, ...), custom_call_target="tpu_custom_call", output_to_operand_aliasing={{}: (3, {})} | custom-call | flops 19327352832 | bytes 34603008 | tf_op jit(solution)/shard_map/pallas_call | solution.py:1376
  513.2 28.3 %shard_map.252 = f32[1024,1536]{1,0:T(8,128)} custom-call(bf16[1024,3072]{1,0:T(8,128)(2,1)} %copy-done.2, bf16[1024,3072]{1,0:T(8,128)(2,1)} %add_convert_fusion.y1_ref.refs_1_, bf16[2,1536,6144]{2,1,0:T(8,128)(2,1)} %bitcast.152, bf16[2,1536,6144]{2,1,0:T(8,128)(2,1)} %bitcast.153), custom_call_target="tpu_custom_call" | custom-call | flops 19327352832 | bytes 38654704 | tf_op jit(solution)/shard_map/pallas_call | solution.py:858
  541.5 5.9 multiply_reduce_fusion
  547.5 13.3 %fusion.42 = (bf16[1024,1536]{1,0:T(8,128)(2,1)S(1)}, f32[1024,1536]{1,0:T(8,128)}) fusion(f32[1024]{0:T(1024)S(1)} %broadcast_multiply_fusion.6, f32[1024,1536]{1,0:T(8,128)S(1)} %bitcast.171, f32[1024]{0:T(1024)S(1)} %copy-done.48, f32[1024]{0:T(1024)S(1)} %broadcast_multiply_fusion.7, f32[1024,1536]{1,0:T(8,128)} %shard_map.252, f32[1536]{0:T(1024)S(1)} %copy-done.42, ...), kind=kLoop, calls=%fused_computation.142 | loop fusion | flops 18874368 | bytes 28334080 | tf_op jit(solution)/shard_map/convert_element_type | solution.py:31
  560.8 8.4 shard_map.253.g_ref
  569.2 20.3 %shard_map.254 = (bf16[2,1024,768]{2,1,0:T(8,128)(2,1)S(1)}, bf16[2,64,768]{2,1,0:T(8,128)(2,1)S(1)}, bf16[2,64,768]{2,1,0:T(8,128)(2,1)S(1)}) custom-call(bf16[2,1024,768]{2,1,0:T(8,128)(2,1)S(1)} %copy-done.13, bf16[2,64,1536]{2,1,0:T(8,128)(2,1)S(1)} %copy-done.16, bf16[2,64,1536]{2,1,0:T(8,128)(2,1)S(1)} %copy-done.16, ...), custom_call_target="tpu_custom_call" | custom-call | flops 6442450944 | bytes 9437184 | tf_op jit(solution)/shard_map/pallas_call | solution.py:1336
  592.5 10.6 shard_map.255
  603.2 5.2 multiply_reduce_fusion.1
  608.5 5.8 fusion.41
  614.4 8.0 shard_map.256.refs_3_
  622.4 1.7 copy-done.1
  624.1 18.7 %shard_map.257 = (bf16[2,4,2,96,2304]{4,3,2,1,0:T(8,128)(2,1)}, bf16[2,4,2,96,2304]{4,3,2,1,0:T(8,128)(2,1)}) custom-call(bf16[1024,1536]{1,0:T(8,128)(2,1)} %copy-done.8, bf16[64,1536]{1,0:T(8,128)(2,1)} %copy-done.36, bf16[2,1024,768]{2,1,0:T(8,128)(2,1)} %copy-done.5, bf16[2,1024,768]{2,1,0:T(8,128)(2,1)} %copy-done.5, bf16[2,64,768]{2,1,0:T(8,128)(2,1)} %copy-done.19, ...), custom_call_target="tpu_custom_call" | custom-call | flops 14495514624 | bytes 28991028 | tf_op jit(solution)/shard_map/pallas_call | solution.py:858
  642.9 62.0 %shard_map.258 = (bf16[2,1024,512]{2,1,0:T(8,128)(2,1)}, bf16[2,1024,512]{2,1,0:T(8,128)(2,1)}, bf16[2,1024,512]{2,1,0:T(8,128)(2,1)}, bf16[4,2,48,2304]{3,2,1,0:T(8,128)(2,1)}, bf16[2,4,48,2304]{3,2,1,0:T(8,128)(2,1)}) custom-call(bf16[2,1024,2304]{2,1,0:T(8,128)(2,1)} %copy-done, bf16[2,1024,2304]{2,1,0:T(8,128)(2,1)} %copy-done, ...), custom_call_target="tpu_custom_call" | custom-call | flops 8589934592 | bytes 17179868 | tf_op jit(solution)/shard_map/pallas_call | solution.py:858
  704.9 4.0 fusion.12
  709.0 4.1 fusion.17
  714.5 19.4 %shard_map.259 = (bf16[2,4,2,96,1536]{4,3,2,1,0:T(8,128)(2,1)}, bf16[2,4,2,96,1536]{4,3,2,1,0:T(8,128)(2,1)}) custom-call(bf16[1024,1536]{1,0:T(8,128)(2,1)} %copy-done.9, bf16[1024,1536]{1,0:T(8,128)(2,1)} %copy-done.6, bf16[2,1024,768]{2,1,0:T(8,128)(2,1)} %copy-done.4, bf16[2,1024,768]{2,1,0:T(8,128)(2,1)} %copy-done.4, bf16[2,1024,768]{2,1,0:T(8,128)(2,1)} %copy-done.3, ...), custom_call_target="tpu_custom_call" | custom-call | flops 9663676416 | bytes 19327352 | tf_op jit(solution)/shard_map/pallas_call | solution.py:858
  733.8 46.4 %shard_map.260 = (f32[1024,1536]{1,0:T(8,128)}, bf16[4,2,48,1536]{3,2,1,0:T(8,128)(2,1)}, bf16[2,4,48,1536]{3,2,1,0:T(8,128)(2,1)}) custom-call(bf16[1024,3072]{1,0:T(8,128)(2,1)} %copy-done.21, bf16[1024,3072]{1,0:T(8,128)(2,1)} %get-tuple-element.121.y1_ref.refs_1_, bf16[2,1536,3072]{2,1,0:T(8,128)(2,1)} %bitcast.188, bf16[2,1536,3072]{2,1,0:T(8,128)(2,1)} %bitcast.189, ...), custom_call_target="tpu_custom_call" | custom-call | flops 19327352832 | bytes 38654704 | tf_op jit(solution)/shard_map/pallas_call | solution.py:858
  780.2 3.4 dynamic-slice_convert_fusion.1.refs_15_
  783.7 32.5 %shard_map.261 = (bf16[2,4,2,96,1536]{4,3,2,1,0:T(8,128)(2,1)}, bf16[2,4,2,96,1536]{4,3,2,1,0:T(8,128)(2,1)}, bf16[32,1536]{1,0:T(8,128)(2,1)}, bf16[4,48,2304]{2,1,0:T(8,128)(2,1)}, bf16[4,48,2304]{2,1,0:T(8,128)(2,1)}) custom-call(bf16[1024,1536]{1,0:T(8,128)(2,1)} %copy-done.7, bf16[2,1024,512]{2,1,0:T(8,128)(2,1)} %get-tuple-element.128.refs_1_.refs_4_.refs_0_.refs_6_, ...), custom_call_target="tpu_custom_call" | custom-call | flops 9663676416 | bytes 19327352 | tf_op jit(solution)/shard_map/pallas_call | solution.py:858
  816.2 60.4 %shard_map.262 = (bf16[2,1024,256]{2,1,0:T(8,128)(2,1)}, bf16[2,1024,256]{2,1,0:T(8,128)(2,1)}, bf16[2,1024,256]{2,1,0:T(8,128)(2,1)}, bf16[4,48,1536]{2,1,0:T(8...) custom-call(bf16[2,1024,2304]{2,1,0:T(8,128)(2,1)} %copy-done, ...), custom_call_target="tpu_custom_call" | custom-call | flops 4294967296 | bytes 8589934 | tf_op jit(solution)/shard_map/pallas_call | solution.py:858
  876.6 34.1 %shard_map.263 = (bf16[2,4,2,96,768]{4,3,2,1,0:T(8,128)(2,1)}, bf16[2,4,2,96,768]{4,3,2,1,0:T(8,128)(2,1)}, bf16[4,2,48,1536]{3,2,1,0:T(8,128)(2,1)}, bf16[2,4,48,1536]{3,2,1,0:T(8,128)(2,1)}) custom-call(bf16[1024,1536]{1,0:T(8,128)(2,1)} %copy-done.7, bf16[2,1024,256]{2,1,0:T(8,128)(2,1)} %get-tuple-element.135.refs_1_.refs_4_.refs_3_.refs_9_, ...), custom_call_target="tpu_custom_call" | custom-call | flops 4831838208 | bytes 9663676 | tf_op jit(solution)/shard_map/pallas_call | solution.py:858
  911.9 1.9 slice.182
  913.8 36.0 %shard_map.264 = (f32[1024,1536]{1,0:T(8,128)}, bf16[4,2,48,768]{3,2,1,0:T(8,128)(2,1)}, bf16[2,4,48,768]{3,2,1,0:T(8,128)(2,1)}, bf16[4,48,1536]{2,1,0:T(8,128)...) custom-call(bf16[2,1024,512]{2,1,0:T(8,128)(2,1)} %get-tuple-element.128.refs_1_.ref, ...), custom_call_target="tpu_custom_call" | custom-call | flops 14495514624 | bytes 28991028 | tf_op jit(solution)/shard_map/pallas_call | solution.py:858
  950.0 4.9 multiply_reduce_fusion.3
  955.8 7.8 multiply_add_fusion
  963.6 2.7 copy-done.28
  967.7 46.0 %shard_map.265 = (f32[8,1536]{1,0:T(8,128)}, bf16[4,48,768]{2,1,0:T(8,128)(2,1)}, bf16[4,48,768]{2,1,0:T(8,128)(2,1)}, bf16[3,48,1536]{2,1,0:T(8,128)(2,1)}, bf1...) custom-call(f32[8,1536]{1,0:T(8,128)} %pad.10.refs_0_, ...), custom_call_target="tpu_custom_call" | custom-call | flops 1000000000 | bytes 2000000 | tf_op jit(solution)/shard_map/pallas_call | solution.py:858
  1014.9 1.7 slice.197
  1016.5 18.8 %shard_map.266 = (bf16[3,48,768]{2,1,0:T(8,128)(2,1)}, bf16[3,48,768]{2,1,0:T(8,128)(2,1)}, bf16[256,1536]{1,0:T(8,128)(2,1)}, f32[96,1536]{1,0:T(8,128)}) custom-call(bf16[2,4,2,96,768]{4,3,2,1,0:T(8,128)(2,1)} %get-tuple-element.140.refs_14_.refs_1_.refs_0_, bf16[2,4,2,96,768]{4,3,2,1,0:T(8,128)(2,1)} %get-tuple-element.141.refs_15_.refs_2_.refs_1_, ...), custom_call_target="tpu_custom_call" | custom-call | flops 1000000000 | bytes 2000000 | tf_op jit(solution)/shard_map/pallas_call | solution.py:858
  1045.4 2.4 fusion.46
  1047.9 2.2 dynamic-slice_bitcast_fusion
  1051.9 5.4 maximum_select_fusion.2
  1057.3 2.9 fusion.45
  (253 shorter events, 47.6 us)
Async XLA Ops:
  7.2 8.1 copy-start.61
  7.2 11.5 %copy-start.49 = (f32[2,32,1536]{2,1,0:T(8,128)S(1)}, f32[2,32,1536]{2,1,0:T(8,128)}, u32[]{:S(2)}) copy-start(f32[2,32,1536]{2,1,0:T(8,128)} %param.13) | copy-start | bytes 1179652
  7.2 324.3 %all-gather.3.cloned.1.call-start = ((), (), s32[]{:S(2)}) async-start(), calls=%async_computation.1 | async-start | bytes 38928384 | tf_op jit(solution)/shard_map/all_gather | solution.py:1459
  8.6 12.8 %copy-start.32 = (f32[96,3072]{1,0:T(8,128)S(1)}, f32[96,3072]{1,0:T(8,128)}, u32[]{:S(2)}) copy-start(f32[96,3072]{1,0:T(8,128)} %param.23) | copy-start | bytes 3538948
  21.3 428.7 %all-gather.5.cloned.1.call-start = ((), (), s32[]{:S(2)}) async-start(), calls=%async_computation.2 | async-start | bytes 19464192 | tf_op jit(solution)/shard_map/all_gather | solution.py:1459
  22.3 1035.0 %reduce-scatter.2.cloned.1.call-start = ((), (), s32[]{:S(2)}) async-start(), calls=%async_computation.3 | async-start | bytes 38928384 | tf_op jit(solution)/shard_map/reduce_scatter | solution.py:1541
  22.3 206.4 %slice-start.6 = ((s8[6291456]{0:T(1024)(128)(4,1)}), s8[2097152]{0:T(1024)(128)(4,1)S(1)}, s32[]{:S(2)}) async-start(s8[6291456]{0:T(1024)(128)(4,1)} %bitcast.173), calls=%async_computation.10 | async-start | bytes 4194304
  223.4 5.4 slice-start.7
  228.8 94.3 %copy-start.39 = (f32[1536]{0:T(1024)}, f32[1536]{0:T(1024)S(1)}, u32[]{:S(2)}) copy-start(f32[1536]{0:T(1024)S(1)} %get-tuple-element.235) | copy-start | bytes 18436
  228.8 153.4 %copy-start.41 = (f32[1536]{0:T(1024)}, f32[1536]{0:T(1024)S(1)}, u32[]{:S(2)}) copy-start(f32[1536]{0:T(1024)S(1)} %get-tuple-element.232) | copy-start | bytes 18436
  231.2 22.4 %copy-start.52 = (f32[1024]{0:T(1024)}, f32[1024]{0:T(1024)S(1)}, u32[]{:S(2)}) copy-start(f32[1024]{0:T(1024)S(1)} %add_rsqrt_fusion.2) | copy-start | bytes 12292
  234.5 19.1 %copy-start.7 = (bf16[1024,1536]{1,0:T(8,128)(2,1)}, bf16[1024,1536]{1,0:T(8,128)(2,1)S(1)}, u32[]{:S(2)}) copy-start(bf16[1024,1536]{1,0:T(8,128)(2,1)S(1)} %add_convert_fusion.4.x_ref.refs_0_) | copy-start | bytes 9437188
  253.6 45.5 %copy-start = (bf16[2,1024,2304]{2,1,0:T(8,128)(2,1)}, bf16[2,1024,2304]{2,1,0:T(8,128)(2,1)S(1)}, u32[]{:S(2)}) copy-start(bf16[2,1024,2304]{2,1,0:T(8,128)(2,1)S(1)} %shard_map.244.q_ref.k_ref.v_ref.refs_0_.refs_1_.refs_2_) | copy-start | bytes 28311556
  259.3 65.2 %collective-permute-start = (bf16[512,1536]{1,0:T(8,128)(2,1)}, bf16[512,1536]{1,0:T(8,128)(2,1)}, u32[]{:S(2)}, u32[]{:S(2)}) collective-permute-start(bf16[512,1536]{1,0:T(8,128)(2,1)} %fusion.23), channel_id=1, source_target_pairs={{0,1},{1,0},{2,3},{3,2},{4,5},{5,4},{6,7},{7,6},{8,9},{9,8},{10,11... | collective-permute-start | bytes 4718600 | tf_op jit(solution)/shard_map/ppermute | solution.py:1399
  313.5 7.4 copy-start.51
  316.7 6.4 copy-start.45
  316.7 6.4 copy-start.22
  320.9 13.9 %copy-start.36 = (bf16[64,1536]{1,0:T(8,128)(2,1)}, bf16[64,1536]{1,0:T(8,128)(2,1)S(1)}, u32[]{:S(2)}) copy-start(bf16[64,1536]{1,0:T(8,128)(2,1)S(1)} %maximum_select_fusion.5.refs_1_) | copy-start | bytes 589828
  323.1 4.4 copy-start.26
  324.5 13.6 %copy-start.8 = (bf16[1024,1536]{1,0:T(8,128)(2,1)}, bf16[1024,1536]{1,0:T(8,128)(2,1)S(1)}, u32[]{:S(2)}) copy-start(bf16[1024,1536]{1,0:T(8,128)(2,1)S(1)} %add_convert_fusion.3.x_ref.refs_0_) | copy-start | bytes 9437188
  338.1 7.1 copy-start.15
  345.2 11.7 %copy-start.12 = (bf16[2,1024,768]{2,1,0:T(8,128)(2,1)}, bf16[2,1024,768]{2,1,0:T(8,128)(2,1)S(1)}, u32[]{:S(2)}) copy-start(bf16[2,1024,768]{2,1,0:T(8,128)(2,1)S(1)} %shard_map.247.q_ref) | copy-start | bytes 9437188
  358.7 21.5 %collective-permute-start.1 = (f32[2,2,12]{2,1,0:T(2,128)S(1)}, f32[2,2,12]{2,1,0:T(2,128)S(1)}, u32[]{:S(2)}, u32[]{:S(2)}) collective-permute-start(f32[2,2,12]{2,1,0:T(2,128)S(1)} %constant_dynamic-update-slice_fusion), channel_id=1, source_target_pairs={{0,2},{2,0},{4,6},{6,4},{8,10},{10,8},{12,14},{14,12},{16,18},{18,... | collective-permute-start | bytes 584 | tf_op jit(solution)/shard_map/ppermute | solution.py:1399
  374.7 7.5 copy-start.24
  374.7 8.8 copy-start.47
  380.3 22.2 %copy-start.56 = (f32[1024]{0:T(1024)}, f32[1024]{0:T(1024)S(1)}, u32[]{:S(2)}) copy-start(f32[1024]{0:T(1024)S(1)} %add_rsqrt_fusion) | copy-start | bytes 12292
  380.3 3.7 collective-permute-start.2
  384.0 18.5 %collective-permute-start.3 = (f32[2,2,12]{2,1,0:T(2,128)S(1)}, f32[2,2,12]{2,1,0:T(2,128)S(1)}, u32[]{:S(2)}, u32[]{:S(2)}) collective-permute-start(f32[2,2,12]{2,1,0:T(2,128)S(1)} %max.20), channel_id=1, source_target_pairs={{0,4},{2,6},{4,0},{6,2},{8,12},{10,14},{12,8},{14,10},{16,20},{18,... | collective-permute-start | bytes 584 | tf_op jit(solution)/shard_map/ppermute | solution.py:1399
  402.5 15.8 %copy-start.10 = (bf16[1024,1536]{1,0:T(8,128)(2,1)S(1)}, bf16[1024,1536]{1,0:T(8,128)(2,1)}, u32[]{:S(2)}) copy-start(bf16[1024,1536]{1,0:T(8,128)(2,1)} %fusion.16.x_ref) | copy-start | bytes 9437188
  402.5 15.7 %collective-permute-start.4 = (f32[2,2,12]{2,1,0:T(2,128)S(1)}, f32[2,2,12]{2,1,0:T(2,128)S(1)}, u32[]{:S(2)}, u32[]{:S(2)}) collective-permute-start(f32[2,2,12]{2,1,0:T(2,128)S(1)} %max.21), channel_id=1, source_target_pairs={{0,8},{2,10},{4,12},{6,14},{8,0},{10,2},{12,4},{14,6},{16,24},{18,... | collective-permute-start | bytes 584 | tf_op jit(solution)/shard_map/ppermute | solution.py:1399
  418.2 27.1 %copy-start.21 = (bf16[1024,3072]{1,0:T(8,128)(2,1)}, bf16[1024,3072]{1,0:T(8,128)(2,1)S(1)}, u32[]{:S(2)}) copy-start(bf16[1024,3072]{1,0:T(8,128)(2,1)S(1)} %get-tuple-element.120.y0_ref.refs_0_) | copy-start | bytes 18874372
  418.2 27.1 %collective-permute-start.5 = (f32[2,2,12]{2,1,0:T(2,128)S(1)}, f32[2,2,12]{2,1,0:T(2,128)S(1)}, u32[]{:S(2)}, u32[]{:S(2)}) collective-permute-start(f32[2,2,12]{2,1,0:T(2,128)S(1)} %max.22), channel_id=1, source_target_pairs={{0,16},{2,18},{4,20},{6,22},{8,24},{10,26},{12,28},{14,30},{16,0},... | collective-permute-start | bytes 584 | tf_op jit(solution)/shard_map/ppermute | solution.py:1399
  418.3 29.9 %slice-start.10 = ((f32[96,2,768]{2,1,0:T(2,128)}), f32[96,1,768]{2,1,0:T(1,128)S(1)}, s32[]{:S(2)}) async-start(f32[96,2,768]{2,1,0:T(2,128)} %param.20), calls=%async_computation.14 | async-start | bytes 589824 | tf_op jit(solution)/shard_map/slice | solution.py:1535
  450.1 19.7 %copy-start.11 = (bf16[1024,1536]{1,0:T(8,128)(2,1)S(1)}, bf16[1024,1536]{1,0:T(8,128)(2,1)}, u32[]{:S(2)}) copy-start(bf16[1024,1536]{1,0:T(8,128)(2,1)} %fusion.16.x_ref) | copy-start | bytes 9437188
  486.0 27.1 %copy-start.2 = (bf16[1024,3072]{1,0:T(8,128)(2,1)}, bf16[1024,3072]{1,0:T(8,128)(2,1)S(1)}, u32[]{:S(2)}) copy-start(bf16[1024,3072]{1,0:T(8,128)(2,1)S(1)} %add_convert_fusion.1.y0_ref.refs_0_) | copy-start | bytes 18874372
  513.1 28.4 %slice-start.4 = ((s8[6291456]{0:T(1024)(128)(4,1)}), s8[2097152]{0:T(1024)(128)(4,1)S(1)}, s32[]{:S(2)}) async-start(s8[6291456]{0:T(1024)(128)(4,1)} %bitcast.170), calls=%async_computation.8 | async-start | bytes 4194304
  513.1 28.3 %slice-start.5 = ((s8[6291456]{0:T(1024)(128)(4,1)}), s8[4194304]{0:T(1024)(128)(4,1)S(1)}, s32[]{:S(2)}) async-start(s8[6291456]{0:T(1024)(128)(4,1)} %bitcast.170), calls=%async_computation.9 | async-start | bytes 8388608
  513.2 28.3 %copy-start.42 = (f32[1536]{0:T(1024)S(1)}, f32[1536]{0:T(1024)}, u32[]{:S(2)}) copy-start(f32[1536]{0:T(1024)} %copy-done.41) | copy-start | bytes 18436
  513.2 28.3 %copy-start.48 = (f32[1024]{0:T(1024)S(1)}, f32[1024]{0:T(1024)}, u32[]{:S(2)}) copy-start(f32[1024]{0:T(1024)} %copy-done.47) | copy-start | bytes 12292
  513.2 28.3 %copy-start.57 = (f32[1024]{0:T(1024)S(1)}, f32[1024]{0:T(1024)}, u32[]{:S(2)}) copy-start(f32[1024]{0:T(1024)} %copy-done.56) | copy-start | bytes 12292
  560.8 8.4 copy-start.9
  560.8 8.4 copy-start.13
  560.8 8.4 copy-start.16
  569.2 34.0 %slice-start = ((s8[6291456]{0:T(1024)(128)(4,1)}), s8[4194304]{0:T(1024)(128)(4,1)S(1)}, s32[]{:S(2)}) async-start(s8[6291456]{0:T(1024)(128)(4,1)} %bitcast.166), calls=%async_computation.4 | async-start | bytes 8388608
  592.5 10.6 slice-start.1
  592.5 10.6 copy-start.40
  592.5 10.7 copy-start.46
  592.5 10.7 copy-start.55
  603.2 5.3 copy-start.25
  614.4 8.1 copy-start.6
  642.8 62.0 %copy-start.20 = (bf16[2,64,768]{2,1,0:T(8,128)(2,1)S(1)}, bf16[2,64,768]{2,1,0:T(8,128)(2,1)}, u32[]{:S(2)}) copy-start(bf16[2,64,768]{2,1,0:T(8,128)(2,1)} %copy-done.19) | copy-start | bytes 589828
  642.9 62.0 %copy-start.18 = (bf16[2,64,768]{2,1,0:T(8,128)(2,1)S(1)}, bf16[2,64,768]{2,1,0:T(8,128)(2,1)}, u32[]{:S(2)}) copy-start(bf16[2,64,768]{2,1,0:T(8,128)(2,1)} %copy-done.17) | copy-start | bytes 589828
  876.6 73.3 %slice-start.2 = ((s8[6291456]{0:T(1024)(128)(4,1)}), s8[4194304]{0:T(1024)(128)(4,1)S(1)}, s32[]{:S(2)}) async-start(s8[6291456]{0:T(1024)(128)(4,1)} %bitcast.168), calls=%async_computation.6 | async-start | bytes 8388608
  913.8 36.1 %slice-start.3 = ((s8[6291456]{0:T(1024)(128)(4,1)}), s8[2097152]{0:T(1024)(128)(4,1)S(1)}, s32[]{:S(2)}) async-start(s8[6291456]{0:T(1024)(128)(4,1)} %bitcast.168), calls=%async_computation.7 | async-start | bytes 4194304
  913.8 36.1 %copy-start.38 = (f32[1536]{0:T(1024)S(1)}, f32[1536]{0:T(1024)}, u32[]{:S(2)}) copy-start(f32[1536]{0:T(1024)} %copy-done.37) | copy-start | bytes 18436
  913.8 36.1 %copy-start.44 = (f32[1024]{0:T(1024)S(1)}, f32[1024]{0:T(1024)}, u32[]{:S(2)}) copy-start(f32[1024]{0:T(1024)} %copy-done.43) | copy-start | bytes 12292
  913.8 36.1 %copy-start.53 = (f32[1024]{0:T(1024)S(1)}, f32[1024]{0:T(1024)}, u32[]{:S(2)}) copy-start(f32[1024]{0:T(1024)} %copy-done.52) | copy-start | bytes 12292
  949.9 5.0 copy-start.59
  950.0 5.0 copy-start.58
  950.0 5.7 copy-start.29
  950.0 5.7 copy-start.30
  1035.4 9.2 copy-start.50
  1037.7 12.4 %slice-start.8 = ((s8[6291456]{0:T(1024)(128)(4,1)}), s8[2097152]{0:T(1024)(128)(4,1)S(1)}, s32[]{:S(2)}) async-start(s8[6291456]{0:T(1024)(128)(4,1)} %bitcast.175), calls=%async_computation.12 | async-start | bytes 4194304
  1044.6 5.5 slice-start.9
  (18 other events, 33.6 us)
Sparse Core Ops, SparseCore 0:
  21.4 285.9 all-gather.2
  310.9 123.0 all-gather.4
  513.2 373.2 reduce-scatter.1

commit v3 on v2

--- a/solution.py
+++ b/solution.py
@@ -802,14 +802,15 @@
     return (dp + 1 - 2 * (dp % CORES), lax.axis_index("mp"))
 
 
-def hosted(body, number, grid, args, in_specs, out_shape, out_specs, scratch, plan, flops, core=False):
+def hosted(body, number, grid, args, in_specs, out_shape, out_specs, scratch, plan, flops, core=False, near=False, after=(), closing=None):
     special = {"x0": Swap, "total": Total}
-    hops = [special[k](group) if k in special else Hop(k, group) for k, group in plan]
+    hops = [special[k](group) if k in special else Hop(k, group) for k, group in (*plan, *after)]
+    made = {(id(hop.group), hop.kind): k for k, hop in enumerate(hops)}
     arrays, places = [], {}
     for hop in hops:
         for name in hop.names:
             key = (id(hop.group), name)
-            if key not in places:
+            if key not in places and key not in made:
                 places[key] = len(arrays)
                 arrays.append(hop.group.arrays[name])
     steps = 1
@@ -824,10 +825,12 @@
             parts.append(refs[at : at + n])
             at += n
         for k, hop in enumerate(hops):
-            sources = [parts[1][places[(id(hop.group), name)]] for name in hop.names]
+            keys = [(id(hop.group), name) for name in hop.names]
+            sources = [parts[3][made[key]] if key in made else parts[1][places[key]] for key in keys]
             taken = len(hop.scratch())
             hop.bind(sources, parts[3][k], refs[at : at + taken])
             at += taken
+        first, last = hops[: len(plan)], hops[len(plan) :]
         step = 0
         for axis, n in enumerate(grid):
             step = step * n + pl.program_id(axis)
@@ -835,22 +838,43 @@
         @pl.when(step == 0)
         def _():
             partners = [core_partner()] if core else []
+            if near:
+                dp, mp = lax.axis_index("dp"), lax.axis_index("mp")
+                partners += [(dp, 1 - mp), (dp + CORES - 2 * CORES * ((dp // CORES) % Y), mp)]
             for kind in sorted(kinds):
                 partners += [hop for hop in hops if hop.kind[0] == kind][0].partners()
             if partners:
                 meet(partners)
-            for hop in hops:
+            for hop in first:
                 hop.begin()
 
-        for j in range(max([hop.each(steps) for hop in hops], default=0)):
-            for hop in hops:
+        for j in range(max([hop.each(steps) for hop in first], default=0)):
+            for hop in first:
                 if j < hop.each(steps):
                     hop.work(step, steps, j)
         body(*parts[0], *parts[2], *parts[4])
 
         @pl.when(step == steps - 1)
         def _():
-            for hop in sorted(hops, key=lambda hop: hop.kind != "total"):
+            left = sorted(first, key=lambda hop: hop.kind != "total")
+            if last:
+                for hop in first:
+                    if hop.kind in ("x2", "y2"):
+                        hop.finish()
+                        left.remove(hop)
+                for hop in last:
+                    if hop.kind != "total":
+                        hop.begin()
+                        for j in range(hop.count):
+                            hop.work(0, 1, j)
+            if closing is not None:
+                closing(*parts[0], *parts[2], *parts[4])
+            for hop in left:
+                hop.finish()
+            for hop in last:
+                if hop.kind == "total":
+                    hop.begin()
+            for hop in last:
                 hop.finish()
 
     hbm = pl.BlockSpec(memory_space=pl.ANY)
@@ -1175,7 +1199,7 @@
 
 
 def unproject_both(number, plan, pieces, whole, begin, width, base=None):
-    frames, depth, tile = pieces[0][0].shape[-2], whole.shape[1], 256
+    frames, depth, tile = pieces[0][0].shape[-2], whole.shape[1], 512 if width < 1024 else 256
     first, direct = begin // width, len(pieces) == 2
     bases = [] if base is None else [base]
 
@@ -1218,15 +1242,53 @@
     return [(array, 0, 0), (array, 1, 0)]
 
 
-def relay(number, plan, value):
-    def body(value_ref, total_ref, sums, got, send_sem, recv_sem):
+def norm_back_last(number, plan, after, stream, grad, gain, passed, others):
+    frames, depth = stream.shape
+    steps = 8
+    size, half = frames // steps, steps // 2
+
+    def swapped(got_ref, sent, send_sem, recv_sem, t):
+        return pltpu.make_async_remote_copy(
+            src_ref=sent.at[t],
+            dst_ref=got_ref.at[t],
+            send_sem=send_sem.at[t],
+            recv_sem=recv_sem.at[t],
+            device_id=(lax.axis_index("dp"), 1 - lax.axis_index("mp")),
+            device_id_type=MESH,
+        )
+
+    def body(stream_ref, grad_ref, gain_ref, passed_ref, others_ref, o_ref, got_ref, total_ref, *scratch):
+        sent, send_sem, recv_sem, sums = scratch[:4]
+        step = pl.program_id(0)
+        rows, inverse = norm_rows_of(stream_ref[...])
+        grads = grad_ref[...]
+        scaled = grads * gain_ref[...]
+        products = jnp.mean(scaled * rows, axis=-1, keepdims=True)
+        back = inverse * (scaled - jnp.mean(scaled, axis=-1, keepdims=True) - rows * products)
+        total = passed_ref[...] + back
+        o_ref[...] = total
+
+        @pl.when(step == 0)
+        def _():
+            sums[0] = others_ref[...]
+
+        sums[0, 0:1, :] += jnp.sum(grads * rows, axis=0, keepdims=True)
+        sums[0, 1:2, :] += jnp.sum(grads, axis=0, keepdims=True)
+
+        @pl.when(step // half == 1 - lax.axis_index("mp"))
+        def _():
+            sent[step % half] = total.astype(bf16)
+            swapped(got_ref, sent, send_sem, recv_sem, step % half).start()
+
+    def closing(stream_ref, grad_ref, gain_ref, passed_ref, others_ref, o_ref, got_ref, total_ref, *scratch):
+        sent, swap_send, swap_recv, sums, got, send_sem, recv_sem = scratch
         dp, mp = lax.axis_index("dp"), lax.axis_index("mp")
         group = Y * CORES
         z, rest = dp // group, dp % group
-        partners = [core_partner(), (dp, 1 - mp), (dp + CORES - 2 * CORES * ((dp // CORES) % Y), mp)]
+        partners = [core_partner(), (dp + CORES - 2 * CORES * ((dp // CORES) % Y), mp)]
         partners.append(((z + 1 - 2 * (z % 2)) * group + rest, mp))
         partners.append((((z + 2) % Z) * group + rest, mp))
-        sums[0] = value_ref[...]
+        partners.append((dp, 1 - mp))
         for i, partner in enumerate(partners):
             copy = pltpu.make_async_remote_copy(
                 src_ref=sums.at[i],
@@ -1240,30 +1302,40 @@
             copy.wait()
             sums[i + 1] = sums[i] + got[i]
         total_ref[...] = sums[5]
-
-    whole = pl.BlockSpec(value.shape, lambda i: (0, 0))
-    return hosted(
+        for t in range(half):
+            swapped(got_ref, sent, swap_send, swap_recv, t).wait()
+
+    block = pl.BlockSpec((size, depth), lambda i: (i, 0))
+    hbm = pl.BlockSpec(memory_space=pl.ANY)
+    sums = pl.BlockSpec((8, depth), lambda i: (0, 0))
+    total, got, sums = hosted(
         body,
         number,
-        (1,),
-        [value],
-        [whole],
-        [jax.ShapeDtypeStruct(value.shape, f32)],
-        [whole],
+        (steps,),
+        [stream, grad, gain, passed, others],
+        [block, block, pl.BlockSpec((1, depth), lambda i: (0, 0)), block, sums],
         [
-            pltpu.VMEM((6,) + value.shape, f32),
-            pltpu.VMEM((5,) + value.shape, f32),
+            jax.ShapeDtypeStruct((frames, depth), f32),
+            jax.ShapeDtypeStruct((half, size, depth), bf16),
+            jax.ShapeDtypeStruct((8, depth), f32),
+        ],
+        [block, hbm, sums],
+        [
+            pltpu.VMEM((half, size, depth), bf16),
+            pltpu.SemaphoreType.DMA((half,)),
+            pltpu.SemaphoreType.DMA((half,)),
+            pltpu.VMEM((6, 8, depth), f32),
+            pltpu.VMEM((5, 8, depth), f32),
             pltpu.SemaphoreType.DMA((5,)),
             pltpu.SemaphoreType.DMA((5,)),
         ],
         plan,
         10**9,
         core=True,
-    )[0]
-
-
-def last_hop(number, plan):
-    hosted(lambda: None, number, (1,), [], [], [], [], [], plan, 10**9)
+        after=after,
+        closing=closing,
+    )
+    return total, got.reshape(frames // 2, depth), sums
 
 
 def pair_rows(array, masks):
@@ -1613,26 +1685,25 @@
         0,
         3 * width,
     )
-    back, gain_one, bias_one = norm_back(stream, norms[0], grad_normed)
-    norm_grads = jnp.stack([gain_one, bias_one, gain_two, bias_two, gain_three, bias_three])
-    grad_inputs = grad_stream + back
-    sent = other_frames(grad_inputs)
-    swaps_inputs = [Holder(sent[: sent.shape[0] // 2]), Holder(sent[sent.shape[0] // 2 :])]
-    norm_grads = relay(
+    grad_inputs, got_inputs, norm_grads = norm_back_last(
         9,
         [
             ("x2", group_late),
             ("y2", group_late),
             ("za", group_early),
             ("zb", group_early),
-            ("x0", swaps_inputs[0]),
             ("total", group_pair),
             ("total", group_out),
         ],
-        jnp.pad(norm_grads, ((0, 2), (0, 0))),
-    )[:6]
-    last_hop(10, [("za", group_late), ("zb", group_late), ("x0", swaps_inputs[1]), ("total", group_early)])
-    grad_inputs = own_frames(grad_inputs, jnp.concatenate([h.got() for h in swaps_inputs]))
+        [("za", group_late), ("zb", group_late), ("total", group_early)],
+        stream,
+        grad_normed,
+        norms[0:1],
+        grad_stream,
+        jnp.pad(jnp.stack([gain_two, bias_two, gain_three, bias_three]), ((2, 2), (0, 0))),
+    )
+    norm_grads = norm_grads[:6]
+    grad_inputs = own_frames(grad_inputs, got_inputs)
     grad_text = own_frames(grad_text, swap_text.got())
     output = own_frames(output, swap_output.got())
     shard_pair, shard_outs = group_pair.arrays["total"], group_out.arrays["total"]

time: 1070 us -> 1050 us (0.981)
  other arithmetic: 98.2 us -> 85.4 us
    pallas_call x14 -> x13, Pallas kernels: 437 us -> 429 us  [hosted(): pl.pallas_call(kernel, grid=grid, in_specs=list(in_specs) + [hbm] * len(a...]
  transfers between devices with their start and end apart: 9 -> 9, of which waited for: 1 -> 1; matrix products, arithmetic and copies ran while one was open for 16% -> 15% of each run, Pallas kernels for 73% -> 74%
where the time goes in v3:
time: 1050 us; the launch traced here: 1040 us
  Pallas kernels  799 us (76%)
  other arithmetic  85.4 us (8%)
  matrix products  82.4 us (8%)
  local copies, waits for them, and re-layouts  54.9 us (5%)
  between operations  15.2 us (1%)
    pallas_call x13, Pallas kernels, hosted(): pl.pallas_call(kernel, grid=grid, in_specs=list(in_specs) + [hbm] * len(a...  429 us
    pallas_call x1, Pallas kernels, gather_now(): pl.pallas_call(functools.partial(gather_kernel, parts, len(swaps)), in_sp...  201 us
    dot_general x8, matrix products, dotf(): return lax.dot_general(a, b, dims, preferred_element_type=f32)  82.4 us
    pallas_call x2, Pallas kernels, weight_grad_whole(): pl.pallas_call(weight_grad_whole_kernel, grid=(2, tiles), in_specs=[pl.Bl...  53.6 us
    pallas_call x4, Pallas kernels, project_both(): pl.pallas_call(project_kernel, grid=(2, width // tile), in_specs=[pl.Bloc...  43.2 us
    pallas_call x1, Pallas kernels, self_attend(): pl.pallas_call(functools.partial(self_forward_kernel, 512), grid=(2, pair...  39.8 us
    convert_element_type x14, other arithmetic, rounded(): return values.astype(jnp.bfloat16)  34.6 us
  transfers between devices with their start and end apart: 9, of which 1 were waited for; matrix products, arithmetic and copies ran while one was open for 15% of the time, Pallas kernels for 74%

profile of v3, /device:TPU:0, one launch (start us, length us, event | category | flops | bytes accessed | tf_op | source)
XLA Modules:
  0.0 1042.8 jit_solution(17142717058288492489)
XLA Ops:
  8.6 1.4 convert_element_type.197
  15.5 3.2 fusion.22.refs_1_
  22.4 201.1 %shard_map.243 = (bf16[2,4,4,96,3200]{4,3,2,1,0:T(8,128)(2,1)}, bf16[512,1536]{1,0:T(8,128)(2,1)}, bf16[32,1536]{1,0:T(8,128)(2,1)}) custom-call(bf16[96,3200]{1,0:T(8,128)(2,1)} %fusion.25.refs_0_, bf16[512,1536]{1,0:T(8,128)(2,1)} %fusion.22.refs_1_, bf16[32,1536]{1,0:T(8,128)(2,1)} %get-tuple-element.94.refs_2_), custom_call_target="tpu_custom_call" | custom-call | flops 1000000000 | bytes 100000000 | tf_op jit(solution)/shard_map/pallas_call | solution.py:1155
  223.4 1.8 convert_element_type.202
  227.1 2.1 dynamic-slice_bitcast_fusion.3
  234.4 19.1 %shard_map.244.q_ref.k_ref.v_ref.refs_0_.refs_1_.refs_2_ = bf16[2,1024,2304]{2,1,0:T(8,128)(2,1)S(1)} custom-call(bf16[1024,1536]{1,0:T(8,128)(2,1)S(1)} %add_convert_fusion.4.x_ref.refs_0_, bf16[2,1536,3200]{2,1,0:T(8,128)(2,1)} %bitcast.160), custom_call_target="tpu_custom_call" | custom-call | flops 14495514624 | bytes 23592960 | tf_op jit(solution)/shard_map/pallas_call | solution.py:1183
  253.5 5.6 fusion.23
  259.2 39.8 %shard_map.245 = (bf16[2,1024,768]{2,1,0:T(8,128)(2,1)S(1)}, f32[2,6,8,1024]{3,2,1,0:T(8,128)S(1)}, f32[2,6,8,128]{3,2,1,0:T(8,128)S(1)}) custom-call(bf16[2,1024,2304]{2,1,0:T(8,128)(2,1)S(1)} %shard_map.244.q_ref.k_ref.v_ref.refs_0_.refs_1_.refs_2_, bf16[2,1024,2304]{2,1,0:T(8,128)(2,1)S(1)} %shard_map.244.q_ref.k_ref.v_ref.refs_0_.refs_1_.refs_2_, ...), custom_call_target="tpu_custom_call" | custom-call | flops 12884901888 | bytes 12582912 | tf_op jit(solution)/shard_map/pallas_call | solution.py:480
  299.0 1.6 copy-done.3
  301.6 11.5 %shard_map.246.refs_4_ = f32[1024,1536]{1,0:T(8,128)} custom-call(bf16[2,1024,768]{2,1,0:T(8,128)(2,1)} %copy-done.3, bf16[2,1024,768]{2,1,0:T(8,128)(2,1)} %copy-done.3, bf16[2,1536,3200]{2,1,0:T(8,128)(2,1)} %bitcast.161, bf16[2,1536,3200]{2,1,0:T(8,128)(2,1)} %bitcast.162, f32[1024,1536]{1,0:T(8,128)} %copy-done.24), custom_call_target="tpu_custom_call" | custom-call | flops 4831838208 | bytes 9663676 | tf_op jit(solution)/shard_map/pallas_call | solution.py:882
  313.1 3.2 reduce_sum.144
  316.3 4.1 multiply_reduce_fusion.5
  320.6 2.2 dynamic-slice_bitcast_fusion.2
  322.8 1.4 add_convert_fusion.3.x_ref.refs_0_
  324.2 2.9 convert_element_type.215
  327.1 1.7 copy-done.27
  328.8 2.5 fusion.16.x_ref
  331.3 3.3 fusion.20
  334.6 3.3 fusion.21
  338.0 7.1 shard_map.247.q_ref
  345.0 11.7 %shard_map.248 = (bf16[2,1024,768]{2,1,0:T(8,128)(2,1)S(1)}, f32[2,6,8,128]{3,2,1,0:T(8,128)S(1)}) custom-call(bf16[2,1024,768]{2,1,0:T(8,128)(2,1)S(1)} %shard_map.247.q_ref, bf16[2,64,1536]{2,1,0:T(8,128)(2,1)S(1)} %pad_maximum_fusion.2.k_ref.v_ref, bf16[2,64,1536]{2,1,0:T(8,128)(2,1)S(1)} %pad_maximum_fusion.2.k_ref.v_ref), custom_call_target="tpu_custom_call" | custom-call | flops 3221225472 | bytes 6291456 | tf_op jit(solution)/shard_map/pallas_call | solution.py:1372
  356.8 1.6 copy-done.4
  359.6 11.5 %shard_map.249.refs_4_ = f32[1024,1536]{1,0:T(8,128)} custom-call(bf16[2,1024,768]{2,1,0:T(8,128)(2,1)} %copy-done.4, bf16[2,1024,768]{2,1,0:T(8,128)(2,1)} %copy-done.4, bf16[2,1536,6144]{2,1,0:T(8,128)(2,1)} %bitcast.148, bf16[2,1536,6144]{2,1,0:T(8,128)(2,1)} %bitcast.149, f32[1024,1536]{1,0:T(8,128)} %shard_map.246.refs_4_), custom_call_target="tpu_custom_call" | custom-call | flops 4831838208 | bytes 9663676 | tf_op jit(solution)/shard_map/pallas_call | solution.py:882
  371.1 3.1 reduce_sum.146
  374.3 5.5 multiply_reduce_fusion.4
  379.8 1.8 collective-permute-start.2
  383.5 2.4 collective-permute-start.3
  385.9 16.1 %multiply_convert_fusion = (bf16[1024,3072]{1,0:T(8,128)(2,1)}, f32[1024,3072]{1,0:T(8,128)}) fusion(bf16[1024,1536]{1,0:T(8,128)(2,1)S(1)} %add_convert_fusion.2.x_ref, bf16[2,1536,6144]{2,1,0:T(8,128)(2,1)} %bitcast.150), kind=kOutput, calls=%fused_computation.2 | convolution fusion | flops 9679405056 | bytes 31457280 | tf_op jit(solution)/shard_map/dot_general | solution.py:429
  402.1 15.6 %multiply_convert_fusion.1 = (bf16[1024,3072]{1,0:T(8,128)(2,1)S(1)}, f32[1024,3072]{1,0:T(8,128)}) fusion(bf16[1024,1536]{1,0:T(8,128)(2,1)S(1)} %add_convert_fusion.2.x_ref, bf16[2,1536,6144]{2,1,0:T(8,128)(2,1)} %bitcast.151), kind=kOutput, calls=%fused_computation.4 | convolution fusion | flops 9679405056 | bytes 31457280 | tf_op jit(solution)/shard_map/dot_general | solution.py:429
  417.8 26.9 %shard_map.250.refs_0_ = bf16[2,1536,6144]{2,1,0:T(8,128)(2,1)} custom-call(bf16[1024,1536]{1,0:T(8,128)(2,1)S(1)} %copy-done.10, bf16[1024,3072]{1,0:T(8,128)(2,1)S(1)} %get-tuple-element.118.y0_ref.refs_0_, bf16[1024,3072]{1,0:T(8,128)(2,1)} %get-tuple-element.119.y1_ref.refs_1_), custom_call_target="tpu_custom_call" | custom-call | flops 19327352832 | bytes 34603008 | tf_op jit(solution)/shard_map/pallas_call | solution.py:1448
  445.5 2.1 broadcast_multiply_fusion
  447.6 1.8 fusion.26
  449.4 19.7 %add_convert_fusion.y1_ref.refs_1_ = bf16[1024,3072]{1,0:T(8,128)(2,1)} fusion(f32[1024,3072]{1,0:T(8,128)} %get-tuple-element.260, bf16[1024,1536]{1,0:T(8,128)(2,1)} %fusion.16.x_ref, bf16[2,1536,3072]{2,1,0:T(8,128)(2,1)} %bitcast.181), kind=kOutput, calls=%fused_computation | convolution fusion | flops 9704570880 | bytes 31457280 | tf_op jit(solution)/shard_map/dot_general | solution.py:429
  469.2 16.4 %add_convert_fusion.1.y0_ref.refs_0_ = bf16[1024,3072]{1,0:T(8,128)(2,1)S(1)} fusion(f32[1024,3072]{1,0:T(8,128)} %get-tuple-element.258, bf16[1024,1536]{1,0:T(8,128)(2,1)S(1)} %copy-done.11, bf16[2,1536,3072]{2,1,0:T(8,128)(2,1)} %bitcast.182), kind=kOutput, calls=%fused_computation.1 | convolution fusion | flops 9704570880 | bytes 31457280 | tf_op jit(solution)/shard_map/dot_general | solution.py:429
  485.6 26.7 %shard_map.251 = bf16[2,1536,6144]{2,1,0:T(8,128)(2,1)} custom-call(bf16[1024,1536]{1,0:T(8,128)(2,1)S(1)} %add_convert_fusion.2.x_ref, bf16[1024,3072]{1,0:T(8,128)(2,1)S(1)} %add_convert_fusion.1.y0_ref.refs_0_, bf16[1024,3072]{1,0:T(8,128)(2,1)} %add_convert_fusion.y1_ref.refs_1_, ...), custom_call_target="tpu_custom_call", output_to_operand_aliasing={{}: (3, {})} | custom-call | flops 19327352832 | bytes 34603008 | tf_op jit(solution)/shard_map/pallas_call | solution.py:1448
  512.4 27.9 %shard_map.252 = f32[1024,1536]{1,0:T(8,128)} custom-call(bf16[1024,3072]{1,0:T(8,128)(2,1)} %copy-done.2, bf16[1024,3072]{1,0:T(8,128)(2,1)} %add_convert_fusion.y1_ref.refs_1_, bf16[2,1536,6144]{2,1,0:T(8,128)(2,1)} %bitcast.152, bf16[2,1536,6144]{2,1,0:T(8,128)(2,1)} %bitcast.153), custom_call_target="tpu_custom_call" | custom-call | flops 19327352832 | bytes 38654704 | tf_op jit(solution)/shard_map/pallas_call | solution.py:882
  540.3 5.4 multiply_reduce_fusion
  545.7 13.4 %fusion.43 = (bf16[1024,1536]{1,0:T(8,128)(2,1)S(1)}, f32[1024,1536]{1,0:T(8,128)}) fusion(f32[1024]{0:T(1024)S(1)} %broadcast_multiply_fusion.4, f32[1024,1536]{1,0:T(8,128)S(1)} %bitcast.169, f32[1024]{0:T(1024)S(1)} %copy-done.42, f32[1024]{0:T(1024)S(1)} %broadcast_multiply_fusion.5, f32[1024,1536]{1,0:T(8,128)} %shard_map.252, f32[1536]{0:T(1024)S(1)} %copy-done.38, ...), kind=kLoop, calls=%fused_computation.139 | loop fusion | flops 18874368 | bytes 28334080 | tf_op jit(solution)/shard_map/convert_element_type | solution.py:31
  559.1 8.9 shard_map.253.g_ref
  568.1 20.1 %shard_map.254 = (bf16[2,1024,768]{2,1,0:T(8,128)(2,1)S(1)}, bf16[2,64,768]{2,1,0:T(8,128)(2,1)S(1)}, bf16[2,64,768]{2,1,0:T(8,128)(2,1)S(1)}) custom-call(bf16[2,1024,768]{2,1,0:T(8,128)(2,1)S(1)} %copy-done.13, bf16[2,64,1536]{2,1,0:T(8,128)(2,1)S(1)} %copy-done.16, bf16[2,64,1536]{2,1,0:T(8,128)(2,1)S(1)} %copy-done.16, ...), custom_call_target="tpu_custom_call" | custom-call | flops 6442450944 | bytes 9437184 | tf_op jit(solution)/shard_map/pallas_call | solution.py:1408
  588.2 1.6 copy-done.5
  591.2 9.8 shard_map.255
  601.1 5.2 multiply_reduce_fusion.1
  606.4 5.9 fusion.42
  612.4 8.1 shard_map.256.refs_3_
  620.4 1.6 copy-done.1
  622.1 18.8 %shard_map.257 = (bf16[2,4,2,96,2304]{4,3,2,1,0:T(8,128)(2,1)}, bf16[2,4,2,96,2304]{4,3,2,1,0:T(8,128)(2,1)}) custom-call(bf16[1024,1536]{1,0:T(8,128)(2,1)} %copy-done.8, bf16[64,1536]{1,0:T(8,128)(2,1)} %copy-done.34, bf16[2,1024,768]{2,1,0:T(8,128)(2,1)} %copy-done.5, bf16[2,1024,768]{2,1,0:T(8,128)(2,1)} %copy-done.5, bf16[2,64,768]{2,1,0:T(8,128)(2,1)} %copy-done.19, ...), custom_call_target="tpu_custom_call" | custom-call | flops 14495514624 | bytes 28991028 | tf_op jit(solution)/shard_map/pallas_call | solution.py:882
  640.9 63.4 %shard_map.258 = (bf16[2,1024,512]{2,1,0:T(8,128)(2,1)}, bf16[2,1024,512]{2,1,0:T(8,128)(2,1)}, bf16[2,1024,512]{2,1,0:T(8,128)(2,1)}, bf16[4,2,48,2304]{3,2,1,0:T(8,128)(2,1)}, bf16[2,4,48,2304]{3,2,1,0:T(8,128)(2,1)}) custom-call(bf16[2,1024,2304]{2,1,0:T(8,128)(2,1)} %copy-done, bf16[2,1024,2304]{2,1,0:T(8,128)(2,1)} %copy-done, ...), custom_call_target="tpu_custom_call" | custom-call | flops 8589934592 | bytes 17179868 | tf_op jit(solution)/shard_map/pallas_call | solution.py:882
  704.3 4.0 fusion.12
  708.4 4.1 fusion.17
  713.8 19.0 %shard_map.259 = (bf16[2,4,2,96,1536]{4,3,2,1,0:T(8,128)(2,1)}, bf16[2,4,2,96,1536]{4,3,2,1,0:T(8,128)(2,1)}) custom-call(bf16[1024,1536]{1,0:T(8,128)(2,1)} %copy-done.9, bf16[1024,1536]{1,0:T(8,128)(2,1)} %copy-done.6, bf16[2,1024,768]{2,1,0:T(8,128)(2,1)} %copy-done.4, bf16[2,1024,768]{2,1,0:T(8,128)(2,1)} %copy-done.4, bf16[2,1024,768]{2,1,0:T(8,128)(2,1)} %copy-done.3, ...), custom_call_target="tpu_custom_call" | custom-call | flops 9663676416 | bytes 19327352 | tf_op jit(solution)/shard_map/pallas_call | solution.py:882
  732.9 46.4 %shard_map.260 = (f32[1024,1536]{1,0:T(8,128)}, bf16[4,2,48,1536]{3,2,1,0:T(8,128)(2,1)}, bf16[2,4,48,1536]{3,2,1,0:T(8,128)(2,1)}) custom-call(bf16[1024,3072]{1,0:T(8,128)(2,1)} %copy-done.21, bf16[1024,3072]{1,0:T(8,128)(2,1)} %get-tuple-element.119.y1_ref.refs_1_, bf16[2,1536,3072]{2,1,0:T(8,128)(2,1)} %bitcast.183, bf16[2,1536,3072]{2,1,0:T(8,128)(2,1)} %bitcast.184, ...), custom_call_target="tpu_custom_call" | custom-call | flops 19327352832 | bytes 38654704 | tf_op jit(solution)/shard_map/pallas_call | solution.py:882
  779.2 3.3 dynamic-slice_convert_fusion.refs_15_
  782.5 31.5 %shard_map.261 = (bf16[2,4,2,96,1536]{4,3,2,1,0:T(8,128)(2,1)}, bf16[2,4,2,96,1536]{4,3,2,1,0:T(8,128)(2,1)}, bf16[32,1536]{1,0:T(8,128)(2,1)}, bf16[4,48,2304]{2,1,0:T(8,128)(2,1)}, bf16[4,48,2304]{2,1,0:T(8,128)(2,1)}) custom-call(bf16[1024,1536]{1,0:T(8,128)(2,1)} %copy-done.7, bf16[2,1024,512]{2,1,0:T(8,128)(2,1)} %get-tuple-element.126.refs_1_.refs_4_.refs_0_.refs_6_, ...), custom_call_target="tpu_custom_call" | custom-call | flops 9663676416 | bytes 19327352 | tf_op jit(solution)/shard_map/pallas_call | solution.py:882
  814.0 60.1 %shard_map.262 = (bf16[2,1024,256]{2,1,0:T(8,128)(2,1)}, bf16[2,1024,256]{2,1,0:T(8,128)(2,1)}, bf16[2,1024,256]{2,1,0:T(8,128)(2,1)}, bf16[4,48,1536]{2,1,0:T(8...) custom-call(bf16[2,1024,2304]{2,1,0:T(8,128)(2,1)} %copy-done, ...), custom_call_target="tpu_custom_call" | custom-call | flops 4294967296 | bytes 8589934 | tf_op jit(solution)/shard_map/pallas_call | solution.py:882
  874.2 33.4 %shard_map.263 = (bf16[2,4,2,96,768]{4,3,2,1,0:T(8,128)(2,1)}, bf16[2,4,2,96,768]{4,3,2,1,0:T(8,128)(2,1)}, bf16[4,2,48,1536]{3,2,1,0:T(8,128)(2,1)}, bf16[2,4,48,1536]{3,2,1,0:T(8,128)(2,1)}) custom-call(bf16[1024,1536]{1,0:T(8,128)(2,1)} %copy-done.7, bf16[2,1024,256]{2,1,0:T(8,128)(2,1)} %get-tuple-element.133.refs_1_.refs_4_.refs_3_.refs_9_, ...), custom_call_target="tpu_custom_call" | custom-call | flops 4831838208 | bytes 9663676 | tf_op jit(solution)/shard_map/pallas_call | solution.py:882
  909.8 37.4 %shard_map.264 = (f32[1024,1536]{1,0:T(8,128)}, bf16[4,2,48,768]{3,2,1,0:T(8,128)(2,1)}, bf16[2,4,48,768]{3,2,1,0:T(8,128)(2,1)}, bf16[4,48,1536]{2,1,0:T(8,128)...) custom-call(bf16[2,1024,512]{2,1,0:T(8,128)(2,1)} %get-tuple-element.126.refs_1_.ref, ...), custom_call_target="tpu_custom_call" | custom-call | flops 14495514624 | bytes 28991028 | tf_op jit(solution)/shard_map/pallas_call | solution.py:882
  949.7 58.8 %shard_map.265 = (f32[1024,1536]{1,0:T(8,128)}, bf16[4,128,1536]{2,1,0:T(8,128)(2,1)}, f32[8,1536]{1,0:T(8,128)}, bf16[4,48,768]{2,1,0:T(8,128)(2,1)}, bf16[4,48...) custom-call(f32[1024,1536]{1,0:T(8,128)} %copy-done.24, ...), custom_call_target="tpu_custom_call" | custom-call | flops 1000000000 | bytes 2000000 | tf_op jit(solution)/shard_map/pallas_call | solution.py:882
  1009.7 1.7 slice.189
  1017.2 1.4 fusion.36
  1018.6 1.6 pad_maximum_fusion.3
  1023.7 2.2 dynamic-slice_bitcast_fusion.1
  1027.8 5.4 maximum_select_fusion.2
  1033.2 2.9 fusion.45
  (215 shorter events, 42.6 us)
Async XLA Ops:
  7.2 8.1 copy-start.51
  7.2 11.5 %copy-start.43 = (f32[2,32,1536]{2,1,0:T(8,128)S(1)}, f32[2,32,1536]{2,1,0:T(8,128)}, u32[]{:S(2)}) copy-start(f32[2,32,1536]{2,1,0:T(8,128)} %param.13) | copy-start | bytes 1179652
  7.2 324.1 %all-gather.3.cloned.1.call-start = ((), (), s32[]{:S(2)}) async-start(), calls=%async_computation.1 | async-start | bytes 38928384 | tf_op jit(solution)/shard_map/all_gather | solution.py:1531
  8.6 12.8 %copy-start.30 = (f32[96,3072]{1,0:T(8,128)S(1)}, f32[96,3072]{1,0:T(8,128)}, u32[]{:S(2)}) copy-start(f32[96,3072]{1,0:T(8,128)} %param.23) | copy-start | bytes 3538948
  21.4 428.1 %all-gather.5.cloned.1.call-start = ((), (), s32[]{:S(2)}) async-start(), calls=%async_computation.2 | async-start | bytes 19464192 | tf_op jit(solution)/shard_map/all_gather | solution.py:1531
  22.3 1010.9 %reduce-scatter.2.cloned.1.call-start = ((), (), s32[]{:S(2)}) async-start(), calls=%async_computation.3 | async-start | bytes 38928384 | tf_op jit(solution)/shard_map/reduce_scatter | solution.py:1613
  230.4 2.7 copy-start.24
  230.4 0.8 copy-start.44
  232.3 90.4 %copy-start.35 = (f32[1536]{0:T(1024)}, f32[1536]{0:T(1024)S(1)}, u32[]{:S(2)}) copy-start(f32[1536]{0:T(1024)S(1)} %get-tuple-element.228) | copy-start | bytes 18436
  232.3 149.3 %copy-start.37 = (f32[1536]{0:T(1024)}, f32[1536]{0:T(1024)S(1)}, u32[]{:S(2)}) copy-start(f32[1536]{0:T(1024)S(1)} %get-tuple-element.224) | copy-start | bytes 18436
  234.4 19.1 %copy-start.7 = (bf16[1024,1536]{1,0:T(8,128)(2,1)}, bf16[1024,1536]{1,0:T(8,128)(2,1)S(1)}, u32[]{:S(2)}) copy-start(bf16[1024,1536]{1,0:T(8,128)(2,1)S(1)} %add_convert_fusion.4.x_ref.refs_0_) | copy-start | bytes 9437188
  253.5 45.5 %copy-start = (bf16[2,1024,2304]{2,1,0:T(8,128)(2,1)}, bf16[2,1024,2304]{2,1,0:T(8,128)(2,1)S(1)}, u32[]{:S(2)}) copy-start(bf16[2,1024,2304]{2,1,0:T(8,128)(2,1)S(1)} %shard_map.244.q_ref.k_ref.v_ref.refs_0_.refs_1_.refs_2_) | copy-start | bytes 28311556
  259.2 65.0 %collective-permute-start = (bf16[512,1536]{1,0:T(8,128)(2,1)}, bf16[512,1536]{1,0:T(8,128)(2,1)}, u32[]{:S(2)}, u32[]{:S(2)}) collective-permute-start(bf16[512,1536]{1,0:T(8,128)(2,1)} %fusion.23), channel_id=1, source_target_pairs={{0,1},{1,0},{2,3},{3,2},{4,5},{5,4},{6,7},{7,6},{8,9},{9,8},{10,11... | collective-permute-start | bytes 4718600 | tf_op jit(solution)/shard_map/ppermute | solution.py:1471
  299.0 1.6 copy-start.3
  313.1 7.4 copy-start.32
  313.1 7.4 copy-start.45
  316.3 6.4 copy-start.39
  316.3 6.4 copy-start.22
  320.5 3.7 copy-start.46
  320.5 14.1 %copy-start.34 = (bf16[64,1536]{1,0:T(8,128)(2,1)}, bf16[64,1536]{1,0:T(8,128)(2,1)S(1)}, u32[]{:S(2)}) copy-start(bf16[64,1536]{1,0:T(8,128)(2,1)S(1)} %maximum_select_fusion.5.refs_1_) | copy-start | bytes 589828
  322.7 4.4 copy-start.26
  324.1 13.8 %copy-start.8 = (bf16[1024,1536]{1,0:T(8,128)(2,1)}, bf16[1024,1536]{1,0:T(8,128)(2,1)S(1)}, u32[]{:S(2)}) copy-start(bf16[1024,1536]{1,0:T(8,128)(2,1)S(1)} %add_convert_fusion.3.x_ref.refs_0_) | copy-start | bytes 9437188
  327.1 1.7 copy-start.27
  337.9 7.1 copy-start.15
  345.0 11.7 %copy-start.12 = (bf16[2,1024,768]{2,1,0:T(8,128)(2,1)}, bf16[2,1024,768]{2,1,0:T(8,128)(2,1)S(1)}, u32[]{:S(2)}) copy-start(bf16[2,1024,768]{2,1,0:T(8,128)(2,1)S(1)} %shard_map.247.q_ref) | copy-start | bytes 9437188
  356.8 1.6 copy-start.4
  358.6 21.2 %collective-permute-start.1 = (f32[2,2,12]{2,1,0:T(2,128)S(1)}, f32[2,2,12]{2,1,0:T(2,128)S(1)}, u32[]{:S(2)}, u32[]{:S(2)}) collective-permute-start(f32[2,2,12]{2,1,0:T(2,128)S(1)} %constant_dynamic-update-slice_fusion), channel_id=1, source_target_pairs={{0,2},{2,0},{4,6},{6,4},{8,10},{10,8},{12,14},{14,12},{16,18},{18,... | collective-permute-start | bytes 584 | tf_op jit(solution)/shard_map/ppermute | solution.py:1471
  374.2 7.4 copy-start.23
  374.3 8.7 copy-start.41
  379.8 22.2 %copy-start.48 = (f32[1024]{0:T(1024)}, f32[1024]{0:T(1024)S(1)}, u32[]{:S(2)}) copy-start(f32[1024]{0:T(1024)S(1)} %add_rsqrt_fusion) | copy-start | bytes 12292
  379.8 3.7 collective-permute-start.2
  383.5 18.5 %collective-permute-start.3 = (f32[2,2,12]{2,1,0:T(2,128)S(1)}, f32[2,2,12]{2,1,0:T(2,128)S(1)}, u32[]{:S(2)}, u32[]{:S(2)}) collective-permute-start(f32[2,2,12]{2,1,0:T(2,128)S(1)} %max.20), channel_id=1, source_target_pairs={{0,4},{2,6},{4,0},{6,2},{8,12},{10,14},{12,8},{14,10},{16,20},{18,... | collective-permute-start | bytes 584 | tf_op jit(solution)/shard_map/ppermute | solution.py:1471
  402.0 15.8 %copy-start.10 = (bf16[1024,1536]{1,0:T(8,128)(2,1)S(1)}, bf16[1024,1536]{1,0:T(8,128)(2,1)}, u32[]{:S(2)}) copy-start(bf16[1024,1536]{1,0:T(8,128)(2,1)} %fusion.16.x_ref) | copy-start | bytes 9437188
  402.0 15.7 %collective-permute-start.4 = (f32[2,2,12]{2,1,0:T(2,128)S(1)}, f32[2,2,12]{2,1,0:T(2,128)S(1)}, u32[]{:S(2)}, u32[]{:S(2)}) collective-permute-start(f32[2,2,12]{2,1,0:T(2,128)S(1)} %max.21), channel_id=1, source_target_pairs={{0,8},{2,10},{4,12},{6,14},{8,0},{10,2},{12,4},{14,6},{16,24},{18,... | collective-permute-start | bytes 584 | tf_op jit(solution)/shard_map/ppermute | solution.py:1471
  417.6 27.0 %copy-start.21 = (bf16[1024,3072]{1,0:T(8,128)(2,1)}, bf16[1024,3072]{1,0:T(8,128)(2,1)S(1)}, u32[]{:S(2)}) copy-start(bf16[1024,3072]{1,0:T(8,128)(2,1)S(1)} %get-tuple-element.118.y0_ref.refs_0_) | copy-start | bytes 18874372
  417.6 27.0 %collective-permute-start.5 = (f32[2,2,12]{2,1,0:T(2,128)S(1)}, f32[2,2,12]{2,1,0:T(2,128)S(1)}, u32[]{:S(2)}, u32[]{:S(2)}) collective-permute-start(f32[2,2,12]{2,1,0:T(2,128)S(1)} %max.22), channel_id=1, source_target_pairs={{0,16},{2,18},{4,20},{6,22},{8,24},{10,26},{12,28},{14,30},{16,0},... | collective-permute-start | bytes 584 | tf_op jit(solution)/shard_map/ppermute | solution.py:1471
  417.7 29.9 %slice-start.6 = ((f32[96,2,768]{2,1,0:T(2,128)}), f32[96,1,768]{2,1,0:T(1,128)S(1)}, s32[]{:S(2)}) async-start(f32[96,2,768]{2,1,0:T(2,128)} %param.20), calls=%async_computation.10 | async-start | bytes 589824 | tf_op jit(solution)/shard_map/slice | solution.py:1607
  449.4 19.7 %copy-start.11 = (bf16[1024,1536]{1,0:T(8,128)(2,1)S(1)}, bf16[1024,1536]{1,0:T(8,128)(2,1)}, u32[]{:S(2)}) copy-start(bf16[1024,1536]{1,0:T(8,128)(2,1)} %fusion.16.x_ref) | copy-start | bytes 9437188
  485.5 26.7 %copy-start.2 = (bf16[1024,3072]{1,0:T(8,128)(2,1)}, bf16[1024,3072]{1,0:T(8,128)(2,1)S(1)}, u32[]{:S(2)}) copy-start(bf16[1024,3072]{1,0:T(8,128)(2,1)S(1)} %add_convert_fusion.1.y0_ref.refs_0_) | copy-start | bytes 18874372
  512.3 28.0 %slice-start.2 = ((s8[6291456]{0:T(1024)(128)(4,1)}), s8[2097152]{0:T(1024)(128)(4,1)S(1)}, s32[]{:S(2)}) async-start(s8[6291456]{0:T(1024)(128)(4,1)} %bitcast.168), calls=%async_computation.6 | async-start | bytes 4194304
  512.3 28.0 %slice-start.3 = ((s8[6291456]{0:T(1024)(128)(4,1)}), s8[4194304]{0:T(1024)(128)(4,1)S(1)}, s32[]{:S(2)}) async-start(s8[6291456]{0:T(1024)(128)(4,1)} %bitcast.168), calls=%async_computation.7 | async-start | bytes 8388608
  512.3 28.0 %copy-start.38 = (f32[1536]{0:T(1024)S(1)}, f32[1536]{0:T(1024)}, u32[]{:S(2)}) copy-start(f32[1536]{0:T(1024)} %copy-done.37) | copy-start | bytes 18436
  512.3 28.0 %copy-start.42 = (f32[1024]{0:T(1024)S(1)}, f32[1024]{0:T(1024)}, u32[]{:S(2)}) copy-start(f32[1024]{0:T(1024)} %copy-done.41) | copy-start | bytes 12292
  512.3 28.0 %copy-start.49 = (f32[1024]{0:T(1024)S(1)}, f32[1024]{0:T(1024)}, u32[]{:S(2)}) copy-start(f32[1024]{0:T(1024)} %copy-done.48) | copy-start | bytes 12292
  559.1 9.0 copy-start.9
  559.1 9.0 copy-start.13
  559.1 9.0 copy-start.16
  568.1 32.9 %slice-start = ((s8[6291456]{0:T(1024)(128)(4,1)}), s8[4194304]{0:T(1024)(128)(4,1)S(1)}, s32[]{:S(2)}) async-start(s8[6291456]{0:T(1024)(128)(4,1)} %bitcast.166), calls=%async_computation.4 | async-start | bytes 8388608
  588.2 1.7 copy-start.5
  591.2 9.8 slice-start.1
  591.2 9.8 copy-start.36
  591.2 9.8 copy-start.40
  591.2 9.8 copy-start.47
  601.1 5.3 copy-start.25
  612.4 8.1 copy-start.6
  620.4 1.6 copy-start.1
  640.8 63.4 %copy-start.20 = (bf16[2,64,768]{2,1,0:T(8,128)(2,1)S(1)}, bf16[2,64,768]{2,1,0:T(8,128)(2,1)}, u32[]{:S(2)}) copy-start(bf16[2,64,768]{2,1,0:T(8,128)(2,1)} %copy-done.19) | copy-start | bytes 589828
  640.9 63.4 %copy-start.18 = (bf16[2,64,768]{2,1,0:T(8,128)(2,1)S(1)}, bf16[2,64,768]{2,1,0:T(8,128)(2,1)}, u32[]{:S(2)}) copy-start(bf16[2,64,768]{2,1,0:T(8,128)(2,1)} %copy-done.17) | copy-start | bytes 589828
  712.4 0.7 copy-start.33
  1008.5 14.4 %copy-start.31 = (f32[96,1536]{1,0:T(8,128)S(1)}, f32[96,1536]{1,0:T(8,128)}, u32[]{:S(2)}) copy-start(f32[96,1536]{1,0:T(8,128)} %get-tuple-element.162) | copy-start | bytes 1769476
  1013.3 12.6 %slice-start.4 = ((s8[6291456]{0:T(1024)(128)(4,1)}), s8[2097152]{0:T(1024)(128)(4,1)S(1)}, s32[]{:S(2)}) async-start(s8[6291456]{0:T(1024)(128)(4,1)} %bitcast.171), calls=%async_computation.8 | async-start | bytes 4194304
  1022.1 3.9 slice-start.5
  1023.7 2.6 copy-start.29
  1025.9 1.5 copy-start.28
  (4 other events, 2.7 us)
Sparse Core Ops, SparseCore 0:
  21.5 285.9 all-gather.2
  311.0 123.1 all-gather.4
  512.4 372.7 reduce-scatter.1

commit v4 on v3

--- a/solution.py
+++ b/solution.py
@@ -867,6 +867,10 @@
                         hop.begin()
                         for j in range(hop.count):
                             hop.work(0, 1, j)
+            if last:
+                for hop in [hop for hop in left if hop.kind == "total"]:
+                    hop.finish()
+                    left.remove(hop)
             if closing is not None:
                 closing(*parts[0], *parts[2], *parts[4])
             for hop in left:

time: 1050 us -> 1050 us (level)
  no operation moved by 1% of the time
where the time goes in v4:
time: 1050 us; the launch traced here: 1040 us
  Pallas kernels  796 us (76%)
  other arithmetic  85.4 us (8%)
  matrix products  82.4 us (8%)
  local copies, waits for them, and re-layouts  54.9 us (5%)
  between operations  15.2 us (1%)
    pallas_call x13, Pallas kernels, hosted(): pl.pallas_call(kernel, grid=grid, in_specs=list(in_specs) + [hbm] * len(a...  427 us
    pallas_call x1, Pallas kernels, gather_now(): pl.pallas_call(functools.partial(gather_kernel, parts, len(swaps)), in_sp...  201 us
    dot_general x8, matrix products, dotf(): return lax.dot_general(a, b, dims, preferred_element_type=f32)  82.4 us
    pallas_call x2, Pallas kernels, weight_grad_whole(): pl.pallas_call(weight_grad_whole_kernel, grid=(2, tiles), in_specs=[pl.Bl...  53.6 us
    pallas_call x4, Pallas kernels, project_both(): pl.pallas_call(project_kernel, grid=(2, width // tile), in_specs=[pl.Bloc...  43.2 us
    pallas_call x1, Pallas kernels, self_attend(): pl.pallas_call(functools.partial(self_forward_kernel, 512), grid=(2, pair...  39.8 us
    convert_element_type x14, other arithmetic, rounded(): return values.astype(jnp.bfloat16)  34.6 us
  transfers between devices with their start and end apart: 9, of which 1 were waited for; matrix products, arithmetic and copies ran while one was open for 15% of the time, Pallas kernels for 74%

profile of v4, /device:TPU:0, one launch (start us, length us, event | category | flops | bytes accessed | tf_op | source)
XLA Modules:
  0.0 1040.4 jit_solution(6096284725757919324)
XLA Ops:
  8.6 1.4 convert_element_type.197
  15.5 3.2 fusion.22.refs_1_
  22.4 201.1 %shard_map.243 = (bf16[2,4,4,96,3200]{4,3,2,1,0:T(8,128)(2,1)}, bf16[512,1536]{1,0:T(8,128)(2,1)}, bf16[32,1536]{1,0:T(8,128)(2,1)}) custom-call(bf16[96,3200]{1,0:T(8,128)(2,1)} %fusion.25.refs_0_, bf16[512,1536]{1,0:T(8,128)(2,1)} %fusion.22.refs_1_, bf16[32,1536]{1,0:T(8,128)(2,1)} %get-tuple-element.94.refs_2_), custom_call_target="tpu_custom_call" | custom-call | flops 1000000000 | bytes 100000000 | tf_op jit(solution)/shard_map/pallas_call | solution.py:1159
  223.4 1.8 convert_element_type.202
  227.1 2.1 dynamic-slice_bitcast_fusion.3
  234.4 19.1 %shard_map.244.q_ref.k_ref.v_ref.refs_0_.refs_1_.refs_2_ = bf16[2,1024,2304]{2,1,0:T(8,128)(2,1)S(1)} custom-call(bf16[1024,1536]{1,0:T(8,128)(2,1)S(1)} %add_convert_fusion.4.x_ref.refs_0_, bf16[2,1536,3200]{2,1,0:T(8,128)(2,1)} %bitcast.160), custom_call_target="tpu_custom_call" | custom-call | flops 14495514624 | bytes 23592960 | tf_op jit(solution)/shard_map/pallas_call | solution.py:1187
  253.5 5.6 fusion.23
  259.2 39.8 %shard_map.245 = (bf16[2,1024,768]{2,1,0:T(8,128)(2,1)S(1)}, f32[2,6,8,1024]{3,2,1,0:T(8,128)S(1)}, f32[2,6,8,128]{3,2,1,0:T(8,128)S(1)}) custom-call(bf16[2,1024,2304]{2,1,0:T(8,128)(2,1)S(1)} %shard_map.244.q_ref.k_ref.v_ref.refs_0_.refs_1_.refs_2_, bf16[2,1024,2304]{2,1,0:T(8,128)(2,1)S(1)} %shard_map.244.q_ref.k_ref.v_ref.refs_0_.refs_1_.refs_2_, ...), custom_call_target="tpu_custom_call" | custom-call | flops 12884901888 | bytes 12582912 | tf_op jit(solution)/shard_map/pallas_call | solution.py:480
  299.0 1.6 copy-done.3
  301.6 11.5 %shard_map.246.refs_4_ = f32[1024,1536]{1,0:T(8,128)} custom-call(bf16[2,1024,768]{2,1,0:T(8,128)(2,1)} %copy-done.3, bf16[2,1024,768]{2,1,0:T(8,128)(2,1)} %copy-done.3, bf16[2,1536,3200]{2,1,0:T(8,128)(2,1)} %bitcast.161, bf16[2,1536,3200]{2,1,0:T(8,128)(2,1)} %bitcast.162, f32[1024,1536]{1,0:T(8,128)} %copy-done.24), custom_call_target="tpu_custom_call" | custom-call | flops 4831838208 | bytes 9663676 | tf_op jit(solution)/shard_map/pallas_call | solution.py:886
  313.1 3.2 reduce_sum.144
  316.3 4.1 multiply_reduce_fusion.5
  320.6 2.2 dynamic-slice_bitcast_fusion.2
  322.8 1.4 add_convert_fusion.3.x_ref.refs_0_
  324.2 2.9 convert_element_type.215
  327.1 1.7 copy-done.27
  328.8 2.5 fusion.16.x_ref
  331.3 3.3 fusion.20
  334.6 3.3 fusion.21
  338.0 7.1 shard_map.247.q_ref
  345.0 11.7 %shard_map.248 = (bf16[2,1024,768]{2,1,0:T(8,128)(2,1)S(1)}, f32[2,6,8,128]{3,2,1,0:T(8,128)S(1)}) custom-call(bf16[2,1024,768]{2,1,0:T(8,128)(2,1)S(1)} %shard_map.247.q_ref, bf16[2,64,1536]{2,1,0:T(8,128)(2,1)S(1)} %pad_maximum_fusion.2.k_ref.v_ref, bf16[2,64,1536]{2,1,0:T(8,128)(2,1)S(1)} %pad_maximum_fusion.2.k_ref.v_ref), custom_call_target="tpu_custom_call" | custom-call | flops 3221225472 | bytes 6291456 | tf_op jit(solution)/shard_map/pallas_call | solution.py:1376
  356.8 1.6 copy-done.4
  359.6 11.5 %shard_map.249.refs_4_ = f32[1024,1536]{1,0:T(8,128)} custom-call(bf16[2,1024,768]{2,1,0:T(8,128)(2,1)} %copy-done.4, bf16[2,1024,768]{2,1,0:T(8,128)(2,1)} %copy-done.4, bf16[2,1536,6144]{2,1,0:T(8,128)(2,1)} %bitcast.148, bf16[2,1536,6144]{2,1,0:T(8,128)(2,1)} %bitcast.149, f32[1024,1536]{1,0:T(8,128)} %shard_map.246.refs_4_), custom_call_target="tpu_custom_call" | custom-call | flops 4831838208 | bytes 9663676 | tf_op jit(solution)/shard_map/pallas_call | solution.py:886
  371.1 3.1 reduce_sum.146
  374.3 5.5 multiply_reduce_fusion.4
  379.8 1.8 collective-permute-start.2
  383.5 2.4 collective-permute-start.3
  385.9 16.1 %multiply_convert_fusion = (bf16[1024,3072]{1,0:T(8,128)(2,1)}, f32[1024,3072]{1,0:T(8,128)}) fusion(bf16[1024,1536]{1,0:T(8,128)(2,1)S(1)} %add_convert_fusion.2.x_ref, bf16[2,1536,6144]{2,1,0:T(8,128)(2,1)} %bitcast.150), kind=kOutput, calls=%fused_computation.2 | convolution fusion | flops 9679405056 | bytes 31457280 | tf_op jit(solution)/shard_map/dot_general | solution.py:429
  402.1 15.6 %multiply_convert_fusion.1 = (bf16[1024,3072]{1,0:T(8,128)(2,1)S(1)}, f32[1024,3072]{1,0:T(8,128)}) fusion(bf16[1024,1536]{1,0:T(8,128)(2,1)S(1)} %add_convert_fusion.2.x_ref, bf16[2,1536,6144]{2,1,0:T(8,128)(2,1)} %bitcast.151), kind=kOutput, calls=%fused_computation.4 | convolution fusion | flops 9679405056 | bytes 31457280 | tf_op jit(solution)/shard_map/dot_general | solution.py:429
  417.8 26.9 %shard_map.250.refs_0_ = bf16[2,1536,6144]{2,1,0:T(8,128)(2,1)} custom-call(bf16[1024,1536]{1,0:T(8,128)(2,1)S(1)} %copy-done.10, bf16[1024,3072]{1,0:T(8,128)(2,1)S(1)} %get-tuple-element.118.y0_ref.refs_0_, bf16[1024,3072]{1,0:T(8,128)(2,1)} %get-tuple-element.119.y1_ref.refs_1_), custom_call_target="tpu_custom_call" | custom-call | flops 19327352832 | bytes 34603008 | tf_op jit(solution)/shard_map/pallas_call | solution.py:1452
  445.5 2.1 broadcast_multiply_fusion
  447.6 1.8 fusion.26
  449.4 19.7 %add_convert_fusion.y1_ref.refs_1_ = bf16[1024,3072]{1,0:T(8,128)(2,1)} fusion(f32[1024,3072]{1,0:T(8,128)} %get-tuple-element.260, bf16[1024,1536]{1,0:T(8,128)(2,1)} %fusion.16.x_ref, bf16[2,1536,3072]{2,1,0:T(8,128)(2,1)} %bitcast.181), kind=kOutput, calls=%fused_computation | convolution fusion | flops 9704570880 | bytes 31457280 | tf_op jit(solution)/shard_map/dot_general | solution.py:429
  469.2 16.4 %add_convert_fusion.1.y0_ref.refs_0_ = bf16[1024,3072]{1,0:T(8,128)(2,1)S(1)} fusion(f32[1024,3072]{1,0:T(8,128)} %get-tuple-element.258, bf16[1024,1536]{1,0:T(8,128)(2,1)S(1)} %copy-done.11, bf16[2,1536,3072]{2,1,0:T(8,128)(2,1)} %bitcast.182), kind=kOutput, calls=%fused_computation.1 | convolution fusion | flops 9704570880 | bytes 31457280 | tf_op jit(solution)/shard_map/dot_general | solution.py:429
  485.6 26.7 %shard_map.251 = bf16[2,1536,6144]{2,1,0:T(8,128)(2,1)} custom-call(bf16[1024,1536]{1,0:T(8,128)(2,1)S(1)} %add_convert_fusion.2.x_ref, bf16[1024,3072]{1,0:T(8,128)(2,1)S(1)} %add_convert_fusion.1.y0_ref.refs_0_, bf16[1024,3072]{1,0:T(8,128)(2,1)} %add_convert_fusion.y1_ref.refs_1_, ...), custom_call_target="tpu_custom_call", output_to_operand_aliasing={{}: (3, {})} | custom-call | flops 19327352832 | bytes 34603008 | tf_op jit(solution)/shard_map/pallas_call | solution.py:1452
  512.4 27.9 %shard_map.252 = f32[1024,1536]{1,0:T(8,128)} custom-call(bf16[1024,3072]{1,0:T(8,128)(2,1)} %copy-done.2, bf16[1024,3072]{1,0:T(8,128)(2,1)} %add_convert_fusion.y1_ref.refs_1_, bf16[2,1536,6144]{2,1,0:T(8,128)(2,1)} %bitcast.152, bf16[2,1536,6144]{2,1,0:T(8,128)(2,1)} %bitcast.153), custom_call_target="tpu_custom_call" | custom-call | flops 19327352832 | bytes 38654704 | tf_op jit(solution)/shard_map/pallas_call | solution.py:886
  540.3 5.4 multiply_reduce_fusion
  545.7 13.4 %fusion.43 = (bf16[1024,1536]{1,0:T(8,128)(2,1)S(1)}, f32[1024,1536]{1,0:T(8,128)}) fusion(f32[1024]{0:T(1024)S(1)} %broadcast_multiply_fusion.4, f32[1024,1536]{1,0:T(8,128)S(1)} %bitcast.169, f32[1024]{0:T(1024)S(1)} %copy-done.42, f32[1024]{0:T(1024)S(1)} %broadcast_multiply_fusion.5, f32[1024,1536]{1,0:T(8,128)} %shard_map.252, f32[1536]{0:T(1024)S(1)} %copy-done.38, ...), kind=kLoop, calls=%fused_computation.139 | loop fusion | flops 18874368 | bytes 28334080 | tf_op jit(solution)/shard_map/convert_element_type | solution.py:31
  559.1 8.9 shard_map.253.g_ref
  568.1 20.1 %shard_map.254 = (bf16[2,1024,768]{2,1,0:T(8,128)(2,1)S(1)}, bf16[2,64,768]{2,1,0:T(8,128)(2,1)S(1)}, bf16[2,64,768]{2,1,0:T(8,128)(2,1)S(1)}) custom-call(bf16[2,1024,768]{2,1,0:T(8,128)(2,1)S(1)} %copy-done.13, bf16[2,64,1536]{2,1,0:T(8,128)(2,1)S(1)} %copy-done.16, bf16[2,64,1536]{2,1,0:T(8,128)(2,1)S(1)} %copy-done.16, ...), custom_call_target="tpu_custom_call" | custom-call | flops 6442450944 | bytes 9437184 | tf_op jit(solution)/shard_map/pallas_call | solution.py:1412
  588.2 1.6 copy-done.5
  591.2 9.8 shard_map.255
  601.1 5.2 multiply_reduce_fusion.1
  606.4 5.9 fusion.42
  612.4 8.1 shard_map.256.refs_3_
  620.4 1.6 copy-done.1
  622.1 18.8 %shard_map.257 = (bf16[2,4,2,96,2304]{4,3,2,1,0:T(8,128)(2,1)}, bf16[2,4,2,96,2304]{4,3,2,1,0:T(8,128)(2,1)}) custom-call(bf16[1024,1536]{1,0:T(8,128)(2,1)} %copy-done.8, bf16[64,1536]{1,0:T(8,128)(2,1)} %copy-done.34, bf16[2,1024,768]{2,1,0:T(8,128)(2,1)} %copy-done.5, bf16[2,1024,768]{2,1,0:T(8,128)(2,1)} %copy-done.5, bf16[2,64,768]{2,1,0:T(8,128)(2,1)} %copy-done.19, ...), custom_call_target="tpu_custom_call" | custom-call | flops 14495514624 | bytes 28991028 | tf_op jit(solution)/shard_map/pallas_call | solution.py:886
  640.9 63.4 %shard_map.258 = (bf16[2,1024,512]{2,1,0:T(8,128)(2,1)}, bf16[2,1024,512]{2,1,0:T(8,128)(2,1)}, bf16[2,1024,512]{2,1,0:T(8,128)(2,1)}, bf16[4,2,48,2304]{3,2,1,0:T(8,128)(2,1)}, bf16[2,4,48,2304]{3,2,1,0:T(8,128)(2,1)}) custom-call(bf16[2,1024,2304]{2,1,0:T(8,128)(2,1)} %copy-done, bf16[2,1024,2304]{2,1,0:T(8,128)(2,1)} %copy-done, ...), custom_call_target="tpu_custom_call" | custom-call | flops 8589934592 | bytes 17179868 | tf_op jit(solution)/shard_map/pallas_call | solution.py:886
  704.3 4.0 fusion.12
  708.4 4.1 fusion.17
  713.8 19.0 %shard_map.259 = (bf16[2,4,2,96,1536]{4,3,2,1,0:T(8,128)(2,1)}, bf16[2,4,2,96,1536]{4,3,2,1,0:T(8,128)(2,1)}) custom-call(bf16[1024,1536]{1,0:T(8,128)(2,1)} %copy-done.9, bf16[1024,1536]{1,0:T(8,128)(2,1)} %copy-done.6, bf16[2,1024,768]{2,1,0:T(8,128)(2,1)} %copy-done.4, bf16[2,1024,768]{2,1,0:T(8,128)(2,1)} %copy-done.4, bf16[2,1024,768]{2,1,0:T(8,128)(2,1)} %copy-done.3, ...), custom_call_target="tpu_custom_call" | custom-call | flops 9663676416 | bytes 19327352 | tf_op jit(solution)/shard_map/pallas_call | solution.py:886
  732.9 46.4 %shard_map.260 = (f32[1024,1536]{1,0:T(8,128)}, bf16[4,2,48,1536]{3,2,1,0:T(8,128)(2,1)}, bf16[2,4,48,1536]{3,2,1,0:T(8,128)(2,1)}) custom-call(bf16[1024,3072]{1,0:T(8,128)(2,1)} %copy-done.21, bf16[1024,3072]{1,0:T(8,128)(2,1)} %get-tuple-element.119.y1_ref.refs_1_, bf16[2,1536,3072]{2,1,0:T(8,128)(2,1)} %bitcast.183, bf16[2,1536,3072]{2,1,0:T(8,128)(2,1)} %bitcast.184, ...), custom_call_target="tpu_custom_call" | custom-call | flops 19327352832 | bytes 38654704 | tf_op jit(solution)/shard_map/pallas_call | solution.py:886
  779.2 3.3 dynamic-slice_convert_fusion.refs_15_
  782.5 31.5 %shard_map.261 = (bf16[2,4,2,96,1536]{4,3,2,1,0:T(8,128)(2,1)}, bf16[2,4,2,96,1536]{4,3,2,1,0:T(8,128)(2,1)}, bf16[32,1536]{1,0:T(8,128)(2,1)}, bf16[4,48,2304]{2,1,0:T(8,128)(2,1)}, bf16[4,48,2304]{2,1,0:T(8,128)(2,1)}) custom-call(bf16[1024,1536]{1,0:T(8,128)(2,1)} %copy-done.7, bf16[2,1024,512]{2,1,0:T(8,128)(2,1)} %get-tuple-element.126.refs_1_.refs_4_.refs_0_.refs_6_, ...), custom_call_target="tpu_custom_call" | custom-call | flops 9663676416 | bytes 19327352 | tf_op jit(solution)/shard_map/pallas_call | solution.py:886
  814.0 60.1 %shard_map.262 = (bf16[2,1024,256]{2,1,0:T(8,128)(2,1)}, bf16[2,1024,256]{2,1,0:T(8,128)(2,1)}, bf16[2,1024,256]{2,1,0:T(8,128)(2,1)}, bf16[4,48,1536]{2,1,0:T(8...) custom-call(bf16[2,1024,2304]{2,1,0:T(8,128)(2,1)} %copy-done, ...), custom_call_target="tpu_custom_call" | custom-call | flops 4294967296 | bytes 8589934 | tf_op jit(solution)/shard_map/pallas_call | solution.py:886
  874.2 33.4 %shard_map.263 = (bf16[2,4,2,96,768]{4,3,2,1,0:T(8,128)(2,1)}, bf16[2,4,2,96,768]{4,3,2,1,0:T(8,128)(2,1)}, bf16[4,2,48,1536]{3,2,1,0:T(8,128)(2,1)}, bf16[2,4,48,1536]{3,2,1,0:T(8,128)(2,1)}) custom-call(bf16[1024,1536]{1,0:T(8,128)(2,1)} %copy-done.7, bf16[2,1024,256]{2,1,0:T(8,128)(2,1)} %get-tuple-element.133.refs_1_.refs_4_.refs_3_.refs_9_, ...), custom_call_target="tpu_custom_call" | custom-call | flops 4831838208 | bytes 9663676 | tf_op jit(solution)/shard_map/pallas_call | solution.py:886
  909.8 37.4 %shard_map.264 = (f32[1024,1536]{1,0:T(8,128)}, bf16[4,2,48,768]{3,2,1,0:T(8,128)(2,1)}, bf16[2,4,48,768]{3,2,1,0:T(8,128)(2,1)}, bf16[4,48,1536]{2,1,0:T(8,128)...) custom-call(bf16[2,1024,512]{2,1,0:T(8,128)(2,1)} %get-tuple-element.126.refs_1_.ref, ...), custom_call_target="tpu_custom_call" | custom-call | flops 14495514624 | bytes 28991028 | tf_op jit(solution)/shard_map/pallas_call | solution.py:886
  949.7 56.4 %shard_map.265 = (f32[1024,1536]{1,0:T(8,128)}, bf16[4,128,1536]{2,1,0:T(8,128)(2,1)}, f32[8,1536]{1,0:T(8,128)}, bf16[4,48,768]{2,1,0:T(8,128)(2,1)}, bf16[4,48...) custom-call(f32[1024,1536]{1,0:T(8,128)} %copy-done.24, ...), custom_call_target="tpu_custom_call" | custom-call | flops 1000000000 | bytes 2000000 | tf_op jit(solution)/shard_map/pallas_call | solution.py:886
  1007.3 1.7 slice.189
  1014.8 1.4 fusion.36
  1016.2 1.6 pad_maximum_fusion.3
  1021.3 2.2 dynamic-slice_bitcast_fusion.1
  1025.5 5.4 maximum_select_fusion.2
  1030.8 2.9 fusion.45
  (215 shorter events, 42.6 us)
Async XLA Ops:
  7.2 8.1 copy-start.51
  7.2 11.5 %copy-start.43 = (f32[2,32,1536]{2,1,0:T(8,128)S(1)}, f32[2,32,1536]{2,1,0:T(8,128)}, u32[]{:S(2)}) copy-start(f32[2,32,1536]{2,1,0:T(8,128)} %param.13) | copy-start | bytes 1179652
  7.2 324.1 %all-gather.3.cloned.1.call-start = ((), (), s32[]{:S(2)}) async-start(), calls=%async_computation.1 | async-start | bytes 38928384 | tf_op jit(solution)/shard_map/all_gather | solution.py:1535
  8.6 12.8 %copy-start.30 = (f32[96,3072]{1,0:T(8,128)S(1)}, f32[96,3072]{1,0:T(8,128)}, u32[]{:S(2)}) copy-start(f32[96,3072]{1,0:T(8,128)} %param.23) | copy-start | bytes 3538948
  21.4 428.1 %all-gather.5.cloned.1.call-start = ((), (), s32[]{:S(2)}) async-start(), calls=%async_computation.2 | async-start | bytes 19464192 | tf_op jit(solution)/shard_map/all_gather | solution.py:1535
  22.3 1008.5 %reduce-scatter.2.cloned.1.call-start = ((), (), s32[]{:S(2)}) async-start(), calls=%async_computation.3 | async-start | bytes 38928384 | tf_op jit(solution)/shard_map/reduce_scatter | solution.py:1617
  230.4 2.7 copy-start.24
  230.4 0.8 copy-start.44
  232.3 90.4 %copy-start.35 = (f32[1536]{0:T(1024)}, f32[1536]{0:T(1024)S(1)}, u32[]{:S(2)}) copy-start(f32[1536]{0:T(1024)S(1)} %get-tuple-element.228) | copy-start | bytes 18436
  232.3 149.3 %copy-start.37 = (f32[1536]{0:T(1024)}, f32[1536]{0:T(1024)S(1)}, u32[]{:S(2)}) copy-start(f32[1536]{0:T(1024)S(1)} %get-tuple-element.224) | copy-start | bytes 18436
  234.4 19.1 %copy-start.7 = (bf16[1024,1536]{1,0:T(8,128)(2,1)}, bf16[1024,1536]{1,0:T(8,128)(2,1)S(1)}, u32[]{:S(2)}) copy-start(bf16[1024,1536]{1,0:T(8,128)(2,1)S(1)} %add_convert_fusion.4.x_ref.refs_0_) | copy-start | bytes 9437188
  253.5 45.5 %copy-start = (bf16[2,1024,2304]{2,1,0:T(8,128)(2,1)}, bf16[2,1024,2304]{2,1,0:T(8,128)(2,1)S(1)}, u32[]{:S(2)}) copy-start(bf16[2,1024,2304]{2,1,0:T(8,128)(2,1)S(1)} %shard_map.244.q_ref.k_ref.v_ref.refs_0_.refs_1_.refs_2_) | copy-start | bytes 28311556
  259.2 65.0 %collective-permute-start = (bf16[512,1536]{1,0:T(8,128)(2,1)}, bf16[512,1536]{1,0:T(8,128)(2,1)}, u32[]{:S(2)}, u32[]{:S(2)}) collective-permute-start(bf16[512,1536]{1,0:T(8,128)(2,1)} %fusion.23), channel_id=1, source_target_pairs={{0,1},{1,0},{2,3},{3,2},{4,5},{5,4},{6,7},{7,6},{8,9},{9,8},{10,11... | collective-permute-start | bytes 4718600 | tf_op jit(solution)/shard_map/ppermute | solution.py:1475
  299.0 1.6 copy-start.3
  313.1 7.4 copy-start.32
  313.1 7.4 copy-start.45
  316.3 6.4 copy-start.39
  316.3 6.4 copy-start.22
  320.5 3.7 copy-start.46
  320.5 14.1 %copy-start.34 = (bf16[64,1536]{1,0:T(8,128)(2,1)}, bf16[64,1536]{1,0:T(8,128)(2,1)S(1)}, u32[]{:S(2)}) copy-start(bf16[64,1536]{1,0:T(8,128)(2,1)S(1)} %maximum_select_fusion.5.refs_1_) | copy-start | bytes 589828
  322.7 4.4 copy-start.26
  324.1 13.8 %copy-start.8 = (bf16[1024,1536]{1,0:T(8,128)(2,1)}, bf16[1024,1536]{1,0:T(8,128)(2,1)S(1)}, u32[]{:S(2)}) copy-start(bf16[1024,1536]{1,0:T(8,128)(2,1)S(1)} %add_convert_fusion.3.x_ref.refs_0_) | copy-start | bytes 9437188
  327.1 1.7 copy-start.27
  337.9 7.1 copy-start.15
  345.0 11.7 %copy-start.12 = (bf16[2,1024,768]{2,1,0:T(8,128)(2,1)}, bf16[2,1024,768]{2,1,0:T(8,128)(2,1)S(1)}, u32[]{:S(2)}) copy-start(bf16[2,1024,768]{2,1,0:T(8,128)(2,1)S(1)} %shard_map.247.q_ref) | copy-start | bytes 9437188
  356.8 1.6 copy-start.4
  358.6 21.2 %collective-permute-start.1 = (f32[2,2,12]{2,1,0:T(2,128)S(1)}, f32[2,2,12]{2,1,0:T(2,128)S(1)}, u32[]{:S(2)}, u32[]{:S(2)}) collective-permute-start(f32[2,2,12]{2,1,0:T(2,128)S(1)} %constant_dynamic-update-slice_fusion), channel_id=1, source_target_pairs={{0,2},{2,0},{4,6},{6,4},{8,10},{10,8},{12,14},{14,12},{16,18},{18,... | collective-permute-start | bytes 584 | tf_op jit(solution)/shard_map/ppermute | solution.py:1475
  374.2 7.4 copy-start.23
  374.3 8.7 copy-start.41
  379.8 22.2 %copy-start.48 = (f32[1024]{0:T(1024)}, f32[1024]{0:T(1024)S(1)}, u32[]{:S(2)}) copy-start(f32[1024]{0:T(1024)S(1)} %add_rsqrt_fusion) | copy-start | bytes 12292
  379.8 3.7 collective-permute-start.2
  383.5 18.5 %collective-permute-start.3 = (f32[2,2,12]{2,1,0:T(2,128)S(1)}, f32[2,2,12]{2,1,0:T(2,128)S(1)}, u32[]{:S(2)}, u32[]{:S(2)}) collective-permute-start(f32[2,2,12]{2,1,0:T(2,128)S(1)} %max.20), channel_id=1, source_target_pairs={{0,4},{2,6},{4,0},{6,2},{8,12},{10,14},{12,8},{14,10},{16,20},{18,... | collective-permute-start | bytes 584 | tf_op jit(solution)/shard_map/ppermute | solution.py:1475
  402.0 15.8 %copy-start.10 = (bf16[1024,1536]{1,0:T(8,128)(2,1)S(1)}, bf16[1024,1536]{1,0:T(8,128)(2,1)}, u32[]{:S(2)}) copy-start(bf16[1024,1536]{1,0:T(8,128)(2,1)} %fusion.16.x_ref) | copy-start | bytes 9437188
  402.0 15.7 %collective-permute-start.4 = (f32[2,2,12]{2,1,0:T(2,128)S(1)}, f32[2,2,12]{2,1,0:T(2,128)S(1)}, u32[]{:S(2)}, u32[]{:S(2)}) collective-permute-start(f32[2,2,12]{2,1,0:T(2,128)S(1)} %max.21), channel_id=1, source_target_pairs={{0,8},{2,10},{4,12},{6,14},{8,0},{10,2},{12,4},{14,6},{16,24},{18,... | collective-permute-start | bytes 584 | tf_op jit(solution)/shard_map/ppermute | solution.py:1475
  417.6 27.0 %copy-start.21 = (bf16[1024,3072]{1,0:T(8,128)(2,1)}, bf16[1024,3072]{1,0:T(8,128)(2,1)S(1)}, u32[]{:S(2)}) copy-start(bf16[1024,3072]{1,0:T(8,128)(2,1)S(1)} %get-tuple-element.118.y0_ref.refs_0_) | copy-start | bytes 18874372
  417.6 27.0 %collective-permute-start.5 = (f32[2,2,12]{2,1,0:T(2,128)S(1)}, f32[2,2,12]{2,1,0:T(2,128)S(1)}, u32[]{:S(2)}, u32[]{:S(2)}) collective-permute-start(f32[2,2,12]{2,1,0:T(2,128)S(1)} %max.22), channel_id=1, source_target_pairs={{0,16},{2,18},{4,20},{6,22},{8,24},{10,26},{12,28},{14,30},{16,0},... | collective-permute-start | bytes 584 | tf_op jit(solution)/shard_map/ppermute | solution.py:1475
  417.7 29.9 %slice-start.6 = ((f32[96,2,768]{2,1,0:T(2,128)}), f32[96,1,768]{2,1,0:T(1,128)S(1)}, s32[]{:S(2)}) async-start(f32[96,2,768]{2,1,0:T(2,128)} %param.20), calls=%async_computation.10 | async-start | bytes 589824 | tf_op jit(solution)/shard_map/slice | solution.py:1611
  449.4 19.7 %copy-start.11 = (bf16[1024,1536]{1,0:T(8,128)(2,1)S(1)}, bf16[1024,1536]{1,0:T(8,128)(2,1)}, u32[]{:S(2)}) copy-start(bf16[1024,1536]{1,0:T(8,128)(2,1)} %fusion.16.x_ref) | copy-start | bytes 9437188
  485.5 26.7 %copy-start.2 = (bf16[1024,3072]{1,0:T(8,128)(2,1)}, bf16[1024,3072]{1,0:T(8,128)(2,1)S(1)}, u32[]{:S(2)}) copy-start(bf16[1024,3072]{1,0:T(8,128)(2,1)S(1)} %add_convert_fusion.1.y0_ref.refs_0_) | copy-start | bytes 18874372
  512.3 28.0 %slice-start.2 = ((s8[6291456]{0:T(1024)(128)(4,1)}), s8[2097152]{0:T(1024)(128)(4,1)S(1)}, s32[]{:S(2)}) async-start(s8[6291456]{0:T(1024)(128)(4,1)} %bitcast.168), calls=%async_computation.6 | async-start | bytes 4194304
  512.3 28.0 %slice-start.3 = ((s8[6291456]{0:T(1024)(128)(4,1)}), s8[4194304]{0:T(1024)(128)(4,1)S(1)}, s32[]{:S(2)}) async-start(s8[6291456]{0:T(1024)(128)(4,1)} %bitcast.168), calls=%async_computation.7 | async-start | bytes 8388608
  512.3 28.0 %copy-start.38 = (f32[1536]{0:T(1024)S(1)}, f32[1536]{0:T(1024)}, u32[]{:S(2)}) copy-start(f32[1536]{0:T(1024)} %copy-done.37) | copy-start | bytes 18436
  512.3 28.0 %copy-start.42 = (f32[1024]{0:T(1024)S(1)}, f32[1024]{0:T(1024)}, u32[]{:S(2)}) copy-start(f32[1024]{0:T(1024)} %copy-done.41) | copy-start | bytes 12292
  512.3 28.0 %copy-start.49 = (f32[1024]{0:T(1024)S(1)}, f32[1024]{0:T(1024)}, u32[]{:S(2)}) copy-start(f32[1024]{0:T(1024)} %copy-done.48) | copy-start | bytes 12292
  559.1 9.0 copy-start.9
  559.1 9.0 copy-start.13
  559.1 9.0 copy-start.16
  568.1 32.9 %slice-start = ((s8[6291456]{0:T(1024)(128)(4,1)}), s8[4194304]{0:T(1024)(128)(4,1)S(1)}, s32[]{:S(2)}) async-start(s8[6291456]{0:T(1024)(128)(4,1)} %bitcast.166), calls=%async_computation.4 | async-start | bytes 8388608
  588.2 1.7 copy-start.5
  591.2 9.8 slice-start.1
  591.2 9.8 copy-start.36
  591.2 9.8 copy-start.40
  591.2 9.8 copy-start.47
  601.1 5.3 copy-start.25
  612.4 8.1 copy-start.6
  620.4 1.6 copy-start.1
  640.8 63.4 %copy-start.20 = (bf16[2,64,768]{2,1,0:T(8,128)(2,1)S(1)}, bf16[2,64,768]{2,1,0:T(8,128)(2,1)}, u32[]{:S(2)}) copy-start(bf16[2,64,768]{2,1,0:T(8,128)(2,1)} %copy-done.19) | copy-start | bytes 589828
  640.9 63.4 %copy-start.18 = (bf16[2,64,768]{2,1,0:T(8,128)(2,1)S(1)}, bf16[2,64,768]{2,1,0:T(8,128)(2,1)}, u32[]{:S(2)}) copy-start(bf16[2,64,768]{2,1,0:T(8,128)(2,1)} %copy-done.17) | copy-start | bytes 589828
  712.4 0.7 copy-start.33
  1006.1 14.4 %copy-start.31 = (f32[96,1536]{1,0:T(8,128)S(1)}, f32[96,1536]{1,0:T(8,128)}, u32[]{:S(2)}) copy-start(f32[96,1536]{1,0:T(8,128)} %get-tuple-element.162) | copy-start | bytes 1769476
  1011.0 12.6 %slice-start.4 = ((s8[6291456]{0:T(1024)(128)(4,1)}), s8[2097152]{0:T(1024)(128)(4,1)S(1)}, s32[]{:S(2)}) async-start(s8[6291456]{0:T(1024)(128)(4,1)} %bitcast.171), calls=%async_computation.8 | async-start | bytes 4194304
  1019.7 3.9 slice-start.5
  1021.3 2.6 copy-start.29
  1023.5 1.5 copy-start.28
  (4 other events, 2.7 us)
Sparse Core Ops, SparseCore 0:
  21.5 285.9 all-gather.2
  311.0 123.1 all-gather.4
  512.4 372.7 reduce-scatter.1
